TPU v7x, 32 devices: a whole 2x2x4 slice. The times are simulated.
32 devices in a mesh: row: 4 (over z), col: 8 (over y, x, core).
Axes of the slice: x: 2, y: 2, z: 4, core: 2. Of those that a mesh axis runs over, the one named last changes fastest.
Arguments:
- image: float32 [16, 16, 64, 128], P('row', 'col'), may hold values from -6 to 6
- u_factors: bfloat16 [20, 16, 1024, 256], P('row', 'col'), may hold values from -0.125 to 0.125
- v_factors: bfloat16 [20, 16, 1024, 256], P('row', 'col'), may hold values from -0.1875 to 0.1875
- ranks: int32 [20, 16], P('row', 'col'), may hold values from 16 to 256
- measured: bfloat16 [20480, 128], P('row'), may hold values from -6 to 6
Outputs:
- new_image: float32 [16, 16, 64, 128], P('row', 'col')
All inputs are finite; a program needn't handle non-finite values.
Results may differ from a plain program's by a relative error of at most 0.0051.
Values may be sent and summed in bfloat16 or wider, within the bound.
No kernel may reach another device: no remote copies, remote signals or barrier semaphores. Data moves between devices by JAX's collectives and lax.ppermute only.
A program may use at most 128 MiB of HBM per device.

v0:
```python
import jax
import jax.numpy as jnp
from jax import lax
from jax.sharding import PartitionSpec as P

diff_rate = 0.12
edge_scale = 0.5


def padded_2(block, sides, width):
    for axis, dim in sides:
        count = lax.axis_size(axis)
        forward = [(i, i + 1) for i in range(count - 1)]
        backward = [(target, source) for source, target in forward]
        low = lax.ppermute(
            lax.slice_in_dim(block, block.shape[dim] - width, None, axis=dim), axis, forward
        )
        high = lax.ppermute(lax.slice_in_dim(block, 0, width, axis=dim), axis, backward)
        block = jnp.concatenate([low, block, high], axis=dim)
    return block


def flux(delta):
    scaled = delta / edge_scale
    return delta / (1.0 + scaled * scaled)


def diffuse_margin(extended):
    padded = jnp.pad(extended, ((0, 0), (0, 0), (1, 1), (0, 0)))
    center = padded[1:-1, 1:-1, 1:-1]
    total = flux(padded[2:, 1:-1, 1:-1] - center) + flux(padded[:-2, 1:-1, 1:-1] - center)
    total = total + flux(padded[1:-1, 2:, 1:-1] - center) + flux(padded[1:-1, :-2, 1:-1] - center)
    total = total + flux(padded[1:-1, 1:-1, 2:] - center) + flux(padded[1:-1, 1:-1, :-2] - center)
    return center + diff_rate * total


def body(image, u_factors, v_factors, ranks, measured):
    row_tiles, col_tiles, tile_len, rank_max = u_factors.shape
    frames = image.shape[3]
    local_x, local_y = (image.shape[0], image.shape[1])
    whole = lax.all_gather(image.astype(jnp.bfloat16), "row", axis=0, tiled=True)
    xtiles = whole.reshape(col_tiles, tile_len, frames)
    levels = lax.broadcasted_iota(jnp.int32, (row_tiles, col_tiles, rank_max), 2)
    mask = (levels < ranks[:, :, None]).astype(jnp.float32)
    coef = jnp.einsum("ijkr,jkf->ijrf", v_factors, xtiles, preferred_element_type=jnp.float32)
    coef = (coef * mask[:, :, :, None]).astype(jnp.bfloat16)
    partial_value = jnp.einsum(
        "ijkr,ijrf->ikf", u_factors, coef, preferred_element_type=jnp.float32
    )
    partial_value = partial_value.reshape(row_tiles * tile_len, frames)
    total = lax.psum(partial_value, "col")
    resid = (total - measured.astype(jnp.float32)).astype(jnp.bfloat16)
    resid = resid.reshape(row_tiles, tile_len, frames)
    back = jnp.einsum("ijkr,ikf->ijrf", u_factors, resid, preferred_element_type=jnp.float32)
    back = (back * mask[:, :, :, None]).astype(jnp.bfloat16)
    grad_terms = jnp.einsum("ijkr,ijrf->jkf", v_factors, back, preferred_element_type=jnp.float32)
    grad_terms = grad_terms.reshape(col_tiles * tile_len, frames)
    gradient = lax.psum_scatter(grad_terms, "row", scatter_dimension=0, tiled=True)
    moved = image - gradient.reshape(image.shape)
    extended = padded_2(moved, (("row", 0), ("col", 1)), 2)
    middle = diffuse_margin(extended)
    grid_x = local_x * lax.axis_size("row")
    grid_y = local_y * lax.axis_size("col")
    pos_x = (
        lax.broadcasted_iota(jnp.int32, (local_x + 2, 1, 1, 1), 0)
        + lax.axis_index("row") * local_x
        - 1
    )
    pos_y = (
        lax.broadcasted_iota(jnp.int32, (1, local_y + 2, 1, 1), 1)
        + lax.axis_index("col") * local_y
        - 1
    )
    inside = (pos_x >= 0) & (pos_x < grid_x) & ((pos_y >= 0) & (pos_y < grid_y))
    middle = jnp.where(inside, middle, 0.0)
    moved = diffuse_margin(middle)
    return moved


def solution(mesh):
    placed = (
        P("row", "col", None, None),
        P("row", "col", None, None),
        P("row", "col", None, None),
        P("row", "col"),
        P("row", None),
    )
    return jax.shard_map(
        body, mesh=mesh, in_specs=placed, out_specs=P("row", "col", None, None), check_vma=False
    )
```

profile of v0, /device:TPU:19, one launch (start us, length us, event | category | flops | bytes accessed | tf_op | source)
XLA Modules:
  0.0 174.3 jit_solution(7555312063323355615)
XLA Ops:
  6.5 0.8 copy.20
  7.3 0.1 compare_convert_fusion
  7.4 1.0 convert_element_type.29
  8.4 12.8 %all_gather.3 = bf16[16,2,64,128]{3,2,1,0:T(8,128)(2,1)S(1)} all-gather(bf16[4,2,64,128]{3,2,1,0:T(8,128)(2,1)S(1)} %convert_element_type.29), channel_id=1, replica_groups=mesh['row'=4,'col'=8] {'row'}, dimensions={0}, use_global_device_ids=true | all-gather | bytes 655360 | tf_op jit(solution)/shard_map/all_gather | solution.py:41
  21.2 6.6 %convolution_bitcast_fusion = f32[5,1024,128]{1,2,0:T(8,128)S(1)} fusion(bf16[5,2,1024,256]{3,2,1,0:T(8,128)(2,1)} %param.6, bf16[2,1024,128,1]{2,1,0,3:T(8,128)(2,1)S(1)} %bitcast.37, bf16[5,2,1024,256]{3,2,1,0:T(8,128)(2,1)} %param.7, f32[5,2,256]{2,1,0:T(2,128)S(1)} %compare_convert_fusion), kind=kOutput, calls=%fused_computation.7 | convolution fusion | flops 1342832640 | bytes 13641728 | tf_op jit(solution)/shard_map/ijkr,ijrf->ikf/dot_general | solution.py:47
  27.8 2.1 %copy.21 = f32[5,1024,128]{2,1,0:T(8,128)} copy(f32[5,1024,128]{1,2,0:T(8,128)S(1)} %convolution_bitcast_fusion) | data formatting | bytes 5242880 | tf_op jit(solution)/shard_map/ijkr,ijrf->ikf/dot_general | solution.py:47
  30.0 68.7 %all-reduce.4.cloned.1.call-done = f32[5120,128]{1,0:T(8,128)} async-done(((f32[5120,128]{1,0:T(8,128)}), f32[5120,128]{1,0:T(8,128)}) %all-reduce.4.cloned.1.call-update) | async-done | bytes 2621456 | tf_op jit(solution)/shard_map/psum | solution.py:51
  98.7 2.0 %subtract_convert_fusion = bf16[5120,128]{1,0:T(8,128)(2,1)S(1)} fusion(f32[5120,128]{1,0:T(8,128)} %all-reduce.4.cloned.1.call-done, bf16[5120,128]{1,0:T(8,128)(2,1)S(1)} %copy-done), kind=kLoop, calls=%fused_computation.4 | loop fusion | flops 1966080 | bytes 5242880 | tf_op jit(solution)/shard_map/convert_element_type | solution.py:52
  100.7 7.7 %fusion.8 = f32[2,1024,128]{1,2,0:T(8,128)} fusion(bf16[5,2,1024,256]{3,2,1,0:T(8,128)(2,1)} %param.7, bf16[5,1024,128,1]{2,1,0,3:T(8,128)(2,1)S(1)} %bitcast.38, bf16[5,2,1024,256]{3,2,1,0:T(8,128)(2,1)} %param.6, f32[5,2,256]{2,0,1:T(8,128)S(1)} %copy.24), kind=kOutput, calls=%fused_computation.12 | convolution fusion | flops 1342832640 | bytes 12855296 | tf_op jit(solution)/shard_map/ijkr,ijrf->jkf/dot_general | solution.py:56
  108.4 2.6 %copy.26 = f32[2,1024,128]{2,1,0:T(8,128)} copy(f32[2,1024,128]{1,2,0:T(8,128)} %fusion.8) | data formatting | bytes 2097152 | tf_op jit(solution)/shard_map/ijkr,ijrf->jkf/dot_general | solution.py:56
  111.0 26.1 %reduce-scatter.2.cloned.1.call-done = f32[512,128]{1,0:T(8,128)} async-done(((f32[2048,128]{1,0:T(8,128)}), f32[512,128]{1,0:T(8,128)}) %reduce-scatter.2.cloned.1.call-update) | async-done | bytes 262160 | tf_op jit(solution)/shard_map/reduce_scatter | solution.py:58
  137.1 1.0 sub.51
  138.1 1.9 %collective-permute-start = (f32[2,2,64,128]{3,2,1,0:T(8,128)S(1)}, f32[2,2,64,128]{3,2,1,0:T(8,128)S(1)}, u32[]{:S(2)}, u32[]{:S(2)}) collective-permute-start(f32[2,2,64,128]{3,2,1,0:T(8,128)S(1)} %get-tuple-element.5), channel_id=1, source_target_pairs={{0,8},{8,16},{16,24},{1,9},{9,17},{17,25},{2,10},{10,18},{18,26},{... | collective-permute-start | bytes 393224 | tf_op jit(solution)/shard_map/ppermute | solution.py:15
  140.0 3.4 %collective-permute-start.1 = (f32[2,2,64,128]{3,2,1,0:T(8,128)S(1)}, f32[2,2,64,128]{3,2,1,0:T(8,128)S(1)}, u32[]{:S(2)}, u32[]{:S(2)}) collective-permute-start(f32[2,2,64,128]{3,2,1,0:T(8,128)S(1)} %get-tuple-element.6), channel_id=1, source_target_pairs={{8,0},{16,8},{24,16},{9,1},{17,9},{25,17},{10,2},{18,10},{26,18},{... | collective-permute-start | bytes 393224 | tf_op jit(solution)/shard_map/ppermute | solution.py:18
  143.4 0.9 collective-permute-done
  144.3 1.4 collective-permute-done.1
  145.8 5.4 %collective-permute-start.2 = (f32[8,2,64,128]{3,2,1,0:T(8,128)S(1)}, f32[8,2,64,128]{3,2,1,0:T(8,128)S(1)}, u32[]{:S(2)}, u32[]{:S(2)}) collective-permute-start(f32[8,2,64,128]{3,2,1,0:T(8,128)S(1)} %pad_maximum_fusion.7), channel_id=1, source_target_pairs={{0,1},{1,2},{2,3},{3,4},{4,5},{5,6},{6,7},{8,9},{9,10},{10,11},{11... | collective-permute-start | bytes 1572872 | tf_op jit(solution)/shard_map/ppermute | solution.py:15
  151.2 1.9 %collective-permute-start.3 = (f32[8,2,64,128]{3,2,1,0:T(8,128)S(1)}, f32[8,2,64,128]{3,2,1,0:T(8,128)S(1)}, u32[]{:S(2)}, u32[]{:S(2)}) collective-permute-start(f32[8,2,64,128]{3,2,1,0:T(8,128)S(1)} %pad_maximum_fusion.7), channel_id=1, source_target_pairs={{1,0},{2,1},{3,2},{4,3},{5,4},{6,5},{7,6},{9,8},{10,9},{11,10},{12... | collective-permute-start | bytes 1572872 | tf_op jit(solution)/shard_map/ppermute | solution.py:18
  153.2 0.1 broadcast_and_fusion
  153.3 6.9 %collective-permute-done.2 = f32[8,2,64,128]{3,2,1,0:T(8,128)S(1)} collective-permute-done((f32[8,2,64,128]{3,2,1,0:T(8,128)S(1)}, f32[8,2,64,128]{3,2,1,0:T(8,128)S(1)}, u32[]{:S(2)}, u32[]{:S(2)}) %collective-permute-start.2) | collective-permute-done | bytes 524320 | tf_op jit(solution)/shard_map/ppermute | solution.py:15
  160.2 4.4 %collective-permute-done.3 = f32[8,2,64,128]{3,2,1,0:T(8,128)S(1)} collective-permute-done((f32[8,2,64,128]{3,2,1,0:T(8,128)S(1)}, f32[8,2,64,128]{3,2,1,0:T(8,128)S(1)}, u32[]{:S(2)}, u32[]{:S(2)}) %collective-permute-start.3) | collective-permute-done | bytes 524320 | tf_op jit(solution)/shard_map/ppermute | solution.py:18
  164.6 0.2 pad_maximum_fusion
  164.7 1.6 add_select_fusion
  166.4 1.1 multiply_add_fusion
  (13 shorter events, 0.2 us)
Async XLA Ops:
  6.5 92.2 %all-reduce.4.cloned.1.call-start = ((), (), s32[]{:S(2)}) async-start(), calls=%async_computation.1 | async-start | bytes 5242880 | tf_op jit(solution)/shard_map/psum | solution.py:51
  29.9 68.8 %copy-start = (bf16[5120,128]{1,0:T(8,128)(2,1)S(1)}, bf16[5120,128]{1,0:T(8,128)(2,1)}, u32[]{:S(2)}) copy-start(bf16[5120,128]{1,0:T(8,128)(2,1)} %param.9) | copy-start | bytes 3932164
  29.9 107.2 %reduce-scatter.2.cloned.1.call-start = ((), (), s32[]{:S(2)}) async-start(), calls=%async_computation.2 | async-start | bytes 1310720 | tf_op jit(solution)/shard_map/reduce_scatter | solution.py:58
  108.4 28.7 %copy-start.1 = (f32[4,2,64,128]{3,2,1,0:T(8,128)S(1)}, f32[4,2,64,128]{3,2,1,0:T(8,128)}, u32[]{:S(2)}) copy-start(f32[4,2,64,128]{3,2,1,0:T(8,128)} %param.5) | copy-start | bytes 786436
  138.1 6.2 %collective-permute-start = (f32[2,2,64,128]{3,2,1,0:T(8,128)S(1)}, f32[2,2,64,128]{3,2,1,0:T(8,128)S(1)}, u32[]{:S(2)}, u32[]{:S(2)}) collective-permute-start(f32[2,2,64,128]{3,2,1,0:T(8,128)S(1)} %get-tuple-element.5), channel_id=1, source_target_pairs={{0,8},{8,16},{16,24},{1,9},{9,17},{17,25},{2,10},{10,18},{18,26},{... | collective-permute-start | bytes 393224 | tf_op jit(solution)/shard_map/ppermute | solution.py:15
  140.0 5.7 %collective-permute-start.1 = (f32[2,2,64,128]{3,2,1,0:T(8,128)S(1)}, f32[2,2,64,128]{3,2,1,0:T(8,128)S(1)}, u32[]{:S(2)}, u32[]{:S(2)}) collective-permute-start(f32[2,2,64,128]{3,2,1,0:T(8,128)S(1)} %get-tuple-element.6), channel_id=1, source_target_pairs={{8,0},{16,8},{24,16},{9,1},{17,9},{25,17},{10,2},{18,10},{26,18},{... | collective-permute-start | bytes 393224 | tf_op jit(solution)/shard_map/ppermute | solution.py:18
  145.8 14.4 %collective-permute-start.2 = (f32[8,2,64,128]{3,2,1,0:T(8,128)S(1)}, f32[8,2,64,128]{3,2,1,0:T(8,128)S(1)}, u32[]{:S(2)}, u32[]{:S(2)}) collective-permute-start(f32[8,2,64,128]{3,2,1,0:T(8,128)S(1)} %pad_maximum_fusion.7), channel_id=1, source_target_pairs={{0,1},{1,2},{2,3},{3,4},{4,5},{5,6},{6,7},{8,9},{9,10},{10,11},{11... | collective-permute-start | bytes 1572872 | tf_op jit(solution)/shard_map/ppermute | solution.py:15
  151.2 13.3 %collective-permute-start.3 = (f32[8,2,64,128]{3,2,1,0:T(8,128)S(1)}, f32[8,2,64,128]{3,2,1,0:T(8,128)S(1)}, u32[]{:S(2)}, u32[]{:S(2)}) collective-permute-start(f32[8,2,64,128]{3,2,1,0:T(8,128)S(1)} %pad_maximum_fusion.7), channel_id=1, source_target_pairs={{1,0},{2,1},{3,2},{4,3},{5,4},{6,5},{7,6},{9,8},{10,9},{11,10},{12... | collective-permute-start | bytes 1572872 | tf_op jit(solution)/shard_map/ppermute | solution.py:18
Sparse Core Ops, SparseCore 0:
  30.1 68.6 all-reduce.3
  111.2 25.9 reduce-scatter.1
where the time goes:
time: 176 us; the launch traced here: 174 us
  waiting for transfers between devices  108 us (61%)
  matrix products  14.3 us (8%)
  between operations  13.5 us (8%)
  blocking collectives  12.8 us (7%)
  starting transfers between devices  12.7 us (7%)
  other arithmetic  7.07 us (4%)
  local copies, waits for them, and re-layouts  5.47 us (3%)
    psum x1, waiting for transfers between devices, body(): total = lax.psum(partial_value, 'col')  68.7 us
    reduce_scatter x1, waiting for transfers between devices, body(): lax.psum_scatter(grad_terms, 'row', scatter_dimension=0, tiled=True)  26.1 us
    all_gather x1, blocking collectives, body(): lax.all_gather(image.astype(jnp.bfloat16), 'row', axis=0, tiled=True)  12.8 us
    ppermute x2, waiting for transfers between devices, padded_2(): lax.ppermute(lax.slice_in_dim(block, block.shape[dim] - width, None, axis...  7.82 us
    dot_general x1, matrix products, body(): jnp.einsum('ijkr,ijrf->jkf', v_factors, back, preferred_element_type=jnp....  7.72 us
    ppermute x2, starting transfers between devices, padded_2(): lax.ppermute(lax.slice_in_dim(block, block.shape[dim] - width, None, axis...  7.33 us
    dot_general x1, matrix products, body(): jnp.einsum('ijkr,ijrf->ikf', u_factors, coef, preferred_element_type=jnp....  6.62 us
    ppermute x2, waiting for transfers between devices, padded_2(): lax.ppermute(lax.slice_in_dim(block, 0, width, axis=dim), axis, backward)  5.83 us
  transfers between devices with their start and end apart: 6, of which 6 were waited for; matrix products, arithmetic and copies ran while one was open for 0% of the time, Pallas kernels for 0%

commit v1 on v0

--- a/solution.py
+++ b/solution.py
@@ -5,6 +5,20 @@
 
 diff_rate = 0.12
 edge_scale = 0.5
+
+
+def swap(value, axis, distance):
+    count = lax.axis_size(axis)
+    return lax.ppermute(value, axis, [(i, i ^ distance) for i in range(count)])
+
+
+def bits_of(count):
+    bit = 1
+    found = []
+    while bit < count:
+        found.append(bit)
+        bit *= 2
+    return found
 
 
 def padded_2(block, sides, width):
@@ -38,8 +52,19 @@
     row_tiles, col_tiles, tile_len, rank_max = u_factors.shape
     frames = image.shape[3]
     local_x, local_y = (image.shape[0], image.shape[1])
-    whole = lax.all_gather(image.astype(jnp.bfloat16), "row", axis=0, tiled=True)
+    rows, cols = lax.axis_size("row"), lax.axis_size("col")
+    me_row, me_col = lax.axis_index("row"), lax.axis_index("col")
+
+    have = {0: image.astype(jnp.bfloat16).reshape(-1, frames)}
+    for bit in reversed(bits_of(rows)):
+        for distance in list(have):
+            have[distance ^ bit] = swap(have[distance], "row", bit)
+    brick = have[0].shape[0]
+    whole = jnp.zeros((rows * brick, frames), jnp.bfloat16)
+    for distance, piece in have.items():
+        whole = lax.dynamic_update_slice(whole, piece, ((me_row ^ distance) * brick, 0))
     xtiles = whole.reshape(col_tiles, tile_len, frames)
+
     levels = lax.broadcasted_iota(jnp.int32, (row_tiles, col_tiles, rank_max), 2)
     mask = (levels < ranks[:, :, None]).astype(jnp.float32)
     coef = jnp.einsum("ijkr,jkf->ijrf", v_factors, xtiles, preferred_element_type=jnp.float32)
@@ -47,34 +72,52 @@
     partial_value = jnp.einsum(
         "ijkr,ijrf->ikf", u_factors, coef, preferred_element_type=jnp.float32
     )
-    partial_value = partial_value.reshape(row_tiles * tile_len, frames)
-    total = lax.psum(partial_value, "col")
-    resid = (total - measured.astype(jnp.float32)).astype(jnp.bfloat16)
-    resid = resid.reshape(row_tiles, tile_len, frames)
+    part_len = tile_len // cols
+    partial_value = partial_value.reshape(row_tiles, cols, part_len, frames)
+    own = lambda distance: lax.dynamic_index_in_dim(
+        partial_value, me_col ^ distance, axis=1, keepdims=False
+    )
+    evens = list(range(0, cols, 2))
+    crossed = swap(jnp.stack([own(e + 1) for e in evens]).astype(jnp.bfloat16), "col", 1)
+    chip = [own(e) + crossed[i].astype(jnp.float32) for i, e in enumerate(evens)]
+    total = chip[0]
+    for i, e in enumerate(evens[1:], 1):
+        total = total + swap(chip[i].astype(jnp.bfloat16), "col", e).astype(jnp.float32)
+    wanted = lax.dynamic_index_in_dim(
+        measured.reshape(row_tiles, cols, part_len, frames), me_col, axis=1, keepdims=False
+    )
+    mine = (total - wanted.astype(jnp.float32)).astype(jnp.bfloat16)
+    resid = jnp.zeros((row_tiles, tile_len, frames), jnp.bfloat16)
+    for e in evens:
+        piece = swap(mine, "col", e) if e else mine
+        other = swap(piece, "col", 1)
+        resid = lax.dynamic_update_slice(resid, piece, (0, (me_col ^ e) * part_len, 0))
+        resid = lax.dynamic_update_slice(resid, other, (0, (me_col ^ (e + 1)) * part_len, 0))
+
     back = jnp.einsum("ijkr,ikf->ijrf", u_factors, resid, preferred_element_type=jnp.float32)
     back = (back * mask[:, :, :, None]).astype(jnp.bfloat16)
     grad_terms = jnp.einsum("ijkr,ijrf->jkf", v_factors, back, preferred_element_type=jnp.float32)
-    grad_terms = grad_terms.reshape(col_tiles * tile_len, frames)
-    gradient = lax.psum_scatter(grad_terms, "row", scatter_dimension=0, tiled=True)
-    moved = image - gradient.reshape(image.shape)
+    grad_terms = grad_terms.reshape(rows, brick, frames)
+    part = {
+        distance: lax.dynamic_index_in_dim(grad_terms, me_row ^ distance, axis=0, keepdims=False)
+        for distance in range(rows)
+    }
+    for bit in bits_of(rows):
+        part = {
+            d: part[d] + swap(part[d ^ bit].astype(jnp.bfloat16), "row", bit).astype(jnp.float32)
+            for d in part
+            if not d & bit
+        }
+    moved = image - part[0].reshape(image.shape)
     extended = padded_2(moved, (("row", 0), ("col", 1)), 2)
     middle = diffuse_margin(extended)
-    grid_x = local_x * lax.axis_size("row")
-    grid_y = local_y * lax.axis_size("col")
-    pos_x = (
-        lax.broadcasted_iota(jnp.int32, (local_x + 2, 1, 1, 1), 0)
-        + lax.axis_index("row") * local_x
-        - 1
-    )
-    pos_y = (
-        lax.broadcasted_iota(jnp.int32, (1, local_y + 2, 1, 1), 1)
-        + lax.axis_index("col") * local_y
-        - 1
-    )
+    grid_x = local_x * rows
+    grid_y = local_y * cols
+    pos_x = lax.broadcasted_iota(jnp.int32, (local_x + 2, 1, 1, 1), 0) + me_row * local_x - 1
+    pos_y = lax.broadcasted_iota(jnp.int32, (1, local_y + 2, 1, 1), 1) + me_col * local_y - 1
     inside = (pos_x >= 0) & (pos_x < grid_x) & ((pos_y >= 0) & (pos_y < grid_y))
     middle = jnp.where(inside, middle, 0.0)
-    moved = diffuse_margin(middle)
-    return moved
+    return diffuse_margin(middle)
 
 
 def solution(mesh):

time: 176 us -> 113 us (0.64)
  waiting for transfers between devices: 108 us -> 40.1 us
  starting transfers between devices: 12.7 us -> 36.8 us
  between operations: 13.5 us -> 0.41 us
  blocking collectives: 12.8 us -> 0 us
  local copies, waits for them, and re-layouts: 5.47 us -> 13.9 us
    psum x1 -> x0, waiting for transfers between devices: 68.7 us -> none  [body(): total = lax.psum(partial_value, 'col')]
    reduce_scatter x1 -> x0, waiting for transfers between devices: 26.1 us -> none  [body(): lax.psum_scatter(grad_terms, 'row', scatter_dimension=0, tiled=True)]
    ppermute x0 -> x17, waiting for transfers between devices: none -> 24.9 us  [swap(): return lax.ppermute(value, axis, [(i, i ^ distance) for i in range(count)])]
    ppermute x0 -> x17, starting transfers between devices: none -> 20.6 us  [swap(): return lax.ppermute(value, axis, [(i, i ^ distance) for i in range(count)])]
    all_gather x1 -> x0, blocking collectives: 12.8 us -> none  [body(): lax.all_gather(image.astype(jnp.bfloat16), 'row', axis=0, tiled=True)]
    dynamic_slice x0 -> x6, local copies, waits for them, and re-layouts: none -> 6.87 us  [body(): lax.dynamic_index_in_dim(partial_value, me_col ^ distance, axis=1, keepdi...]
    ppermute x2, starting transfers between devices: 7.33 us -> 12.3 us  [padded_2(): lax.ppermute(lax.slice_in_dim(block, block.shape[dim] - width, None, axis...]
    unnamed x5 -> x12, local copies, waits for them, and re-layouts: 0.77 us -> 4.52 us
  transfers between devices with their start and end apart: 6 -> 21, of which waited for: 6 -> 13; matrix products, arithmetic and copies ran while one was open for 0% -> 7% of each run, Pallas kernels for 0% -> 0%
where the time goes in v1:
time: 113 us
  waiting for transfers between devices  40.1 us (35%)
  starting transfers between devices  36.8 us (33%)
  local copies, waits for them, and re-layouts  13.9 us (12%)
  matrix products  13.2 us (12%)
  other arithmetic  8.45 us (7%)
    ppermute x17, waiting for transfers between devices, swap(): return lax.ppermute(value, axis, [(i, i ^ distance) for i in range(count)])  24.9 us
    ppermute x17, starting transfers between devices, swap(): return lax.ppermute(value, axis, [(i, i ^ distance) for i in range(count)])  20.6 us
    ppermute x2, starting transfers between devices, padded_2(): lax.ppermute(lax.slice_in_dim(block, block.shape[dim] - width, None, axis...  12.3 us
    ppermute x2, waiting for transfers between devices, padded_2(): lax.ppermute(lax.slice_in_dim(block, 0, width, axis=dim), axis, backward)  8.19 us
    ppermute x2, waiting for transfers between devices, padded_2(): lax.ppermute(lax.slice_in_dim(block, block.shape[dim] - width, None, axis...  6.94 us
    dynamic_slice x6, local copies, waits for them, and re-layouts, body(): lax.dynamic_index_in_dim(partial_value, me_col ^ distance, axis=1, keepdi...  6.87 us
    dot_general x1, matrix products, body(): jnp.einsum('ijkr,ijrf->ikf', u_factors, coef, preferred_element_type=jnp....  6.62 us
    dot_general x1, matrix products, body(): jnp.einsum('ijkr,ijrf->jkf', v_factors, back, preferred_element_type=jnp....  6.6 us
  transfers between devices with their start and end apart: 21, of which 13 were waited for; matrix products, arithmetic and copies ran while one was open for 7% of the time, Pallas kernels for 0%

profile of v1, /device:TPU:19, one launch (start us, length us, event | category | flops | bytes accessed | tf_op | source)
XLA Modules:
  0.0 112.8 jit_solution(4268934017405715636)
XLA Ops:
  3.4 2.9 %collective-permute-done = bf16[512,128]{1,0:T(8,128)(2,1)S(1)} collective-permute-done((bf16[512,128]{1,0:T(8,128)(2,1)S(1)}, bf16[512,128]{1,0:T(8,128)(2,1)S(1)}, u32[]{:S(2)}, u32[]{:S(2)}) %collective-permute-start) | collective-permute-done | bytes 131104 | tf_op jit(solution)/shard_map/ppermute | solution.py:12
  6.3 5.0 %collective-permute-start.2 = (bf16[512,128]{1,0:T(8,128)(2,1)S(1)}, bf16[512,128]{1,0:T(8,128)(2,1)S(1)}, u32[]{:S(2)}, u32[]{:S(2)}) collective-permute-start(bf16[512,128]{1,0:T(8,128)(2,1)S(1)} %collective-permute-done), channel_id=1, source_target_pairs={{0,8},{8,0},{16,24},{24,16},{1,9},{9,1},{17,25},{25,17},{2,10},{10... | collective-permute-start | bytes 393224 | tf_op jit(solution)/shard_map/ppermute | solution.py:12
  11.4 3.3 %collective-permute-done.2 = bf16[512,128]{1,0:T(8,128)(2,1)S(1)} collective-permute-done((bf16[512,128]{1,0:T(8,128)(2,1)S(1)}, bf16[512,128]{1,0:T(8,128)(2,1)S(1)}, u32[]{:S(2)}, u32[]{:S(2)}) %collective-permute-start.2) | collective-permute-done | bytes 131104 | tf_op jit(solution)/shard_map/ppermute | solution.py:12
  14.7 6.6 %fusion.21 = f32[5,128,1024,1]{2,1,3,0:T(8,128)S(1)} fusion(bf16[5,2,1024,256]{3,2,1,0:T(8,128)(2,1)} %param.6, bf16[2,1024,128,1]{2,1,0,3:T(8,128)(2,1)S(1)} %bitcast.107, bf16[5,2,1024,256]{3,2,1,0:T(8,128)(2,1)} %param.7, f32[5,2,256]{2,1,0:T(2,128)S(1)} %compare_convert_fusion), kind=kOutput, calls=%fused_computation.15 | convolution fusion | flops 1342832640 | bytes 13641728 | tf_op jit(solution)/shard_map/ijkr,ijrf->ikf/dot_general | solution.py:72
  22.0 2.2 %constant_dynamic-slice_fusion.6 = (bf16[5,1,128,128]{2,1,3,0:T(2,128)(2,1)S(1)}, bf16[5,1,128,128]{2,1,3,0:T(2,128)(2,1)}, bf16[5,1,128,128]{2,1,3,0:T(2,128)(2,1)S(1)}, bf16[5,1,128,128]{2,1,3,0:T(2,128)(2,1)S(1)}) fusion(f32[5,8,128,128]{2,1,3,0:T(8,128)S(1)} %bitcast.102, s32[]{:T(128)S(6)} %select_n.85, s32[]{:T(128)S(6)} %select_n.87, ...), kind=kLoop, calls=%fused_computation.85 | loop fusion | bytes 1310736 | tf_op jit(solution)/shard_map/jit(dynamic_index_in_dim)/dynamic_slice | solution.py:77
  24.4 2.0 %copy.74 = bf16[5,1,128,128]{3,2,0,1:T(8,128)(2,1)} copy(bf16[5,1,128,128]{2,1,3,0:T(2,128)(2,1)} %get-tuple-element.10) | data formatting | bytes 327680
  27.4 1.9 %pad_maximum_fusion.7 = bf16[4,5,128,128]{3,2,1,0:T(8,128)(2,1)} fusion(bf16[1,5,128,128]{3,2,1,0:T(8,128)(2,1)S(1)} %bitcast.109, bf16[1,5,128,128]{3,2,1,0:T(8,128)(2,1)} %bitcast.110, bf16[1,5,128,128]{3,2,1,0:T(8,128)(2,1)} %bitcast.111, bf16[1,5,128,128]{3,2,1,0:T(8,128)(2,1)S(1)} %bitcast.112), kind=kLoop, calls=%fused_computation.31 | loop fusion | flops 983040 | bytes 1310720 | tf_op jit(solution)/shard_map/stack | solution.py:81
  30.4 2.1 %constant_dynamic-slice_fusion.2 = (f32[5,1,128,128]{2,1,3,0:T(1,128)}, f32[5,1,128,128]{2,1,3,0:T(1,128)}, f32[5,1,128,128]{2,1,3,0:T(1,128)S(1)}, f32[5,1,128,128]{2,1,3,0:T(1,128)S(1)}) fusion(f32[5,8,128,128]{2,1,3,0:T(8,128)S(1)} %bitcast.103, s32[]{:T(128)S(6)} %select_n.89, s32[]{:T(128)S(6)} %select_n.90, s32[]{:T(128)S(6)} %select_n.91, s32[]{:T(128)S(6)} %select_n.84), kind=kLoop, calls=%fused_computation.81 | loop fusion | bytes 2621456 | tf_op jit(solution)/shard_map/jit(dynamic_index_in_dim)/dynamic_slice | solution.py:77
  39.0 2.9 %collective-permute-done.4 = bf16[5,128,128]{2,1,0:T(8,128)(2,1)S(1)} collective-permute-done((bf16[5,128,128]{2,1,0:T(8,128)(2,1)S(1)}, bf16[5,128,128]{2,1,0:T(8,128)(2,1)S(1)}, u32[]{:S(2)}, u32[]{:S(2)}) %collective-permute-start.4) | collective-permute-done | bytes 163872 | tf_op jit(solution)/shard_map/ppermute | solution.py:12
  41.9 4.5 %collective-permute-done.6 = bf16[5,128,128]{2,1,0:T(8,128)(2,1)S(1)} collective-permute-done((bf16[5,128,128]{2,1,0:T(8,128)(2,1)S(1)}, bf16[5,128,128]{2,1,0:T(8,128)(2,1)S(1)}, u32[]{:S(2)}, u32[]{:S(2)}) %collective-permute-start.6) | collective-permute-done | bytes 163872 | tf_op jit(solution)/shard_map/ppermute | solution.py:12
  51.7 2.4 %collective-permute-done.8 = bf16[5,128,128]{2,1,0:T(8,128)(2,1)S(1)} collective-permute-done((bf16[5,128,128]{2,1,0:T(8,128)(2,1)S(1)}, bf16[5,128,128]{2,1,0:T(8,128)(2,1)S(1)}, u32[]{:S(2)}, u32[]{:S(2)}) %collective-permute-start.8) | collective-permute-done | bytes 163872 | tf_op jit(solution)/shard_map/ppermute | solution.py:12
  56.0 3.5 %collective-permute-start.11 = (bf16[5,128,128]{2,1,0:T(8,128)(2,1)S(1)}, bf16[5,128,128]{2,1,0:T(8,128)(2,1)S(1)}, u32[]{:S(2)}, u32[]{:S(2)}) collective-permute-start(bf16[5,128,128]{2,1,0:T(8,128)(2,1)S(1)} %collective-permute-done.10), channel_id=1, source_target_pairs={{0,1},{1,0},{2,3},{3,2},{4,5},{5,4},{6,7},{7,6},{8,9},{9,8},{10,11... | collective-permute-start | bytes 491528 | tf_op jit(solution)/shard_map/ppermute | solution.py:12
  61.4 6.6 %fusion.8 = f32[2,1024,128]{1,2,0:T(8,128)S(1)} fusion(bf16[5,2,1024,256]{3,2,1,0:T(8,128)(2,1)} %param.7, bf16[5,2,1024,256]{3,2,1,0:T(8,128)(2,1)} %param.6, bf16[5,1024,128]{1,2,0:T(8,128)(2,1)S(1)} %constant_dynamic-update-slice_fusion, f32[5,2,256]{2,0,1:T(8,128)S(1)} %copy.65), kind=kOutput, calls=%fused_computation.10 | convolution fusion | flops 1342832640 | bytes 12855296 | tf_op jit(solution)/shard_map/ijkr,ijrf->jkf/dot_general | solution.py:99
  70.0 3.4 %collective-permute-done.15 = bf16[512,128]{1,0:T(8,128)(2,1)S(1)} collective-permute-done((bf16[512,128]{1,0:T(8,128)(2,1)S(1)}, bf16[512,128]{1,0:T(8,128)(2,1)S(1)}, u32[]{:S(2)}, u32[]{:S(2)}) %collective-permute-start.15) | collective-permute-done | bytes 131104 | tf_op jit(solution)/shard_map/ppermute | solution.py:12
  73.5 2.7 %collective-permute-done.14 = bf16[512,128]{1,0:T(8,128)(2,1)S(1)} collective-permute-done((bf16[512,128]{1,0:T(8,128)(2,1)S(1)}, bf16[512,128]{1,0:T(8,128)(2,1)S(1)}, u32[]{:S(2)}, u32[]{:S(2)}) %collective-permute-start.14) | collective-permute-done | bytes 131104 | tf_op jit(solution)/shard_map/ppermute | solution.py:12
  76.2 2.1 %collective-permute-done.16 = bf16[512,128]{1,0:T(8,128)(2,1)S(1)} collective-permute-done((bf16[512,128]{1,0:T(8,128)(2,1)S(1)}, bf16[512,128]{1,0:T(8,128)(2,1)S(1)}, u32[]{:S(2)}, u32[]{:S(2)}) %collective-permute-start.16) | collective-permute-done | bytes 131104 | tf_op jit(solution)/shard_map/ppermute | solution.py:12
  78.4 6.7 %collective-permute-start.17 = (f32[2,2,64,128]{3,2,1,0:T(8,128)S(1)}, f32[2,2,64,128]{3,2,1,0:T(8,128)S(1)}, u32[]{:S(2)}, u32[]{:S(2)}) collective-permute-start(f32[2,2,64,128]{3,2,1,0:T(8,128)S(1)} %get-tuple-element.18), channel_id=1, source_target_pairs={{0,8},{8,16},{16,24},{1,9},{9,17},{17,25},{2,10},{10,18},{18,26},{... | collective-permute-start | bytes 393224 | tf_op jit(solution)/shard_map/ppermute | solution.py:29
  85.2 1.9 %collective-permute-start.18 = (f32[2,2,64,128]{3,2,1,0:T(8,128)S(1)}, f32[2,2,64,128]{3,2,1,0:T(8,128)S(1)}, u32[]{:S(2)}, u32[]{:S(2)}) collective-permute-start(f32[2,2,64,128]{3,2,1,0:T(8,128)S(1)} %get-tuple-element.19), channel_id=1, source_target_pairs={{8,0},{16,8},{24,16},{9,1},{17,9},{25,17},{10,2},{18,10},{26,18},{... | collective-permute-start | bytes 393224 | tf_op jit(solution)/shard_map/ppermute | solution.py:32
  87.1 3.8 %collective-permute-done.18 = f32[2,2,64,128]{3,2,1,0:T(8,128)S(1)} collective-permute-done((f32[2,2,64,128]{3,2,1,0:T(8,128)S(1)}, f32[2,2,64,128]{3,2,1,0:T(8,128)S(1)}, u32[]{:S(2)}, u32[]{:S(2)}) %collective-permute-start.18) | collective-permute-done | bytes 131104 | tf_op jit(solution)/shard_map/ppermute | solution.py:32
  90.9 5.6 %collective-permute-start.19 = (f32[8,2,64,128]{3,2,1,0:T(8,128)S(1)}, f32[8,2,64,128]{3,2,1,0:T(8,128)S(1)}, u32[]{:S(2)}, u32[]{:S(2)}) collective-permute-start(f32[8,2,64,128]{3,2,1,0:T(8,128)S(1)} %pad_maximum_fusion.8), channel_id=1, source_target_pairs={{0,1},{1,2},{2,3},{3,4},{4,5},{5,6},{6,7},{8,9},{9,10},{10,11},{11... | collective-permute-start | bytes 1572872 | tf_op jit(solution)/shard_map/ppermute | solution.py:29
  96.5 1.9 %collective-permute-start.20 = (f32[8,2,64,128]{3,2,1,0:T(8,128)S(1)}, f32[8,2,64,128]{3,2,1,0:T(8,128)S(1)}, u32[]{:S(2)}, u32[]{:S(2)}) collective-permute-start(f32[8,2,64,128]{3,2,1,0:T(8,128)S(1)} %pad_maximum_fusion.8), channel_id=1, source_target_pairs={{1,0},{2,1},{3,2},{4,3},{5,4},{6,5},{7,6},{9,8},{10,9},{11,10},{12... | collective-permute-start | bytes 1572872 | tf_op jit(solution)/shard_map/ppermute | solution.py:32
  98.6 6.9 %collective-permute-done.19 = f32[8,2,64,128]{3,2,1,0:T(8,128)S(1)} collective-permute-done((f32[8,2,64,128]{3,2,1,0:T(8,128)S(1)}, f32[8,2,64,128]{3,2,1,0:T(8,128)S(1)}, u32[]{:S(2)}, u32[]{:S(2)}) %collective-permute-start.19) | collective-permute-done | bytes 524320 | tf_op jit(solution)/shard_map/ppermute | solution.py:29
  105.5 4.4 %collective-permute-done.20 = f32[8,2,64,128]{3,2,1,0:T(8,128)S(1)} collective-permute-done((f32[8,2,64,128]{3,2,1,0:T(8,128)S(1)}, f32[8,2,64,128]{3,2,1,0:T(8,128)S(1)}, u32[]{:S(2)}, u32[]{:S(2)}) %collective-permute-start.20) | collective-permute-done | bytes 524320 | tf_op jit(solution)/shard_map/ppermute | solution.py:32
  110.1 1.6 %add_select_fusion = f32[6,4,64,128]{3,2,1,0:T(8,128)S(1)} fusion(f32[8,6,64,128]{3,2,1,0:T(8,128)S(1)} %pad_maximum_fusion, f32[2,2,64,128]{3,2,1,0:T(8,128)S(1)} %collective-permute-done.18, f32[4,2,64,128]{3,2,1,0:T(8,128)S(1)} %sub.51, f32[2,2,64,128]{3,2,1,0:T(8,128)S(1)} %collective-permute-done.17, f32[8,2,64,128]{3,2,1,0:T(8,128)S(1)} %collective-permute-done.19, ...), kind=kLoop, calls=%fused_computation.30 | loop fusion | flops 8650752 | bytes 6292480 | tf_op jit(solution)/shard_map/jit(_where)/select_n | solution.py:119
  (79 shorter events, 25.4 us)
Async XLA Ops:
  1.0 5.4 %collective-permute-start = (bf16[512,128]{1,0:T(8,128)(2,1)S(1)}, bf16[512,128]{1,0:T(8,128)(2,1)S(1)}, u32[]{:S(2)}, u32[]{:S(2)}) collective-permute-start(bf16[512,128]{1,0:T(8,128)(2,1)S(1)} %bitcast.113), channel_id=1, source_target_pairs={{0,16},{8,24},{16,0},{24,8},{1,17},{9,25},{17,1},{25,9},{2,18},{10... | collective-permute-start | bytes 393224 | tf_op jit(solution)/shard_map/ppermute | solution.py:12
  1.1 10.3 %collective-permute-start.1 = (bf16[512,128]{1,0:T(8,128)(2,1)S(1)}, bf16[512,128]{1,0:T(8,128)(2,1)S(1)}, u32[]{:S(2)}, u32[]{:S(2)}) collective-permute-start(bf16[512,128]{1,0:T(8,128)(2,1)S(1)} %bitcast.114), channel_id=1, source_target_pairs={{0,8},{8,0},{16,24},{24,16},{1,9},{9,1},{17,25},{25,17},{2,10},{10... | collective-permute-start | bytes 393224 | tf_op jit(solution)/shard_map/ppermute | solution.py:12
  6.3 8.4 %collective-permute-start.2 = (bf16[512,128]{1,0:T(8,128)(2,1)S(1)}, bf16[512,128]{1,0:T(8,128)(2,1)S(1)}, u32[]{:S(2)}, u32[]{:S(2)}) collective-permute-start(bf16[512,128]{1,0:T(8,128)(2,1)S(1)} %collective-permute-done), channel_id=1, source_target_pairs={{0,8},{8,0},{16,24},{24,16},{1,9},{9,1},{17,25},{25,17},{2,10},{10... | collective-permute-start | bytes 393224 | tf_op jit(solution)/shard_map/ppermute | solution.py:12
  22.0 2.2 %copy-start = (f32[80,8,8,128]{3,2,1,0:T(8,128)}, f32[80,8,8,128]{3,2,1,0:T(8,128)S(1)}, u32[]{:S(2)}) copy-start(f32[80,8,8,128]{3,2,1,0:T(8,128)S(1)} %copy.77) | copy-start | bytes 7864324
  24.4 6.0 %copy-start.1 = (f32[80,8,8,128]{3,2,1,0:T(8,128)S(1)}, f32[80,8,8,128]{3,2,1,0:T(8,128)}, u32[]{:S(2)}) copy-start(f32[80,8,8,128]{3,2,1,0:T(8,128)} %copy-done) | copy-start | bytes 7864324
  29.3 5.6 %collective-permute-start.3 = (bf16[4,5,128,128]{3,2,1,0:T(8,128)(2,1)}, bf16[4,5,128,128]{3,2,1,0:T(8,128)(2,1)}, u32[]{:S(2)}, u32[]{:S(2)}) collective-permute-start(bf16[4,5,128,128]{3,2,1,0:T(8,128)(2,1)} %pad_maximum_fusion.7), channel_id=1, source_target_pairs={{0,1},{1,0},{2,3},{3,2},{4,5},{5,4},{6,7},{7,6},{8,9},{9,8},{10,11... | collective-permute-start | bytes 1966088 | tf_op jit(solution)/shard_map/ppermute | solution.py:12
  36.1 5.8 %collective-permute-start.4 = (bf16[5,128,128]{2,1,0:T(8,128)(2,1)S(1)}, bf16[5,128,128]{2,1,0:T(8,128)(2,1)S(1)}, u32[]{:S(2)}, u32[]{:S(2)}) collective-permute-start(bf16[5,128,128]{2,1,0:T(8,128)(2,1)S(1)} %get-tuple-element.15), channel_id=1, source_target_pairs={{0,2},{1,3},{2,0},{3,1},{4,6},{5,7},{6,4},{7,5},{8,10},{9,11},{10,... | collective-permute-start | bytes 491528 | tf_op jit(solution)/shard_map/ppermute | solution.py:12
  36.4 5.5 %collective-permute-start.5 = (bf16[5,128,128]{2,1,0:T(8,128)(2,1)S(1)}, bf16[5,128,128]{2,1,0:T(8,128)(2,1)S(1)}, u32[]{:S(2)}, u32[]{:S(2)}) collective-permute-start(bf16[5,128,128]{2,1,0:T(8,128)(2,1)S(1)} %get-tuple-element.17), channel_id=1, source_target_pairs={{0,4},{1,5},{2,6},{3,7},{4,0},{5,1},{6,2},{7,3},{8,12},{9,13},{10,... | collective-permute-start | bytes 491528 | tf_op jit(solution)/shard_map/ppermute | solution.py:12
  37.6 8.7 %collective-permute-start.6 = (bf16[5,128,128]{2,1,0:T(8,128)(2,1)S(1)}, bf16[5,128,128]{2,1,0:T(8,128)(2,1)S(1)}, u32[]{:S(2)}, u32[]{:S(2)}) collective-permute-start(bf16[5,128,128]{2,1,0:T(8,128)(2,1)S(1)} %get-tuple-element.16), channel_id=1, source_target_pairs={{0,6},{1,7},{2,4},{3,5},{4,2},{5,3},{6,0},{7,1},{8,14},{9,15},{10,... | collective-permute-start | bytes 491528 | tf_op jit(solution)/shard_map/ppermute | solution.py:12
  47.5 4.0 %collective-permute-start.7 = (bf16[5,128,128]{2,1,0:T(8,128)(2,1)S(1)}, bf16[5,128,128]{2,1,0:T(8,128)(2,1)S(1)}, u32[]{:S(2)}, u32[]{:S(2)}) collective-permute-start(bf16[5,128,128]{2,1,0:T(8,128)(2,1)S(1)} %fusion.32), channel_id=1, source_target_pairs={{0,1},{1,0},{2,3},{3,2},{4,5},{5,4},{6,7},{7,6},{8,9},{9,8},{10,11... | collective-permute-start | bytes 491528 | tf_op jit(solution)/shard_map/ppermute | solution.py:12
  48.4 5.7 %collective-permute-start.8 = (bf16[5,128,128]{2,1,0:T(8,128)(2,1)S(1)}, bf16[5,128,128]{2,1,0:T(8,128)(2,1)S(1)}, u32[]{:S(2)}, u32[]{:S(2)}) collective-permute-start(bf16[5,128,128]{2,1,0:T(8,128)(2,1)S(1)} %fusion.32), channel_id=1, source_target_pairs={{0,2},{1,3},{2,0},{3,1},{4,6},{5,7},{6,4},{7,5},{8,10},{9,11},{10,... | collective-permute-start | bytes 491528 | tf_op jit(solution)/shard_map/ppermute | solution.py:12
  49.1 6.7 %collective-permute-start.10 = (bf16[5,128,128]{2,1,0:T(8,128)(2,1)S(1)}, bf16[5,128,128]{2,1,0:T(8,128)(2,1)S(1)}, u32[]{:S(2)}, u32[]{:S(2)}) collective-permute-start(bf16[5,128,128]{2,1,0:T(8,128)(2,1)S(1)} %fusion.32), channel_id=1, source_target_pairs={{0,4},{1,5},{2,6},{3,7},{4,0},{5,1},{6,2},{7,3},{8,12},{9,13},{10,... | collective-permute-start | bytes 491528 | tf_op jit(solution)/shard_map/ppermute | solution.py:12
  50.4 9.1 %collective-permute-start.12 = (bf16[5,128,128]{2,1,0:T(8,128)(2,1)S(1)}, bf16[5,128,128]{2,1,0:T(8,128)(2,1)S(1)}, u32[]{:S(2)}, u32[]{:S(2)}) collective-permute-start(bf16[5,128,128]{2,1,0:T(8,128)(2,1)S(1)} %fusion.32), channel_id=1, source_target_pairs={{0,6},{1,7},{2,4},{3,5},{4,2},{5,3},{6,0},{7,1},{8,14},{9,15},{10,... | collective-permute-start | bytes 491528 | tf_op jit(solution)/shard_map/ppermute | solution.py:12
  54.1 5.7 %collective-permute-start.9 = (bf16[5,128,128]{2,1,0:T(8,128)(2,1)S(1)}, bf16[5,128,128]{2,1,0:T(8,128)(2,1)S(1)}, u32[]{:S(2)}, u32[]{:S(2)}) collective-permute-start(bf16[5,128,128]{2,1,0:T(8,128)(2,1)S(1)} %collective-permute-done.8), channel_id=1, source_target_pairs={{0,1},{1,0},{2,3},{3,2},{4,5},{5,4},{6,7},{7,6},{8,9},{9,8},{10,11... | collective-permute-start | bytes 491528 | tf_op jit(solution)/shard_map/ppermute | solution.py:12
  56.0 4.6 %collective-permute-start.11 = (bf16[5,128,128]{2,1,0:T(8,128)(2,1)S(1)}, bf16[5,128,128]{2,1,0:T(8,128)(2,1)S(1)}, u32[]{:S(2)}, u32[]{:S(2)}) collective-permute-start(bf16[5,128,128]{2,1,0:T(8,128)(2,1)S(1)} %collective-permute-done.10), channel_id=1, source_target_pairs={{0,1},{1,0},{2,3},{3,2},{4,5},{5,4},{6,7},{7,6},{8,9},{9,8},{10,11... | collective-permute-start | bytes 491528 | tf_op jit(solution)/shard_map/ppermute | solution.py:12
  59.7 1.5 %collective-permute-start.13 = (bf16[5,128,128]{2,1,0:T(8,128)(2,1)S(1)}, bf16[5,128,128]{2,1,0:T(8,128)(2,1)S(1)}, u32[]{:S(2)}, u32[]{:S(2)}) collective-permute-start(bf16[5,128,128]{2,1,0:T(8,128)(2,1)S(1)} %collective-permute-done.12), channel_id=1, source_target_pairs={{0,1},{1,0},{2,3},{3,2},{4,5},{5,4},{6,7},{7,6},{8,9},{9,8},{10,11... | collective-permute-start | bytes 491528 | tf_op jit(solution)/shard_map/ppermute | solution.py:12
  68.3 10.0 %copy-start.2 = (f32[4,2,64,128]{3,2,1,0:T(8,128)S(1)}, f32[4,2,64,128]{3,2,1,0:T(8,128)}, u32[]{:S(2)}) copy-start(f32[4,2,64,128]{3,2,1,0:T(8,128)} %param.5) | copy-start | bytes 786436
  68.4 5.0 %collective-permute-start.15 = (bf16[512,128]{1,0:T(8,128)(2,1)S(1)}, bf16[512,128]{1,0:T(8,128)(2,1)S(1)}, u32[]{:S(2)}, u32[]{:S(2)}) collective-permute-start(bf16[512,128]{1,0:T(8,128)(2,1)S(1)} %get-tuple-element.14), channel_id=1, source_target_pairs={{0,8},{8,0},{16,24},{24,16},{1,9},{9,1},{17,25},{25,17},{2,10},{10... | collective-permute-start | bytes 393224 | tf_op jit(solution)/shard_map/ppermute | solution.py:12
  69.9 6.3 %collective-permute-start.14 = (bf16[512,128]{1,0:T(8,128)(2,1)S(1)}, bf16[512,128]{1,0:T(8,128)(2,1)S(1)}, u32[]{:S(2)}, u32[]{:S(2)}) collective-permute-start(bf16[512,128]{1,0:T(8,128)(2,1)S(1)} %get-tuple-element.13), channel_id=1, source_target_pairs={{0,8},{8,0},{16,24},{24,16},{1,9},{9,1},{17,25},{25,17},{2,10},{10... | collective-permute-start | bytes 393224 | tf_op jit(solution)/shard_map/ppermute | solution.py:12
  73.4 4.9 %collective-permute-start.16 = (bf16[512,128]{1,0:T(8,128)(2,1)S(1)}, bf16[512,128]{1,0:T(8,128)(2,1)S(1)}, u32[]{:S(2)}, u32[]{:S(2)}) collective-permute-start(bf16[512,128]{1,0:T(8,128)(2,1)S(1)} %fusion.41), channel_id=1, source_target_pairs={{0,16},{8,24},{16,0},{24,8},{1,17},{9,25},{17,1},{25,9},{2,18},{10... | collective-permute-start | bytes 393224 | tf_op jit(solution)/shard_map/ppermute | solution.py:12
  78.4 8.7 %collective-permute-start.17 = (f32[2,2,64,128]{3,2,1,0:T(8,128)S(1)}, f32[2,2,64,128]{3,2,1,0:T(8,128)S(1)}, u32[]{:S(2)}, u32[]{:S(2)}) collective-permute-start(f32[2,2,64,128]{3,2,1,0:T(8,128)S(1)} %get-tuple-element.18), channel_id=1, source_target_pairs={{0,8},{8,16},{16,24},{1,9},{9,17},{17,25},{2,10},{10,18},{18,26},{... | collective-permute-start | bytes 393224 | tf_op jit(solution)/shard_map/ppermute | solution.py:29
  85.2 5.7 %collective-permute-start.18 = (f32[2,2,64,128]{3,2,1,0:T(8,128)S(1)}, f32[2,2,64,128]{3,2,1,0:T(8,128)S(1)}, u32[]{:S(2)}, u32[]{:S(2)}) collective-permute-start(f32[2,2,64,128]{3,2,1,0:T(8,128)S(1)} %get-tuple-element.19), channel_id=1, source_target_pairs={{8,0},{16,8},{24,16},{9,1},{17,9},{25,17},{10,2},{18,10},{26,18},{... | collective-permute-start | bytes 393224 | tf_op jit(solution)/shard_map/ppermute | solution.py:32
  90.9 14.6 %collective-permute-start.19 = (f32[8,2,64,128]{3,2,1,0:T(8,128)S(1)}, f32[8,2,64,128]{3,2,1,0:T(8,128)S(1)}, u32[]{:S(2)}, u32[]{:S(2)}) collective-permute-start(f32[8,2,64,128]{3,2,1,0:T(8,128)S(1)} %pad_maximum_fusion.8), channel_id=1, source_target_pairs={{0,1},{1,2},{2,3},{3,4},{4,5},{5,6},{6,7},{8,9},{9,10},{10,11},{11... | collective-permute-start | bytes 1572872 | tf_op jit(solution)/shard_map/ppermute | solution.py:29
  96.5 13.4 %collective-permute-start.20 = (f32[8,2,64,128]{3,2,1,0:T(8,128)S(1)}, f32[8,2,64,128]{3,2,1,0:T(8,128)S(1)}, u32[]{:S(2)}, u32[]{:S(2)}) collective-permute-start(f32[8,2,64,128]{3,2,1,0:T(8,128)S(1)} %pad_maximum_fusion.8), channel_id=1, source_target_pairs={{1,0},{2,1},{3,2},{4,3},{5,4},{6,5},{7,6},{9,8},{10,9},{11,10},{12... | collective-permute-start | bytes 1572872 | tf_op jit(solution)/shard_map/ppermute | solution.py:32

commit v2 on v0

v2 whole, which is shorter than its diff:
```python
import functools

import jax
import jax.numpy as jnp
from jax import lax
from jax.experimental import pallas as pl
from jax.experimental.pallas import tpu as pltpu
from jax.sharding import PartitionSpec as P

diff_rate = 0.12
edge_scale = 0.5
BF16, F32 = jnp.bfloat16, jnp.float32


def swap(value, axis, distance):
    count = lax.axis_size(axis)
    return lax.ppermute(value, axis, [(i, i ^ distance) for i in range(count)])


def swap_odd(value, axis):
    count = lax.axis_size(axis)
    pairs = [(i, i + 1) for i in range(1, count - 1, 2)]
    return lax.ppermute(value, axis, pairs + [(b, a) for a, b in pairs])


def bits_of(count):
    bit, found = 1, []
    while bit < count:
        found.append(bit)
        bit *= 2
    return found


def dot_nt(a, b):
    return lax.dot_general(a, b, (((1,), (1,)), ((), ())), preferred_element_type=F32)


def call(kernel, name, scalars, arrays, outs, scratch=()):
    smem = pl.BlockSpec(memory_space=pltpu.SMEM)
    vmem = pl.BlockSpec(memory_space=pltpu.VMEM)
    return pl.pallas_call(
        kernel,
        name=name,
        out_shape=[jax.ShapeDtypeStruct(shape, kind) for shape, kind in outs],
        in_specs=[smem] * len(scalars) + [vmem] * len(arrays),
        out_specs=[vmem] * len(outs),
        scratch_shapes=list(scratch),
    )(*scalars, *arrays)


def cast_kernel(image_ref, out_ref):
    flat = image_ref[...].reshape(out_ref.shape[1], out_ref.shape[0])
    out_ref[...] = flat.T.astype(BF16)


def keep_rank(value, rank):
    level = lax.broadcasted_iota(jnp.int32, value.shape, 1)
    return jnp.where(level < rank, value, 0.0).astype(BF16)


def half_rows(u_ref, coef_ref, i, core):
    total = None
    for j in range(u_ref.shape[1]):
        rows = u_ref[i, j, :, core]
        rows = rows.reshape(rows.shape[0] * rows.shape[1], rows.shape[2])
        term = dot_nt(rows, coef_ref[i, j])
        total = term if total is None else total + term
    return total.reshape(u_ref.shape[2], u_ref.shape[4], total.shape[1])


def forward_kernel(count, at_ref, ranks_ref, *refs):
    pieces, (u_ref, v_ref, cross_ref, coef_ref, held) = refs[:count], refs[count:]
    row_tiles, col_tiles, chips = u_ref.shape[:3]
    me_row, me_col = at_ref[0], at_ref[1]
    for distance in range(count):
        held[me_row ^ distance] = pieces[distance][...]
    per_tile = count // col_tiles
    for j in range(col_tiles):
        lhs = jnp.concatenate([held[j * per_tile + p] for p in range(per_tile)], axis=1)
        for i in range(row_tiles):
            value = jnp.dot(lhs, v_ref[i, j], preferred_element_type=F32)
            coef_ref[i, j] = keep_rank(value, ranks_ref[i, j])
    chip, core = me_col // 2, me_col % 2
    for i in range(row_tiles):
        value = half_rows(u_ref, coef_ref, i, 1 - core)
        for q in range(chips):
            cross_ref[chip ^ q, i] = value[q].astype(cross_ref.dtype)


def own_kernel(at_ref, u_ref, coef_ref, mine_ref):
    me_col = at_ref[1]
    chip, core = me_col // 2, me_col % 2
    for i in range(u_ref.shape[0]):
        value = half_rows(u_ref, coef_ref, i, core)
        for q in range(u_ref.shape[2]):
            mine_ref[chip ^ q, i] = value[q]


def sum_kernel(at_ref, mine_ref, crossed_ref, measured_ref, own_ref, *send_refs):
    me_col = at_ref[1]
    value = mine_ref[0] + crossed_ref[0].astype(F32)
    own_ref[...] = value - measured_ref[:, me_col].astype(F32)
    for q, send_ref in enumerate(send_refs, 1):
        send_ref[...] = (mine_ref[q] + crossed_ref[q].astype(F32)).astype(BF16)


def resid_kernel(own_ref, *refs):
    out_ref = refs[-1]
    for i in range(own_ref.shape[0]):
        value = own_ref[i]
        for ref in refs[:-1]:
            value = value + ref[i].astype(F32)
        out_ref[i] = value.T.astype(BF16)


def gradient_piece(v_ref, back_ref, start, brick):
    tile_len = v_ref.shape[2]
    tile = start // tile_len
    inside = pl.multiple_of(start % tile_len, brick)
    total = None
    for i in range(v_ref.shape[0]):
        term = dot_nt(v_ref[i, tile, pl.ds(inside, brick)], back_ref[i, tile])
        total = term if total is None else total + term
    return total


def adjoint_kernel(count, at_ref, ranks_ref, *refs):
    pieces, (u_ref, v_ref, back_ref), rest = refs[:count], refs[count : count + 3], refs[count + 3 :]
    outs, held = rest[:-1], rest[-1]
    row_tiles, col_tiles = u_ref.shape[:2]
    me_row, me_col = at_ref[0], at_ref[1]
    for distance in range(count):
        held[me_col ^ distance] = pieces[distance][...]
    for i in range(row_tiles):
        lhs = jnp.concatenate([held[p, i] for p in range(count)], axis=1)
        for j in range(col_tiles):
            value = jnp.dot(lhs, u_ref[i, j], preferred_element_type=F32)
            back_ref[i, j] = keep_rank(value, ranks_ref[i, j])
    for n, out_ref in enumerate(outs):
        brick = out_ref.shape[0]
        out_ref[...] = gradient_piece(v_ref, back_ref, (me_row ^ (2 * n + 1)) * brick, brick).astype(BF16)


def adjoint_rest_kernel(at_ref, v_ref, back_ref, *outs):
    for n, out_ref in enumerate(outs):
        brick = out_ref.shape[0]
        out_ref[...] = gradient_piece(v_ref, back_ref, (at_ref[0] ^ (2 * n)) * brick, brick)


def move_kernel(count, at_ref, image_ref, part_ref, *refs):
    received, (moved_ref, even_ref, odd_ref, side_ref) = refs[:count], refs[count:]
    gradient = part_ref[...]
    for ref in received:
        gradient = gradient + ref[...].astype(F32)
    moved = image_ref[...] - gradient.reshape(image_ref.shape)
    moved_ref[...] = moved
    side_ref[...] = moved.astype(BF16)
    width = even_ref.shape[0]
    far = image_ref.shape[0] - width
    odd = at_ref[0] % 2
    even_ref[...] = moved_ref[pl.ds((1 - odd) * far, width)].astype(BF16)
    odd_ref[...] = moved_ref[pl.ds(odd * far, width)].astype(BF16)


def corner_kernel(at_ref, even_ref, odd_ref, to_even_ref, to_odd_ref):
    last = even_ref.shape[1] - 1
    row_odd, col_odd = at_ref[0] % 2, at_ref[1] % 2
    near, side = (1 - col_odd) * last, col_odd * last
    for out_ref, y in ((to_even_ref, near), (to_odd_ref, side)):
        low = jnp.where(row_odd == 1, even_ref[1, y], odd_ref[1, y])
        high = jnp.where(row_odd == 1, odd_ref[0, y], even_ref[0, y])
        out_ref[0] = low
        out_ref[1] = high


def flux(delta):
    scaled = delta / edge_scale
    return delta / (1.0 + scaled * scaled)


def diffuse_kernel(at_ref, moved_ref, row_even, row_odd, col_even, col_odd, corner_even, corner_odd, out_ref, field):
    nx, ny, depth, frames = moved_ref.shape
    rows, cols = at_ref[2], at_ref[3]
    me_row, me_col = at_ref[0], at_ref[1]
    r_odd, c_odd = me_row % 2, me_col % 2
    r_even, c_even = 1 - r_odd, 1 - c_odd
    field[2 : 2 + nx, 2 : 2 + ny] = moved_ref[...]
    far_x, far_y = nx + 2, ny + 2
    field[pl.ds(r_even * far_x, 2), 2 : 2 + ny] = row_even[...].astype(F32)
    field[pl.ds(r_odd * far_x, 2), 2 : 2 + ny] = row_odd[...].astype(F32)
    field[2 : 2 + nx, pl.ds(c_even * far_y, 2)] = col_even[...].astype(F32)
    field[2 : 2 + nx, pl.ds(c_odd * far_y, 2)] = col_odd[...].astype(F32)
    for y, ref in ((c_even * (ny + 1) + 1, corner_even), (c_odd * (ny + 1) + 1, corner_odd)):
        field[1, y] = ref[0].astype(F32)
        field[nx + 2, y] = ref[1].astype(F32)
    level = lax.broadcasted_iota(jnp.int32, (depth, frames), 0)
    low_x, high_x = me_row > 0, me_row < rows - 1
    low_y, high_y = me_col > 0, me_col < cols - 1

    def along_depth(u):
        below = jnp.where(level == 0, 0.0, pltpu.roll(u, 1, 0))
        down = flux(u - below)
        up = jnp.where(level == depth - 1, flux(-u), pltpu.roll(down, depth - 1, 0))
        return up - down

    def diffuse(cells, get):
        faces = {}

        def face(kind, x, y):
            key = (kind, x, y)
            if key not in faces:
                x2, y2 = (x + 1, y) if kind == 0 else (x, y + 1)
                faces[key] = flux(get(x2, y2) - get(x, y))
            return faces[key]

        new = {}
        for x, y in cells:
            u = get(x, y)
            total = face(0, x, y) - face(0, x - 1, y)
            total = total + (face(1, x, y) - face(1, x, y - 1))
            new[x, y] = u + diff_rate * (total + along_depth(u))
        return new

    inner = [(x, y) for x in range(2, 2 + nx) for y in range(2, 2 + ny)]
    ring = [(x, y) for x in (1, nx + 2) for y in range(2, 2 + ny)]
    ring += [(x, y) for x in range(2, 2 + nx) for y in (1, ny + 2)]
    first = diffuse(sorted(inner + ring), lambda x, y: field[x, y])
    for x, y in first:
        value = first[x, y]
        for at, end, open_end in ((x, 1, low_x), (x, nx + 2, high_x), (y, 1, low_y), (y, ny + 2, high_y)):
            if at == end:
                value = jnp.where(open_end, value, 0.0)
        field[x, y] = value
    second = diffuse(inner, lambda x, y: field[x, y])
    for x, y in inner:
        out_ref[x - 2, y - 2] = second[x, y]


def body(image, u_factors, v_factors, ranks, measured):
    row_tiles, col_tiles, tile_len, rank_max = u_factors.shape
    nx, ny, depth, frames = image.shape
    brick = nx * ny * depth
    rows, cols = lax.axis_size("row"), lax.axis_size("col")
    chips, part_len = cols // 2, tile_len // cols
    at = jnp.stack([lax.axis_index("row"), lax.axis_index("col"), rows, cols]).astype(jnp.int32)

    have = {0: call(cast_kernel, "cast", (), (image,), [((frames, brick), BF16)])[0]}
    for bit in reversed(bits_of(rows)):
        for distance in list(have):
            have[distance ^ bit] = swap(have[distance], "row", bit)
    pieces = [have[distance] for distance in range(rows)]

    u_parts = u_factors.reshape(row_tiles, col_tiles, chips, 2, part_len, rank_max)
    half = (chips, row_tiles, part_len, frames)
    cross, coef = call(
        functools.partial(forward_kernel, rows),
        "forward",
        (at, ranks),
        (*pieces, u_parts, v_factors),
        [(half, BF16), ((row_tiles, col_tiles, frames, rank_max), BF16)],
        [pltpu.VMEM((rows, frames, brick), BF16)],
    )
    crossed = swap(cross, "col", 1)
    (mine,) = call(own_kernel, "own", (at,), (u_parts, coef), [(half, F32)])
    part = (row_tiles, part_len, frames)
    own, *sends = call(
        sum_kernel,
        "sum",
        (at,),
        (mine, crossed, measured.reshape(row_tiles, cols, part_len, frames)),
        [(part, F32)] + [(part, BF16)] * (chips - 1),
    )
    received = [swap(value, "col", 2 * q) for q, value in enumerate(sends, 1)]
    (resid,) = call(
        resid_kernel, "resid", (), (own, *received), [((row_tiles, frames, part_len), BF16)]
    )
    parts = {}
    for q in range(chips):
        parts[2 * q] = swap(resid, "col", 2 * q) if q else resid
        parts[2 * q + 1] = swap(parts[2 * q], "col", 1)

    back, *odds = call(
        functools.partial(adjoint_kernel, cols),
        "adjoint",
        (at, ranks),
        (*[parts[d] for d in range(cols)], u_factors, v_factors),
        [((row_tiles, col_tiles, frames, rank_max), BF16)] + [((brick, frames), BF16)] * (rows // 2),
        [pltpu.VMEM((cols, row_tiles, frames, part_len), BF16)],
    )
    crossing = [swap(value, "row", 1) for value in odds]
    evens = call(
        adjoint_rest_kernel, "rest", (at,), (v_factors, back), [((brick, frames), F32)] * (rows // 2)
    )
    sums = {2 * n: (evens[n], [crossing[n]]) for n in range(rows // 2)}
    for bit in bits_of(rows)[1:]:
        for d in [d for d in sums if d & bit]:
            base, extra = sums.pop(d)
            for value in extra:
                base = base + value.astype(F32)
            sums[d ^ bit][1].append(swap(base.astype(BF16), "row", bit))
    base, extra = sums[0]

    edge = (2, ny, depth, frames)
    moved, to_even, to_odd, side = call(
        functools.partial(move_kernel, len(extra)),
        "move",
        (at,),
        (image, base, *extra),
        [(image.shape, F32), (edge, BF16), (edge, BF16), (image.shape, BF16)],
    )
    row_even, row_odd = swap(to_even, "row", 1), swap_odd(to_odd, "row")
    col_odd, col_even = swap_odd(side, "col"), swap(side, "col", 1)
    corner = (2, depth, frames)
    to_even, to_odd = call(
        corner_kernel, "corner", (at,), (row_even, row_odd), [(corner, BF16)] * 2
    )
    corner_odd, corner_even = swap_odd(to_odd, "col"), swap(to_even, "col", 1)
    return call(
        diffuse_kernel,
        "diffuse",
        (at,),
        (moved, row_even, row_odd, col_even, col_odd, corner_even, corner_odd),
        [(image.shape, F32)],
        [pltpu.VMEM((nx + 4, ny + 4, depth, frames), F32)],
    )[0]


def solution(mesh):
    placed = (
        P("row", "col", None, None),
        P("row", "col", None, None),
        P("row", "col", None, None),
        P("row", "col"),
        P("row", None),
    )
    return jax.shard_map(
        body, mesh=mesh, in_specs=placed, out_specs=P("row", "col", None, None), check_vma=False
    )
```

time: 176 us -> 109 us (0.62)
  waiting for transfers between devices: 108 us -> 30.1 us
  Pallas kernels: 0 us -> 35.6 us
  starting transfers between devices: 12.7 us -> 34.8 us
  matrix products: 14.3 us -> 0 us
  between operations: 13.5 us -> 0.16 us
  blocking collectives: 12.8 us -> 0 us
  other arithmetic: 7.07 us -> 1.64 us
    psum x1 -> x0, waiting for transfers between devices: 68.7 us -> none  [body(): total = lax.psum(partial_value, 'col')]
    pallas_call x0 -> x10, Pallas kernels: none -> 35.6 us  [call(): pl.pallas_call(kernel, name=name, out_shape=[jax.ShapeDtypeStruct(shape,...]
    reduce_scatter x1 -> x0, waiting for transfers between devices: 26.1 us -> none  [body(): lax.psum_scatter(grad_terms, 'row', scatter_dimension=0, tiled=True)]
    ppermute x4 -> x23, starting transfers between devices: 12.6 us -> 34.8 us  [the longest x20 25.5 us: swap(): return lax.ppermute(value, axis, [(i, i ^ distance) for i in range(count)])]
    ppermute x4 -> x23, waiting for transfers between devices: 13.6 us -> 30.1 us  [the longest x20 23.3 us: swap(): return lax.ppermute(value, axis, [(i, i ^ distance) for i in range(count)])]
    dot_general x2 -> x0, matrix products: 14.3 us -> none  [the longest x1 7.72 us: body(): jnp.einsum('ijkr,ijrf->jkf', v_factors, back, preferred_element_type=jnp....]
    all_gather x1 -> x0, blocking collectives: 12.8 us -> none  [body(): lax.all_gather(image.astype(jnp.bfloat16), 'row', axis=0, tiled=True)]
    unnamed x5 -> x47, local copies, waits for them, and re-layouts: 0.77 us -> 6.4 us
  transfers between devices with their start and end apart: 6 -> 23, of which waited for: 6 -> 13; matrix products, arithmetic and copies ran while one was open for 0% -> 3% of each run, Pallas kernels for 0% -> 10%
where the time goes in v2:
time: 109 us
  Pallas kernels  35.6 us (33%)
  starting transfers between devices  34.8 us (32%)
  waiting for transfers between devices  30.1 us (28%)
  local copies, waits for them, and re-layouts  6.4 us (6%)
  other arithmetic  1.64 us (2%)
    pallas_call x10, Pallas kernels, call(): pl.pallas_call(kernel, name=name, out_shape=[jax.ShapeDtypeStruct(shape,...  35.6 us
    ppermute x20, starting transfers between devices, swap(): return lax.ppermute(value, axis, [(i, i ^ distance) for i in range(count)])  25.5 us
    ppermute x20, waiting for transfers between devices, swap(): return lax.ppermute(value, axis, [(i, i ^ distance) for i in range(count)])  23.3 us
    ppermute x3, starting transfers between devices, swap_odd(): return lax.ppermute(value, axis, pairs + [(b, a) for a, b in pairs])  9.26 us
    ppermute x3, waiting for transfers between devices, swap_odd(): return lax.ppermute(value, axis, pairs + [(b, a) for a, b in pairs])  6.76 us
    unnamed x47, local copies, waits for them, and re-layouts  6.4 us
  transfers between devices with their start and end apart: 23, of which 13 were waited for; matrix products, arithmetic and copies ran while one was open for 3% of the time, Pallas kernels for 10%

profile of v2, /device:TPU:19, one launch (start us, length us, event | category | flops | bytes accessed | tf_op | source)
XLA Modules:
  0.0 108.7 jit_solution(7682097036553262739)
XLA Ops:
  0.0 1.7 %cast.1.refs_0_ = bf16[128,512]{1,0:T(8,128)(2,1)} custom-call(f32[4,2,64,128]{3,2,1,0:T(8,128)} %image_ref.3), custom_call_target="tpu_custom_call" | custom-call | tf_op jit(solution)/shard_map/cast/pallas_call | solution.py:41
  3.1 4.1 %collective-permute-done.1.refs_2_ = bf16[128,512]{1,0:T(8,128)(2,1)S(1)} collective-permute-done((bf16[128,512]{1,0:T(8,128)(2,1)}, bf16[128,512]{1,0:T(8,128)(2,1)S(1)}, u32[]{:S(2)}, u32[]{:S(2)}) %collective-permute-start.1) | collective-permute-done | bytes 131104 | tf_op jit(solution)/shard_map/ppermute | solution.py:17
  7.2 5.0 %collective-permute-start.2 = (bf16[128,512]{1,0:T(8,128)(2,1)S(1)}, bf16[128,512]{1,0:T(8,128)(2,1)S(1)}, u32[]{:S(2)}, u32[]{:S(2)}) collective-permute-start(bf16[128,512]{1,0:T(8,128)(2,1)S(1)} %collective-permute-done.1.refs_2_), channel_id=1, source_target_pairs={{0,8},{8,0},{16,24},{24,16},{1,9},{9,1},{17,25},{25,17},{2,10},{10... | collective-permute-start | bytes 393224 | tf_op jit(solution)/shard_map/ppermute | solution.py:17
  16.3 6.7 %forward.1 = (bf16[4,5,128,128]{3,2,1,0:T(8,128)(2,1)}, bf16[5,2,128,256]{3,2,1,0:T(8,128)(2,1)}) custom-call(s32[4]{0:T(128)} %pad_add_fusion.at_ref, s32[5,2]{1,0:T(8,128)} %copy.7.ranks_ref, bf16[128,512]{1,0:T(8,128)(2,1)} %cast.1.refs_0_, bf16[128,512]{1,0:T(8,128)(2,1)} %copy-done.14, bf16[128,512]{1,0:T(8,128)(2,1)} %copy-done.13, ...), custom_call_target="tpu_custom_call" | custom-call | tf_op jit(solution)/shard_map/forward/pallas_call | solution.py:41
  24.1 4.6 %own.1.mine_ref = f32[4,5,128,128]{3,2,1,0:T(8,128)} custom-call(s32[4]{0:T(128)} %pad_add_fusion.at_ref, bf16[5,2,4,2,128,256]{5,4,3,2,1,0:T(8,128)(2,1)} %bitcast.5, bf16[5,2,128,256]{3,2,1,0:T(8,128)(2,1)} %get-tuple-element.22.coef_ref), custom_call_target="tpu_custom_call" | custom-call | tf_op jit(solution)/shard_map/own/pallas_call | solution.py:41
  29.5 2.8 %sum.1 = (f32[5,128,128]{2,1,0:T(8,128)}, bf16[5,128,128]{2,1,0:T(8,128)(2,1)}, bf16[5,128,128]{2,1,0:T(8,128)(2,1)}, bf16[5,128,128]{2,1,0:T(8,128)(2,1)}) custom-call(s32[4]{0:T(128)} %pad_add_fusion.at_ref, f32[4,5,128,128]{3,2,1,0:T(8,128)} %own.1.mine_ref, bf16[4,5,128,128]{3,2,1,0:T(8,128)(2,1)} %copy-done, bf16[5,8,128,128]{3,2,1,0:T(8,128)(2,1)} %bitcast.6), custom_call_target="tpu_custom_call" | custom-call | tf_op jit(solution)/shard_map/sum/pallas_call | solution.py:41
  35.0 3.3 %collective-permute-done.4.refs_0_ = bf16[5,128,128]{2,1,0:T(8,128)(2,1)S(1)} collective-permute-done((bf16[5,128,128]{2,1,0:T(8,128)(2,1)}, bf16[5,128,128]{2,1,0:T(8,128)(2,1)S(1)}, u32[]{:S(2)}, u32[]{:S(2)}) %collective-permute-start.4) | collective-permute-done | bytes 163872 | tf_op jit(solution)/shard_map/ppermute | solution.py:17
  38.3 4.5 %collective-permute-done.6.refs_2_ = bf16[5,128,128]{2,1,0:T(8,128)(2,1)S(1)} collective-permute-done((bf16[5,128,128]{2,1,0:T(8,128)(2,1)}, bf16[5,128,128]{2,1,0:T(8,128)(2,1)S(1)}, u32[]{:S(2)}, u32[]{:S(2)}) %collective-permute-start.6) | collective-permute-done | bytes 163872 | tf_op jit(solution)/shard_map/ppermute | solution.py:17
  43.4 2.0 %resid.1.refs_0_ = bf16[5,128,128]{2,1,0:T(8,128)(2,1)} custom-call(f32[5,128,128]{2,1,0:T(8,128)} %get-tuple-element.24.own_ref, bf16[5,128,128]{2,1,0:T(8,128)(2,1)} %copy-done.3, bf16[5,128,128]{2,1,0:T(8,128)(2,1)} %copy-done.4, bf16[5,128,128]{2,1,0:T(8,128)(2,1)} %copy-done.5), custom_call_target="tpu_custom_call" | custom-call | tf_op jit(solution)/shard_map/resid/pallas_call | solution.py:41
  48.1 1.7 %collective-permute-start.7 = (bf16[5,128,128]{2,1,0:T(8,128)(2,1)}, bf16[5,128,128]{2,1,0:T(8,128)(2,1)S(1)}, u32[]{:S(2)}, u32[]{:S(2)}) collective-permute-start(bf16[5,128,128]{2,1,0:T(8,128)(2,1)} %resid.1.refs_0_), channel_id=1, source_target_pairs={{0,1},{1,0},{2,3},{3,2},{4,5},{5,4},{6,7},{7,6},{8,9},{9,8},{10,11... | collective-permute-start | bytes 491528 | tf_op jit(solution)/shard_map/ppermute | solution.py:17
  51.5 3.0 %collective-permute-start.13 = (bf16[5,128,128]{2,1,0:T(8,128)(2,1)S(1)}, bf16[5,128,128]{2,1,0:T(8,128)(2,1)S(1)}, u32[]{:S(2)}, u32[]{:S(2)}) collective-permute-start(bf16[5,128,128]{2,1,0:T(8,128)(2,1)S(1)} %collective-permute-done.12.refs_6_), channel_id=1, source_target_pairs={{0,1},{1,0},{2,3},{3,2},{4,5},{5,4},{6,7},{7,6},{8,9},{9,8},{10,11... | collective-permute-start | bytes 491528 | tf_op jit(solution)/shard_map/ppermute | solution.py:17
  59.0 7.0 %adjoint.1 = (bf16[5,2,128,256]{3,2,1,0:T(8,128)(2,1)}, bf16[512,128]{1,0:T(8,128)(2,1)}, bf16[512,128]{1,0:T(8,128)(2,1)}) custom-call(s32[4]{0:T(128)} %pad_add_fusion.at_ref, s32[5,2]{1,0:T(8,128)} %copy.7.ranks_ref, bf16[5,128,128]{2,1,0:T(8,128)(2,1)} %resid.1.refs_0_, bf16[5,128,128]{2,1,0:T(8,128)(2,1)} %copy-done.9, bf16[5,128,128]{2,1,0:T(8,128)(2,1)} %copy-done.8, ...), custom_call_target="tpu_custom_call" | custom-call | tf_op jit(solution)/shard_map/adjoint/pallas_call | solution.py:41
  67.5 4.3 %rest.1 = (f32[512,128]{1,0:T(8,128)}, f32[512,128]{1,0:T(8,128)}) custom-call(s32[4]{0:T(128)} %pad_add_fusion.at_ref, bf16[5,2,1024,256]{3,2,1,0:T(8,128)(2,1)} %v_ref.1, bf16[5,2,128,256]{3,2,1,0:T(8,128)(2,1)} %get-tuple-element.28.back_ref), custom_call_target="tpu_custom_call" | custom-call | tf_op jit(solution)/shard_map/rest/pallas_call | solution.py:41
  72.9 3.3 %collective-permute-done.14.refs_0_ = bf16[512,128]{1,0:T(8,128)(2,1)S(1)} collective-permute-done((bf16[512,128]{1,0:T(8,128)(2,1)S(1)}, bf16[512,128]{1,0:T(8,128)(2,1)S(1)}, u32[]{:S(2)}, u32[]{:S(2)}) %collective-permute-start.14) | collective-permute-done | bytes 131104 | tf_op jit(solution)/shard_map/ppermute | solution.py:17
  76.2 1.8 %collective-permute-done.16.refs_1_ = bf16[512,128]{1,0:T(8,128)(2,1)S(1)} collective-permute-done((bf16[512,128]{1,0:T(8,128)(2,1)S(1)}, bf16[512,128]{1,0:T(8,128)(2,1)S(1)}, u32[]{:S(2)}, u32[]{:S(2)}) %collective-permute-start.16) | collective-permute-done | bytes 131104 | tf_op jit(solution)/shard_map/ppermute | solution.py:17
  78.6 2.0 %move.1 = (f32[4,2,64,128]{3,2,1,0:T(8,128)}, bf16[2,2,64,128]{3,2,1,0:T(8,128)(2,1)}, bf16[2,2,64,128]{3,2,1,0:T(8,128)(2,1)}, bf16[4,2,64,128]{3,2,1,0:T(8,128)(2,1)}) custom-call(s32[4]{0:T(128)} %pad_add_fusion.at_ref, f32[4,2,64,128]{3,2,1,0:T(8,128)} %image_ref.3, f32[512,128]{1,0:T(8,128)} %get-tuple-element.29.part_ref, bf16[512,128]{1,0:T(8,128)(2,1)} %copy-done.18, ...), custom_call_target="tpu_custom_call" | custom-call | tf_op jit(solution)/shard_map/move/pallas_call | solution.py:41
  80.6 4.9 %collective-permute-start.20 = (bf16[4,2,64,128]{3,2,1,0:T(8,128)(2,1)}, bf16[4,2,64,128]{3,2,1,0:T(8,128)(2,1)S(1)}, u32[]{:S(2)}, u32[]{:S(2)}) collective-permute-start(bf16[4,2,64,128]{3,2,1,0:T(8,128)(2,1)} %get-tuple-element.36), channel_id=1, source_target_pairs={{1,2},{3,4},{5,6},{2,1},{4,3},{6,5},{9,10},{11,12},{13,14},{10,9},... | collective-permute-start | bytes 393224 | tf_op jit(solution)/shard_map/ppermute | solution.py:23
  85.5 4.0 %collective-permute-start.17 = (bf16[2,2,64,128]{3,2,1,0:T(8,128)(2,1)}, bf16[2,2,64,128]{3,2,1,0:T(8,128)(2,1)S(1)}, u32[]{:S(2)}, u32[]{:S(2)}) collective-permute-start(bf16[2,2,64,128]{3,2,1,0:T(8,128)(2,1)} %get-tuple-element.34), channel_id=1, source_target_pairs={{0,8},{8,0},{16,24},{24,16},{1,9},{9,1},{17,25},{25,17},{2,10},{10... | collective-permute-start | bytes 196616 | tf_op jit(solution)/shard_map/ppermute | solution.py:17
  89.5 1.9 %collective-permute-start.18 = (bf16[2,2,64,128]{3,2,1,0:T(8,128)(2,1)}, bf16[2,2,64,128]{3,2,1,0:T(8,128)(2,1)S(1)}, u32[]{:S(2)}, u32[]{:S(2)}) collective-permute-start(bf16[2,2,64,128]{3,2,1,0:T(8,128)(2,1)} %get-tuple-element.35), channel_id=1, source_target_pairs={{8,16},{16,8},{9,17},{17,9},{10,18},{18,10},{11,19},{19,11},{12,20... | collective-permute-start | bytes 196616 | tf_op jit(solution)/shard_map/ppermute | solution.py:23
  91.7 3.0 %collective-permute-done.18.odd_ref.row_odd = bf16[2,2,64,128]{3,2,1,0:T(8,128)(2,1)S(1)} collective-permute-done((bf16[2,2,64,128]{3,2,1,0:T(8,128)(2,1)}, bf16[2,2,64,128]{3,2,1,0:T(8,128)(2,1)S(1)}, u32[]{:S(2)}, u32[]{:S(2)}) %collective-permute-start.18) | collective-permute-done | bytes 65568 | tf_op jit(solution)/shard_map/ppermute | solution.py:23
  96.8 1.9 %collective-permute-start.21 = (bf16[2,64,128]{2,1,0:T(8,128)(2,1)}, bf16[2,64,128]{2,1,0:T(8,128)(2,1)S(1)}, u32[]{:S(2)}, u32[]{:S(2)}) collective-permute-start(bf16[2,64,128]{2,1,0:T(8,128)(2,1)} %get-tuple-element.37), channel_id=1, source_target_pairs={{0,1},{1,0},{2,3},{3,2},{4,5},{5,4},{6,7},{7,6},{8,9},{9,8},{10,11... | collective-permute-start | bytes 98312 | tf_op jit(solution)/shard_map/ppermute | solution.py:17
  98.7 2.5 %collective-permute-start.22 = (bf16[2,64,128]{2,1,0:T(8,128)(2,1)}, bf16[2,64,128]{2,1,0:T(8,128)(2,1)S(1)}, u32[]{:S(2)}, u32[]{:S(2)}) collective-permute-start(bf16[2,64,128]{2,1,0:T(8,128)(2,1)} %get-tuple-element.38), channel_id=1, source_target_pairs={{1,2},{3,4},{5,6},{2,1},{4,3},{6,5},{9,10},{11,12},{13,14},{10,9},... | collective-permute-start | bytes 98312 | tf_op jit(solution)/shard_map/ppermute | solution.py:23
  101.2 3.8 %collective-permute-done.22.corner_odd = bf16[2,64,128]{2,1,0:T(8,128)(2,1)S(1)} collective-permute-done((bf16[2,64,128]{2,1,0:T(8,128)(2,1)}, bf16[2,64,128]{2,1,0:T(8,128)(2,1)S(1)}, u32[]{:S(2)}, u32[]{:S(2)}) %collective-permute-start.22) | collective-permute-done | bytes 32800 | tf_op jit(solution)/shard_map/ppermute | solution.py:23
  105.7 3.0 %diffuse.1 = f32[4,2,64,128]{3,2,1,0:T(8,128)} custom-call(s32[4]{0:T(128)} %pad_add_fusion.at_ref, f32[4,2,64,128]{3,2,1,0:T(8,128)} %get-tuple-element.33.moved_ref, bf16[2,2,64,128]{3,2,1,0:T(8,128)(2,1)} %copy-done.1, bf16[2,2,64,128]{3,2,1,0:T(8,128)(2,1)} %copy-done.2, bf16[4,2,64,128]{3,2,1,0:T(8,128)(2,1)} %copy-done.17, ...), custom_call_target="tpu_custom_call" | custom-call | tf_op jit(solution)/shard_map/diffuse/pallas_call | solution.py:41
  (81 shorter events, 25.9 us)
Async XLA Ops:
  1.7 5.5 %collective-permute-start.1 = (bf16[128,512]{1,0:T(8,128)(2,1)}, bf16[128,512]{1,0:T(8,128)(2,1)S(1)}, u32[]{:S(2)}, u32[]{:S(2)}) collective-permute-start(bf16[128,512]{1,0:T(8,128)(2,1)} %cast.1.refs_0_), channel_id=1, source_target_pairs={{0,16},{8,24},{16,0},{24,8},{1,17},{9,25},{17,1},{25,9},{2,18},{10... | collective-permute-start | bytes 393224 | tf_op jit(solution)/shard_map/ppermute | solution.py:17
  1.8 12.5 %collective-permute-start = (bf16[128,512]{1,0:T(8,128)(2,1)}, bf16[128,512]{1,0:T(8,128)(2,1)S(1)}, u32[]{:S(2)}, u32[]{:S(2)}) collective-permute-start(bf16[128,512]{1,0:T(8,128)(2,1)} %cast.1.refs_0_), channel_id=1, source_target_pairs={{0,8},{8,0},{16,24},{24,16},{1,9},{9,1},{17,25},{25,17},{2,10},{10... | collective-permute-start | bytes 393224 | tf_op jit(solution)/shard_map/ppermute | solution.py:17
  7.2 8.4 %copy-start.13 = (bf16[128,512]{1,0:T(8,128)(2,1)}, bf16[128,512]{1,0:T(8,128)(2,1)S(1)}, u32[]{:S(2)}) copy-start(bf16[128,512]{1,0:T(8,128)(2,1)S(1)} %collective-permute-done.1.refs_2_) | copy-start | bytes 393220
  7.2 8.4 %collective-permute-start.2 = (bf16[128,512]{1,0:T(8,128)(2,1)S(1)}, bf16[128,512]{1,0:T(8,128)(2,1)S(1)}, u32[]{:S(2)}, u32[]{:S(2)}) collective-permute-start(bf16[128,512]{1,0:T(8,128)(2,1)S(1)} %collective-permute-done.1.refs_2_), channel_id=1, source_target_pairs={{0,8},{8,0},{16,24},{24,16},{1,9},{9,1},{17,25},{25,17},{2,10},{10... | collective-permute-start | bytes 393224 | tf_op jit(solution)/shard_map/ppermute | solution.py:17
  23.0 5.7 %collective-permute-start.3 = (bf16[4,5,128,128]{3,2,1,0:T(8,128)(2,1)}, bf16[4,5,128,128]{3,2,1,0:T(8,128)(2,1)S(1)}, u32[]{:S(2)}, u32[]{:S(2)}) collective-permute-start(bf16[4,5,128,128]{3,2,1,0:T(8,128)(2,1)} %get-tuple-element.23), channel_id=1, source_target_pairs={{0,1},{1,0},{2,3},{3,2},{4,5},{5,4},{6,7},{7,6},{8,9},{9,8},{10,11... | collective-permute-start | bytes 1966088 | tf_op jit(solution)/shard_map/ppermute | solution.py:17
  32.4 6.0 %collective-permute-start.4 = (bf16[5,128,128]{2,1,0:T(8,128)(2,1)}, bf16[5,128,128]{2,1,0:T(8,128)(2,1)S(1)}, u32[]{:S(2)}, u32[]{:S(2)}) collective-permute-start(bf16[5,128,128]{2,1,0:T(8,128)(2,1)} %get-tuple-element.25), channel_id=1, source_target_pairs={{0,2},{1,3},{2,0},{3,1},{4,6},{5,7},{6,4},{7,5},{8,10},{9,11},{10,... | collective-permute-start | bytes 491528 | tf_op jit(solution)/shard_map/ppermute | solution.py:17
  32.6 5.7 %collective-permute-start.5 = (bf16[5,128,128]{2,1,0:T(8,128)(2,1)}, bf16[5,128,128]{2,1,0:T(8,128)(2,1)S(1)}, u32[]{:S(2)}, u32[]{:S(2)}) collective-permute-start(bf16[5,128,128]{2,1,0:T(8,128)(2,1)} %get-tuple-element.26), channel_id=1, source_target_pairs={{0,4},{1,5},{2,6},{3,7},{4,0},{5,1},{6,2},{7,3},{8,12},{9,13},{10,... | collective-permute-start | bytes 491528 | tf_op jit(solution)/shard_map/ppermute | solution.py:17
  33.9 8.9 %collective-permute-start.6 = (bf16[5,128,128]{2,1,0:T(8,128)(2,1)}, bf16[5,128,128]{2,1,0:T(8,128)(2,1)S(1)}, u32[]{:S(2)}, u32[]{:S(2)}) collective-permute-start(bf16[5,128,128]{2,1,0:T(8,128)(2,1)} %get-tuple-element.27), channel_id=1, source_target_pairs={{0,6},{1,7},{2,4},{3,5},{4,2},{5,3},{6,0},{7,1},{8,14},{9,15},{10,... | collective-permute-start | bytes 491528 | tf_op jit(solution)/shard_map/ppermute | solution.py:17
  45.4 6.0 %collective-permute-start.12 = (bf16[5,128,128]{2,1,0:T(8,128)(2,1)}, bf16[5,128,128]{2,1,0:T(8,128)(2,1)S(1)}, u32[]{:S(2)}, u32[]{:S(2)}) collective-permute-start(bf16[5,128,128]{2,1,0:T(8,128)(2,1)} %resid.1.refs_0_), channel_id=1, source_target_pairs={{0,6},{1,7},{2,4},{3,5},{4,2},{5,3},{6,0},{7,1},{8,14},{9,15},{10,... | collective-permute-start | bytes 491528 | tf_op jit(solution)/shard_map/ppermute | solution.py:17
  46.7 9.5 %collective-permute-start.10 = (bf16[5,128,128]{2,1,0:T(8,128)(2,1)}, bf16[5,128,128]{2,1,0:T(8,128)(2,1)S(1)}, u32[]{:S(2)}, u32[]{:S(2)}) collective-permute-start(bf16[5,128,128]{2,1,0:T(8,128)(2,1)} %resid.1.refs_0_), channel_id=1, source_target_pairs={{0,4},{1,5},{2,6},{3,7},{4,0},{5,1},{6,2},{7,3},{8,12},{9,13},{10,... | collective-permute-start | bytes 491528 | tf_op jit(solution)/shard_map/ppermute | solution.py:17
  46.9 9.8 %collective-permute-start.8 = (bf16[5,128,128]{2,1,0:T(8,128)(2,1)}, bf16[5,128,128]{2,1,0:T(8,128)(2,1)S(1)}, u32[]{:S(2)}, u32[]{:S(2)}) collective-permute-start(bf16[5,128,128]{2,1,0:T(8,128)(2,1)} %resid.1.refs_0_), channel_id=1, source_target_pairs={{0,2},{1,3},{2,0},{3,1},{4,6},{5,7},{6,4},{7,5},{8,10},{9,11},{10,... | collective-permute-start | bytes 491528 | tf_op jit(solution)/shard_map/ppermute | solution.py:17
  48.1 8.7 %collective-permute-start.7 = (bf16[5,128,128]{2,1,0:T(8,128)(2,1)}, bf16[5,128,128]{2,1,0:T(8,128)(2,1)S(1)}, u32[]{:S(2)}, u32[]{:S(2)}) collective-permute-start(bf16[5,128,128]{2,1,0:T(8,128)(2,1)} %resid.1.refs_0_), channel_id=1, source_target_pairs={{0,1},{1,0},{2,3},{3,2},{4,5},{5,4},{6,7},{7,6},{8,9},{9,8},{10,11... | collective-permute-start | bytes 491528 | tf_op jit(solution)/shard_map/ppermute | solution.py:17
  51.5 5.3 %collective-permute-start.13 = (bf16[5,128,128]{2,1,0:T(8,128)(2,1)S(1)}, bf16[5,128,128]{2,1,0:T(8,128)(2,1)S(1)}, u32[]{:S(2)}, u32[]{:S(2)}) collective-permute-start(bf16[5,128,128]{2,1,0:T(8,128)(2,1)S(1)} %collective-permute-done.12.refs_6_), channel_id=1, source_target_pairs={{0,1},{1,0},{2,3},{3,2},{4,5},{5,4},{6,7},{7,6},{8,9},{9,8},{10,11... | collective-permute-start | bytes 491528 | tf_op jit(solution)/shard_map/ppermute | solution.py:17
  56.2 1.5 %collective-permute-start.11 = (bf16[5,128,128]{2,1,0:T(8,128)(2,1)S(1)}, bf16[5,128,128]{2,1,0:T(8,128)(2,1)S(1)}, u32[]{:S(2)}, u32[]{:S(2)}) collective-permute-start(bf16[5,128,128]{2,1,0:T(8,128)(2,1)S(1)} %collective-permute-done.10.refs_4_), channel_id=1, source_target_pairs={{0,1},{1,0},{2,3},{3,2},{4,5},{5,4},{6,7},{7,6},{8,9},{9,8},{10,11... | collective-permute-start | bytes 491528 | tf_op jit(solution)/shard_map/ppermute | solution.py:17
  56.7 1.4 %collective-permute-start.9 = (bf16[5,128,128]{2,1,0:T(8,128)(2,1)S(1)}, bf16[5,128,128]{2,1,0:T(8,128)(2,1)S(1)}, u32[]{:S(2)}, u32[]{:S(2)}) collective-permute-start(bf16[5,128,128]{2,1,0:T(8,128)(2,1)S(1)} %collective-permute-done.8.refs_2_), channel_id=1, source_target_pairs={{0,1},{1,0},{2,3},{3,2},{4,5},{5,4},{6,7},{7,6},{8,9},{9,8},{10,11... | collective-permute-start | bytes 491528 | tf_op jit(solution)/shard_map/ppermute | solution.py:17
  66.0 5.8 %collective-permute-start.15 = (bf16[512,128]{1,0:T(8,128)(2,1)}, bf16[512,128]{1,0:T(8,128)(2,1)S(1)}, u32[]{:S(2)}, u32[]{:S(2)}) collective-permute-start(bf16[512,128]{1,0:T(8,128)(2,1)} %get-tuple-element.32), channel_id=1, source_target_pairs={{0,8},{8,0},{16,24},{24,16},{1,9},{9,1},{17,25},{25,17},{2,10},{10... | collective-permute-start | bytes 393224 | tf_op jit(solution)/shard_map/ppermute | solution.py:17
  71.8 4.4 %collective-permute-start.14 = (bf16[512,128]{1,0:T(8,128)(2,1)S(1)}, bf16[512,128]{1,0:T(8,128)(2,1)S(1)}, u32[]{:S(2)}, u32[]{:S(2)}) collective-permute-start(bf16[512,128]{1,0:T(8,128)(2,1)S(1)} %copy-done.22), channel_id=1, source_target_pairs={{0,8},{8,0},{16,24},{24,16},{1,9},{9,1},{17,25},{25,17},{2,10},{10... | collective-permute-start | bytes 393224 | tf_op jit(solution)/shard_map/ppermute | solution.py:17
  72.8 5.1 %collective-permute-start.16 = (bf16[512,128]{1,0:T(8,128)(2,1)S(1)}, bf16[512,128]{1,0:T(8,128)(2,1)S(1)}, u32[]{:S(2)}, u32[]{:S(2)}) collective-permute-start(bf16[512,128]{1,0:T(8,128)(2,1)S(1)} %add_convert_fusion), channel_id=1, source_target_pairs={{0,16},{8,24},{16,0},{24,8},{1,17},{9,25},{17,1},{25,9},{2,18},{10... | collective-permute-start | bytes 393224 | tf_op jit(solution)/shard_map/ppermute | solution.py:17
  80.6 24.4 %collective-permute-start.20 = (bf16[4,2,64,128]{3,2,1,0:T(8,128)(2,1)}, bf16[4,2,64,128]{3,2,1,0:T(8,128)(2,1)S(1)}, u32[]{:S(2)}, u32[]{:S(2)}) collective-permute-start(bf16[4,2,64,128]{3,2,1,0:T(8,128)(2,1)} %get-tuple-element.36), channel_id=1, source_target_pairs={{1,2},{3,4},{5,6},{2,1},{4,3},{6,5},{9,10},{11,12},{13,14},{10,9},... | collective-permute-start | bytes 393224 | tf_op jit(solution)/shard_map/ppermute | solution.py:23
  85.5 19.6 %collective-permute-start.19 = (bf16[4,2,64,128]{3,2,1,0:T(8,128)(2,1)}, bf16[4,2,64,128]{3,2,1,0:T(8,128)(2,1)S(1)}, u32[]{:S(2)}, u32[]{:S(2)}) collective-permute-start(bf16[4,2,64,128]{3,2,1,0:T(8,128)(2,1)} %get-tuple-element.36), channel_id=1, source_target_pairs={{0,1},{1,0},{2,3},{3,2},{4,5},{5,4},{6,7},{7,6},{8,9},{9,8},{10,11... | collective-permute-start | bytes 393224 | tf_op jit(solution)/shard_map/ppermute | solution.py:17
  85.5 6.2 %collective-permute-start.17 = (bf16[2,2,64,128]{3,2,1,0:T(8,128)(2,1)}, bf16[2,2,64,128]{3,2,1,0:T(8,128)(2,1)S(1)}, u32[]{:S(2)}, u32[]{:S(2)}) collective-permute-start(bf16[2,2,64,128]{3,2,1,0:T(8,128)(2,1)} %get-tuple-element.34), channel_id=1, source_target_pairs={{0,8},{8,0},{16,24},{24,16},{1,9},{9,1},{17,25},{25,17},{2,10},{10... | collective-permute-start | bytes 196616 | tf_op jit(solution)/shard_map/ppermute | solution.py:17
  89.5 5.2 %collective-permute-start.18 = (bf16[2,2,64,128]{3,2,1,0:T(8,128)(2,1)}, bf16[2,2,64,128]{3,2,1,0:T(8,128)(2,1)S(1)}, u32[]{:S(2)}, u32[]{:S(2)}) collective-permute-start(bf16[2,2,64,128]{3,2,1,0:T(8,128)(2,1)} %get-tuple-element.35), channel_id=1, source_target_pairs={{8,16},{16,8},{9,17},{17,9},{10,18},{18,10},{11,19},{19,11},{12,20... | collective-permute-start | bytes 196616 | tf_op jit(solution)/shard_map/ppermute | solution.py:23
  96.8 4.4 %collective-permute-start.21 = (bf16[2,64,128]{2,1,0:T(8,128)(2,1)}, bf16[2,64,128]{2,1,0:T(8,128)(2,1)S(1)}, u32[]{:S(2)}, u32[]{:S(2)}) collective-permute-start(bf16[2,64,128]{2,1,0:T(8,128)(2,1)} %get-tuple-element.37), channel_id=1, source_target_pairs={{0,1},{1,0},{2,3},{3,2},{4,5},{5,4},{6,7},{7,6},{8,9},{9,8},{10,11... | collective-permute-start | bytes 98312 | tf_op jit(solution)/shard_map/ppermute | solution.py:17
  98.7 6.3 %collective-permute-start.22 = (bf16[2,64,128]{2,1,0:T(8,128)(2,1)}, bf16[2,64,128]{2,1,0:T(8,128)(2,1)S(1)}, u32[]{:S(2)}, u32[]{:S(2)}) collective-permute-start(bf16[2,64,128]{2,1,0:T(8,128)(2,1)} %get-tuple-element.38), channel_id=1, source_target_pairs={{1,2},{3,4},{5,6},{2,1},{4,3},{6,5},{9,10},{11,12},{13,14},{10,9},... | collective-permute-start | bytes 98312 | tf_op jit(solution)/shard_map/ppermute | solution.py:23
  (22 other events, 43.9 us)

commit v3 on v2

v3 whole, which is shorter than its diff:
```python
import functools

import jax
import jax.numpy as jnp
from jax import lax
from jax.experimental import pallas as pl
from jax.experimental.pallas import tpu as pltpu
from jax.sharding import PartitionSpec as P


diff_rate = 0.12
edge_scale = 0.5
BF16, F32 = jnp.bfloat16, jnp.float32


def swap(value, axis, distance):
    count = lax.axis_size(axis)
    return lax.ppermute(value, axis, [(i, i ^ distance) for i in range(count)])


def swap_odd(value, axis):
    count = lax.axis_size(axis)
    pairs = [(i, i + 1) for i in range(1, count - 1, 2)]
    return lax.ppermute(value, axis, pairs + [(b, a) for a, b in pairs])


def bits_of(count):
    bit, found = 1, []
    while bit < count:
        found.append(bit)
        bit *= 2
    return found


def dot_nt(a, b):
    return lax.dot_general(a, b, (((1,), (1,)), ((), ())), preferred_element_type=F32)


def call(kernel, arrays, outs, scratch=(), kept=pltpu.VMEM, through=0):
    arrays = [pltpu.with_memory_space_constraint(value, pltpu.VMEM) for value in arrays]
    vmem = pl.BlockSpec(memory_space=pltpu.VMEM)
    count, made = len(arrays), len(outs)
    outs = [*outs, *[(value.shape, value.dtype) for value in arrays[count - through :]]]

    def run(*refs):
        kernel(*refs[: count + made], *refs[count + made + through :])

    return pl.pallas_call(
        run,
        out_shape=[kept(shape, kind) for shape, kind in outs],
        in_specs=[vmem] * count,
        out_specs=[vmem] * len(outs),
        input_output_aliases={count - through + n: made + n for n in range(through)},
        scratch_shapes=list(scratch),
        compiler_params=pltpu.CompilerParams(vmem_limit_bytes=2**23),
    )(*arrays)


def load_kernel(factor_ref, samples_ref, *refs):
    out_ref, wanted_ref, sems = refs[-3:]
    copies = [(factor_ref.at[i], out_ref.at[i]) for i in range(factor_ref.shape[0])]
    copies.append((samples_ref.at[:, lax.axis_index("col")], wanted_ref))
    copies = [pltpu.make_async_copy(a, b, sems.at[n]) for n, (a, b) in enumerate(copies)]
    for copy in copies:
        copy.start()
    for copy in copies:
        copy.wait()


def load(factors, samples, after):
    vmem, hbm = (pl.BlockSpec(memory_space=space) for space in (pltpu.VMEM, pltpu.HBM))
    parts = (samples.shape[0], *samples.shape[2:])
    return pl.pallas_call(
        load_kernel,
        out_shape=[pltpu.VMEM(factors.shape, factors.dtype), pltpu.VMEM(parts, samples.dtype)],
        in_specs=[hbm, hbm] + [vmem] * len(after),
        out_specs=[vmem, vmem],
        scratch_shapes=[pltpu.SemaphoreType.DMA((factors.shape[0] + 1,))],
        compiler_params=pltpu.CompilerParams(vmem_limit_bytes=2**23),
    )(
        *[pltpu.with_memory_space_constraint(value, pltpu.HBM) for value in (factors, samples)],
        *[pltpu.with_memory_space_constraint(value, pltpu.VMEM) for value in after],
    )


def cast_kernel(image_ref, out_ref):
    flat = image_ref[...].reshape(out_ref.shape[1], out_ref.shape[0])
    out_ref[...] = flat.T.astype(BF16)


def near_kernel(mask_ref, *refs):
    pieces, (v_ref, near_ref, held) = refs[:-3], refs[-3:]
    count, col_tiles = len(pieces), v_ref.shape[1]
    me_row = lax.axis_index("row")
    tile = me_row // count
    for distance in range(count):
        held[(me_row % count) ^ distance] = pieces[distance][...]
    lhs = jnp.concatenate([held[p] for p in range(count)], axis=1)
    for i in range(v_ref.shape[0]):
        value = jnp.dot(lhs, v_ref[i, tile], preferred_element_type=F32)
        near_ref[i] = (value * mask_ref[pl.ds(i * col_tiles + tile, 1)]).astype(BF16)


def half_rows(u_ref, coef_ref, i, core):
    total = None
    for j in range(u_ref.shape[1]):
        rows = u_ref[i, j, :, core]
        rows = rows.reshape(rows.shape[0] * rows.shape[1], rows.shape[2])
        term = dot_nt(rows, coef_ref[i, j])
        total = term if total is None else total + term
    return total.reshape(u_ref.shape[2], u_ref.shape[4], total.shape[1])


def forward_kernel(mask_ref, near_ref, *refs):
    pieces, (u_ref, v_ref, cross_ref, coef_ref, held) = refs[:-5], refs[-5:]
    row_tiles, col_tiles, chips = u_ref.shape[:3]
    per_tile = len(pieces) // (col_tiles - 1)
    me_row, me_col = lax.axis_index("row"), lax.axis_index("col")
    own_tile = me_row // per_tile
    for n, piece in enumerate(pieces, per_tile):
        held[me_row ^ n] = piece[...]
    for i in range(row_tiles):
        coef_ref[i, own_tile] = near_ref[i]
    for n in range(1, col_tiles):
        tile = own_tile ^ n
        lhs = jnp.concatenate([held[tile * per_tile + p] for p in range(per_tile)], axis=1)
        for i in range(row_tiles):
            value = jnp.dot(lhs, v_ref[i, tile], preferred_element_type=F32)
            coef_ref[i, tile] = (value * mask_ref[pl.ds(i * col_tiles + tile, 1)]).astype(BF16)
    chip, core = me_col // 2, me_col % 2
    for i in range(row_tiles):
        value = half_rows(u_ref, coef_ref, i, 1 - core)
        for q in range(chips):
            cross_ref[chip ^ q, i] = value[q].astype(cross_ref.dtype)


def own_kernel(coef_ref, u_ref, mine_ref):
    me_col = lax.axis_index("col")
    chip, core = me_col // 2, me_col % 2
    for i in range(u_ref.shape[0]):
        value = half_rows(u_ref, coef_ref, i, core)
        for q in range(u_ref.shape[2]):
            mine_ref[chip ^ q, i] = value[q]


def sum_kernel(mine_ref, crossed_ref, wanted_ref, own_ref, *send_refs):
    value = mine_ref[0] + crossed_ref[0].astype(F32)
    own_ref[...] = value - wanted_ref[...].astype(F32)
    for q, send_ref in enumerate(send_refs, 1):
        send_ref[...] = (mine_ref[q] + crossed_ref[q].astype(F32)).astype(BF16)


def resid_kernel(own_ref, *refs):
    out_ref = refs[-1]
    for i in range(own_ref.shape[0]):
        value = own_ref[i]
        for ref in refs[:-1]:
            value = value + ref[i].astype(F32)
        out_ref[i] = value.T.astype(BF16)


def back_tile(held, mask_ref, u_ref, tile, i):
    count, col_tiles = held.shape[0], u_ref.shape[1]
    lhs = jnp.concatenate([held[p, i] for p in range(count)], axis=1)
    value = jnp.dot(lhs, u_ref[i, tile], preferred_element_type=F32)
    return (value * mask_ref[pl.ds(i * col_tiles + tile, 1)]).astype(BF16)


def gradient_piece(v_ref, back_ref, tile, inside, brick):
    total = None
    for i in range(v_ref.shape[0]):
        term = dot_nt(v_ref[i, tile, pl.ds(inside, brick)], back_ref[i])
        total = term if total is None else total + term
    return total


def adjoint_kernel(count, first, mask_ref, *refs):
    pieces, (u_ref, v_ref), rest = refs[:count], refs[count : count + 2], refs[count + 2 :]
    outs, (held, back_ref) = rest[:-2], rest[-2:]
    row_tiles, tile_len = u_ref.shape[0], u_ref.shape[2]
    brick = outs[0].shape[0]
    per_tile = tile_len // brick
    me_row, me_col = lax.axis_index("row"), lax.axis_index("col")
    for distance in range(count):
        held[me_col ^ distance] = pieces[distance][...]
    for n in range(len(outs) // per_tile):
        tile = (me_row // per_tile) ^ (first + n)
        for i in range(row_tiles):
            back_ref[i] = back_tile(held, mask_ref, u_ref, tile, i)
        for p in reversed(range(per_tile)):
            inside = pl.multiple_of(((me_row % per_tile) ^ p) * brick, brick)
            out_ref = outs[n * per_tile + p]
            value = gradient_piece(v_ref, back_ref, tile, inside, brick)
            out_ref[...] = value.astype(out_ref.dtype)


def add_kernel(part_ref, *refs):
    value = part_ref[...]
    for ref in refs[:-1]:
        value = value + ref[...].astype(F32)
    refs[-1][...] = value.astype(BF16)


def move_kernel(image_ref, part_ref, *refs):
    received, (moved_ref, even_ref, odd_ref, side_ref) = refs[:-4], refs[-4:]
    gradient = part_ref[...]
    for ref in received:
        gradient = gradient + ref[...].astype(F32)
    moved = image_ref[...] - gradient.reshape(image_ref.shape)
    moved_ref[...] = moved
    side_ref[...] = moved.astype(BF16)
    width = even_ref.shape[0]
    far = image_ref.shape[0] - width
    odd = lax.axis_index("row") % 2
    even_ref[...] = moved_ref[pl.ds((1 - odd) * far, width)].astype(BF16)
    odd_ref[...] = moved_ref[pl.ds(odd * far, width)].astype(BF16)


def corner_kernel(even_ref, odd_ref, to_even_ref, to_odd_ref):
    last = even_ref.shape[1] - 1
    row_odd, col_odd = lax.axis_index("row") % 2, lax.axis_index("col") % 2
    near, side = (1 - col_odd) * last, col_odd * last
    for out_ref, y in ((to_even_ref, near), (to_odd_ref, side)):
        low = jnp.where(row_odd == 1, even_ref[1, y], odd_ref[1, y])
        high = jnp.where(row_odd == 1, odd_ref[0, y], even_ref[0, y])
        out_ref[0] = low
        out_ref[1] = high


def flux(delta):
    scaled = delta / edge_scale
    return delta / (1.0 + scaled * scaled)


def diffuse_kernel(moved_ref, row_even, row_odd, col_even, col_odd, corner_even, corner_odd, out_ref, field):
    nx, ny, depth, frames = moved_ref.shape
    rows, cols = lax.axis_size("row"), lax.axis_size("col")
    me_row, me_col = lax.axis_index("row"), lax.axis_index("col")
    r_odd, c_odd = me_row % 2, me_col % 2
    r_even, c_even = 1 - r_odd, 1 - c_odd
    field[2 : 2 + nx, 2 : 2 + ny] = moved_ref[...]
    far_x, far_y = nx + 2, ny + 2
    field[pl.ds(r_even * far_x, 2), 2 : 2 + ny] = row_even[...].astype(F32)
    field[pl.ds(r_odd * far_x, 2), 2 : 2 + ny] = row_odd[...].astype(F32)
    field[2 : 2 + nx, pl.ds(c_even * far_y, 2)] = col_even[...].astype(F32)
    field[2 : 2 + nx, pl.ds(c_odd * far_y, 2)] = col_odd[...].astype(F32)
    for y, ref in ((c_even * (ny + 1) + 1, corner_even), (c_odd * (ny + 1) + 1, corner_odd)):
        field[1, y] = ref[0].astype(F32)
        field[nx + 2, y] = ref[1].astype(F32)
    level = lax.broadcasted_iota(jnp.int32, (depth, frames), 0)
    low_x, high_x = me_row > 0, me_row < rows - 1
    low_y, high_y = me_col > 0, me_col < cols - 1

    def along_depth(u):
        below = jnp.where(level == 0, 0.0, pltpu.roll(u, 1, 0))
        down = flux(u - below)
        up = jnp.where(level == depth - 1, flux(-u), pltpu.roll(down, depth - 1, 0))
        return up - down

    def diffuse(cells, get):
        faces = {}

        def face(kind, x, y):
            key = (kind, x, y)
            if key not in faces:
                x2, y2 = (x + 1, y) if kind == 0 else (x, y + 1)
                faces[key] = flux(get(x2, y2) - get(x, y))
            return faces[key]

        new = {}
        for x, y in cells:
            u = get(x, y)
            total = face(0, x, y) - face(0, x - 1, y)
            total = total + (face(1, x, y) - face(1, x, y - 1))
            new[x, y] = u + diff_rate * (total + along_depth(u))
        return new

    inner = [(x, y) for x in range(2, 2 + nx) for y in range(2, 2 + ny)]
    ring = [(x, y) for x in (1, nx + 2) for y in range(2, 2 + ny)]
    ring += [(x, y) for x in range(2, 2 + nx) for y in (1, ny + 2)]
    first = diffuse(sorted(inner + ring), lambda x, y: field[x, y])
    for x, y in first:
        value = first[x, y]
        for at, end, open_end in ((x, 1, low_x), (x, nx + 2, high_x), (y, 1, low_y), (y, ny + 2, high_y)):
            if at == end:
                value = jnp.where(open_end, value, 0.0)
        field[x, y] = value
    second = diffuse(inner, lambda x, y: field[x, y])
    for x, y in inner:
        out_ref[x - 2, y - 2] = second[x, y]


def step(image, u_factors, v_factors, ranks, measured):
    row_tiles, col_tiles, tile_len, rank_max = u_factors.shape
    nx, ny, depth, frames = image.shape
    brick = nx * ny * depth
    per_tile = tile_len // brick
    rows, cols = lax.axis_size("row"), lax.axis_size("col")
    chips, part_len = cols // 2, tile_len // cols
    level = lax.broadcasted_iota(jnp.int32, (row_tiles * col_tiles, rank_max), 1)
    mask = (level < ranks.reshape(-1, 1)).astype(F32)
    samples = measured.reshape(row_tiles, cols, part_len, frames)

    own_x = call(cast_kernel, (image,), [((frames, brick), BF16)])[0]
    have = {0: own_x}
    for bit in reversed(bits_of(rows)):
        for distance in list(have):
            have[distance ^ bit] = swap(have[distance], "row", bit)
    pieces = [have[distance] for distance in range(rows)]
    v_factors, wanted = load(v_factors, samples, (own_x, mask))
    u_factors, _ = load(u_factors, samples, (own_x, mask))

    u_parts = u_factors.reshape(row_tiles, col_tiles, chips, 2, part_len, rank_max)
    half = (chips, row_tiles, part_len, frames)
    near, v_factors = call(
        near_kernel,
        (mask, *pieces[:per_tile], v_factors),
        [((row_tiles, frames, rank_max), BF16)],
        [pltpu.VMEM((per_tile, frames, brick), BF16)],
        through=1,
    )
    cross, coef, u_parts, v_factors = call(
        forward_kernel,
        (mask, near, *pieces[per_tile:], u_parts, v_factors),
        [(half, BF16), ((row_tiles, col_tiles, frames, rank_max), BF16)],
        [pltpu.VMEM((rows, frames, brick), BF16)],
        through=2,
    )
    crossed = swap(cross, "col", 1)
    mine, u_parts = call(own_kernel, (coef, u_parts), [(half, F32)], through=1)
    u_factors = u_parts.reshape(u_factors.shape)
    part = (row_tiles, part_len, frames)
    own, *sends = call(
        sum_kernel, (mine, crossed, wanted), [(part, F32)] + [(part, BF16)] * (chips - 1)
    )
    received = [swap(value, "col", 2 * q) for q, value in enumerate(sends, 1)]
    (resid,) = call(resid_kernel, (own, *received), [((row_tiles, frames, part_len), BF16)])
    parts = {}
    for q in range(chips):
        parts[2 * q] = swap(resid, "col", 2 * q) if q else resid
        parts[2 * q + 1] = swap(parts[2 * q], "col", 1)

    def adjoint(distances, kinds, u_factors, v_factors):
        return call(
            functools.partial(adjoint_kernel, cols, distances[0] // per_tile),
            (mask, *[parts[d] for d in range(cols)], u_factors, v_factors),
            [((brick, frames), kind) for kind in kinds],
            [
                pltpu.VMEM((cols, row_tiles, frames, part_len), BF16),
                pltpu.VMEM((row_tiles, frames, rank_max), BF16),
            ],
            through=2,
        )

    kinds = [BF16 if d % 2 else F32 for d in range(rows)]
    *far, u_factors, v_factors = adjoint(
        range(per_tile, rows), kinds[per_tile:], u_factors, v_factors
    )
    *close, u_factors, v_factors = adjoint(range(per_tile), kinds[:per_tile], u_factors, v_factors)
    terms = close + far
    sums = {}
    for d in range(0, rows, 2):
        sums[d] = (terms[d], [swap(terms[d + 1], "row", 1)])
    for bit in bits_of(rows)[1:]:
        for d in [d for d in sums if d & bit]:
            base, extra = sums.pop(d)
            (base,) = call(add_kernel, (base, *extra), [(base.shape, BF16)])
            sums[d ^ bit][1].append(swap(base, "row", bit))
    base, extra = sums[0]

    edge = (2, ny, depth, frames)
    moved, to_even, to_odd, side = call(
        move_kernel,
        (image, base, *extra),
        [(image.shape, F32), (edge, BF16), (edge, BF16), (image.shape, BF16)],
    )
    row_even = swap(to_even, "row", 1)
    row_odd = swap_odd(to_odd, "row")
    col_odd = swap_odd(side, "col")
    col_even = swap(side, "col", 1)
    corner = (2, depth, frames)
    to_even, to_odd = call(corner_kernel, (row_even, row_odd), [(corner, BF16)] * 2)
    corner_odd = swap_odd(to_odd, "col")
    corner_even = swap(to_even, "col", 1)
    return call(
        diffuse_kernel,
        (moved, row_even, row_odd, col_even, col_odd, corner_even, corner_odd),
        [(image.shape, F32)],
        [pltpu.VMEM((nx + 4, ny + 4, depth, frames), F32)],
        jax.ShapeDtypeStruct,
    )[0]


def solution(mesh):
    placed = (
        P("row", "col", None, None),
        P("row", "col", None, None),
        P("row", "col", None, None),
        P("row", "col"),
        P("row", None),
    )
    return jax.shard_map(
        step, mesh=mesh, in_specs=placed, out_specs=P("row", "col", None, None), check_vma=False
    )
```

time: 109 us -> 78.6 us (0.72)
  Pallas kernels: 35.6 us -> 13.5 us
  local copies, waits for them, and re-layouts: 6.4 us -> 1.8 us
  waiting for transfers between devices: 30.1 us -> 27.5 us
  other arithmetic: 1.64 us -> 0.07 us
    pallas_call x10 -> x14, Pallas kernels: 35.6 us -> 13.5 us  [the longest x12 7.76 us: call(): pl.pallas_call(run, out_shape=[kept(shape, kind) for shape, kind in outs]...]
    unnamed x47 -> x5, local copies, waits for them, and re-layouts: 6.4 us -> 1.72 us
    ppermute x20, waiting for transfers between devices: 23.3 us -> 21.4 us  [swap(): return lax.ppermute(value, axis, [(i, i ^ distance) for i in range(count)])]
  transfers between devices with their start and end apart: 23 -> 23, of which waited for: 13 -> 12; matrix products, arithmetic and copies ran while one was open for 3% -> 1% of each run, Pallas kernels for 10% -> 11%
where the time goes in v3:
time: 78.6 us; the launch traced here: 78.2 us
  starting transfers between devices  35.2 us (45%)
  waiting for transfers between devices  27.5 us (35%)
  Pallas kernels  13.5 us (17%)
  local copies, waits for them, and re-layouts  1.8 us (2%)
    ppermute x20, starting transfers between devices, swap(): return lax.ppermute(value, axis, [(i, i ^ distance) for i in range(count)])  26.5 us
    ppermute x20, waiting for transfers between devices, swap(): return lax.ppermute(value, axis, [(i, i ^ distance) for i in range(count)])  21.4 us
    ppermute x3, starting transfers between devices, swap_odd(): return lax.ppermute(value, axis, pairs + [(b, a) for a, b in pairs])  8.69 us
    pallas_call x12, Pallas kernels, call(): pl.pallas_call(run, out_shape=[kept(shape, kind) for shape, kind in outs]...  7.76 us
    ppermute x3, waiting for transfers between devices, swap_odd(): return lax.ppermute(value, axis, pairs + [(b, a) for a, b in pairs])  6.03 us
    pallas_call x2, Pallas kernels, load(): pl.pallas_call(load_kernel, out_shape=[pltpu.VMEM(factors.shape, factors....  5.75 us
    unnamed x5, local copies, waits for them, and re-layouts  1.72 us
  transfers between devices with their start and end apart: 23, of which 12 were waited for; matrix products, arithmetic and copies ran while one was open for 1% of the time, Pallas kernels for 11%

profile of v3, /device:TPU:19, one launch (start us, length us, event | category | flops | bytes accessed | tf_op | source)
XLA Modules:
  0.0 78.2 jit_solution(15447116297320902888)
XLA Ops:
  1.2 1.3 %collective-permute-start = (bf16[128,512]{1,0:T(8,128)(2,1)S(1)}, bf16[128,512]{1,0:T(8,128)(2,1)S(1)}, u32[]{:S(2)}, u32[]{:S(2)}) collective-permute-start(bf16[128,512]{1,0:T(8,128)(2,1)S(1)} %shard_map.55.refs_0_.refs_1_), channel_id=1, source_target_pairs={{0,8},{8,0},{16,24},{24,16},{1,9},{9,1},{17,25},{25,17},{2,10},{10... | collective-permute-start | bytes 393224 | tf_op jit(solution)/shard_map/ppermute | solution.py:18
  3.3 3.1 %collective-permute-done.1.refs_2_ = bf16[128,512]{1,0:T(8,128)(2,1)S(1)} collective-permute-done((bf16[128,512]{1,0:T(8,128)(2,1)S(1)}, bf16[128,512]{1,0:T(8,128)(2,1)S(1)}, u32[]{:S(2)}, u32[]{:S(2)}) %collective-permute-start.1) | collective-permute-done | bytes 131104 | tf_op jit(solution)/shard_map/ppermute | solution.py:18
  6.4 5.0 %collective-permute-start.2 = (bf16[128,512]{1,0:T(8,128)(2,1)S(1)}, bf16[128,512]{1,0:T(8,128)(2,1)S(1)}, u32[]{:S(2)}, u32[]{:S(2)}) collective-permute-start(bf16[128,512]{1,0:T(8,128)(2,1)S(1)} %collective-permute-done.1.refs_2_), channel_id=1, source_target_pairs={{0,8},{8,0},{16,24},{24,16},{1,9},{9,1},{17,25},{25,17},{2,10},{10... | collective-permute-start | bytes 393224 | tf_op jit(solution)/shard_map/ppermute | solution.py:18
  11.5 2.5 %shard_map.56 = (bf16[5,2,1024,256]{3,2,1,0:T(8,128)(2,1)S(1)}, bf16[5,128,128]{2,1,0:T(8,128)(2,1)S(1)}) custom-call(bf16[5,2,1024,256]{3,2,1,0:T(8,128)(2,1)} %factor_ref.2, bf16[5,8,128,128]{3,2,1,0:T(8,128)(2,1)} %bitcast.5, bf16[128,512]{1,0:T(8,128)(2,1)S(1)} %shard_map.55.refs_0_.refs_1_, f32[10,256]{1,0:T(8,128)S(1)} %fusion.refs_1_.refs_0_), custom_call_target="tpu_custom_call" | custom-call | tf_op jit(solution)/shard_map/pallas_call | solution.py:73
  14.1 3.2 %shard_map.58 = (bf16[5,2,1024,256]{3,2,1,0:T(8,128)(2,1)S(1)}, bf16[5,128,128]{2,1,0:T(8,128)(2,1)}) custom-call(bf16[5,2,1024,256]{3,2,1,0:T(8,128)(2,1)} %factor_ref.3, bf16[5,8,128,128]{3,2,1,0:T(8,128)(2,1)} %bitcast.6, bf16[128,512]{1,0:T(8,128)(2,1)S(1)} %shard_map.55.refs_0_.refs_1_, f32[10,256]{1,0:T(8,128)S(1)} %fusion.refs_1_.refs_0_), custom_call_target="tpu_custom_call" | custom-call | tf_op jit(solution)/shard_map/pallas_call | solution.py:73
  17.8 1.5 %shard_map.59 = (bf16[4,5,128,128]{3,2,1,0:T(8,128)(2,1)S(1)}, bf16[5,2,128,256]{3,2,1,0:T(8,128)(2,1)S(1)}, bf16[5,2,4,2,128,256]{5,4,3,2,1,0:T(8,128)(2,1)S(1)}, bf16[5,2,1024,256]{3,2,1,0:T(8,128)(2,1)S(1)}) custom-call(f32[10,256]{1,0:T(8,128)S(1)} %fusion.refs_1_.refs_0_, ...), custom_call_target="tpu_custom_call", output_to_operand_aliasing={{2}: (4, {}), {3}: (5, {})} | custom-call | tf_op jit(solution)/shard_map/pallas_call | solution.py:48
  24.8 2.7 %collective-permute-done.4.refs_1_ = bf16[5,128,128]{2,1,0:T(8,128)(2,1)S(1)} collective-permute-done((bf16[5,128,128]{2,1,0:T(8,128)(2,1)S(1)}, bf16[5,128,128]{2,1,0:T(8,128)(2,1)S(1)}, u32[]{:S(2)}, u32[]{:S(2)}) %collective-permute-start.4) | collective-permute-done | bytes 163872 | tf_op jit(solution)/shard_map/ppermute | solution.py:18
  27.5 4.5 %collective-permute-done.6.refs_3_ = bf16[5,128,128]{2,1,0:T(8,128)(2,1)S(1)} collective-permute-done((bf16[5,128,128]{2,1,0:T(8,128)(2,1)S(1)}, bf16[5,128,128]{2,1,0:T(8,128)(2,1)S(1)}, u32[]{:S(2)}, u32[]{:S(2)}) %collective-permute-start.6) | collective-permute-done | bytes 163872 | tf_op jit(solution)/shard_map/ppermute | solution.py:18
  34.8 2.1 %collective-permute-start.7 = (bf16[5,128,128]{2,1,0:T(8,128)(2,1)S(1)}, bf16[5,128,128]{2,1,0:T(8,128)(2,1)S(1)}, u32[]{:S(2)}, u32[]{:S(2)}) collective-permute-start(bf16[5,128,128]{2,1,0:T(8,128)(2,1)S(1)} %shard_map.62.refs_1_), channel_id=1, source_target_pairs={{0,1},{1,0},{2,3},{3,2},{4,5},{5,4},{6,7},{7,6},{8,9},{9,8},{10,11... | collective-permute-start | bytes 491528 | tf_op jit(solution)/shard_map/ppermute | solution.py:18
  36.9 2.6 %collective-permute-done.10.refs_5_ = bf16[5,128,128]{2,1,0:T(8,128)(2,1)S(1)} collective-permute-done((bf16[5,128,128]{2,1,0:T(8,128)(2,1)S(1)}, bf16[5,128,128]{2,1,0:T(8,128)(2,1)S(1)}, u32[]{:S(2)}, u32[]{:S(2)}) %collective-permute-start.10) | collective-permute-done | bytes 163872 | tf_op jit(solution)/shard_map/ppermute | solution.py:18
  39.5 2.8 %collective-permute-start.11 = (bf16[5,128,128]{2,1,0:T(8,128)(2,1)S(1)}, bf16[5,128,128]{2,1,0:T(8,128)(2,1)S(1)}, u32[]{:S(2)}, u32[]{:S(2)}) collective-permute-start(bf16[5,128,128]{2,1,0:T(8,128)(2,1)S(1)} %collective-permute-done.10.refs_5_), channel_id=1, source_target_pairs={{0,1},{1,0},{2,3},{3,2},{4,5},{5,4},{6,7},{7,6},{8,9},{9,8},{10,11... | collective-permute-start | bytes 491528 | tf_op jit(solution)/shard_map/ppermute | solution.py:18
  45.9 1.3 %shard_map.64 = (f32[512,128]{1,0:T(8,128)S(1)}, bf16[512,128]{1,0:T(8,128)(2,1)S(1)}, bf16[5,2,1024,256]{3,2,1,0:T(8,128)(2,1)S(1)}, bf16[5,2,1024,256]{3,2,1,0:T(8,128)(2,1)S(1)}) custom-call(f32[10,256]{1,0:T(8,128)S(1)} %fusion.refs_1_.refs_0_, bf16[5,128,128]{2,1,0:T(8,128)(2,1)S(1)} %shard_map.62.refs_1_, ...), custom_call_target="tpu_custom_call", output_to_operand_aliasing={{2}: (9, {}), {3}: (10, {})} | custom-call | tf_op jit(solution)/shard_map/pallas_call | solution.py:48
  47.2 1.5 %collective-permute-start.14 = (bf16[512,128]{1,0:T(8,128)(2,1)S(1)}, bf16[512,128]{1,0:T(8,128)(2,1)S(1)}, u32[]{:S(2)}, u32[]{:S(2)}) collective-permute-start(bf16[512,128]{1,0:T(8,128)(2,1)S(1)} %get-tuple-element.50), channel_id=1, source_target_pairs={{0,8},{8,0},{16,24},{24,16},{1,9},{9,1},{17,25},{25,17},{2,10},{10... | collective-permute-start | bytes 393224 | tf_op jit(solution)/shard_map/ppermute | solution.py:18
  48.7 1.9 %collective-permute-done.15.refs_1_ = bf16[512,128]{1,0:T(8,128)(2,1)S(1)} collective-permute-done((bf16[512,128]{1,0:T(8,128)(2,1)S(1)}, bf16[512,128]{1,0:T(8,128)(2,1)S(1)}, u32[]{:S(2)}, u32[]{:S(2)}) %collective-permute-start.15) | collective-permute-done | bytes 131104 | tf_op jit(solution)/shard_map/ppermute | solution.py:18
  50.7 2.7 %collective-permute-done.14.refs_2_ = bf16[512,128]{1,0:T(8,128)(2,1)S(1)} collective-permute-done((bf16[512,128]{1,0:T(8,128)(2,1)S(1)}, bf16[512,128]{1,0:T(8,128)(2,1)S(1)}, u32[]{:S(2)}, u32[]{:S(2)}) %collective-permute-start.14) | collective-permute-done | bytes 131104 | tf_op jit(solution)/shard_map/ppermute | solution.py:18
  53.4 2.1 %collective-permute-done.16.refs_3_ = bf16[512,128]{1,0:T(8,128)(2,1)S(1)} collective-permute-done((bf16[512,128]{1,0:T(8,128)(2,1)S(1)}, bf16[512,128]{1,0:T(8,128)(2,1)S(1)}, u32[]{:S(2)}, u32[]{:S(2)}) %collective-permute-start.16) | collective-permute-done | bytes 131104 | tf_op jit(solution)/shard_map/ppermute | solution.py:18
  55.6 3.3 %collective-permute-start.19 = (bf16[4,2,64,128]{3,2,1,0:T(8,128)(2,1)S(1)}, bf16[4,2,64,128]{3,2,1,0:T(8,128)(2,1)S(1)}, u32[]{:S(2)}, u32[]{:S(2)}) collective-permute-start(bf16[4,2,64,128]{3,2,1,0:T(8,128)(2,1)S(1)} %get-tuple-element.56), channel_id=1, source_target_pairs={{0,1},{1,0},{2,3},{3,2},{4,5},{5,4},{6,7},{7,6},{8,9},{9,8},{10,11... | collective-permute-start | bytes 393224 | tf_op jit(solution)/shard_map/ppermute | solution.py:18
  58.9 3.0 %collective-permute-start.20 = (bf16[4,2,64,128]{3,2,1,0:T(8,128)(2,1)S(1)}, bf16[4,2,64,128]{3,2,1,0:T(8,128)(2,1)S(1)}, u32[]{:S(2)}, u32[]{:S(2)}) collective-permute-start(bf16[4,2,64,128]{3,2,1,0:T(8,128)(2,1)S(1)} %get-tuple-element.56), channel_id=1, source_target_pairs={{1,2},{3,4},{5,6},{2,1},{4,3},{6,5},{9,10},{11,12},{13,14},{10,9},... | collective-permute-start | bytes 393224 | tf_op jit(solution)/shard_map/ppermute | solution.py:24
  61.9 2.0 %collective-permute-start.17 = (bf16[2,2,64,128]{3,2,1,0:T(8,128)(2,1)S(1)}, bf16[2,2,64,128]{3,2,1,0:T(8,128)(2,1)S(1)}, u32[]{:S(2)}, u32[]{:S(2)}) collective-permute-start(bf16[2,2,64,128]{3,2,1,0:T(8,128)(2,1)S(1)} %get-tuple-element.54), channel_id=1, source_target_pairs={{0,8},{8,0},{16,24},{24,16},{1,9},{9,1},{17,25},{25,17},{2,10},{10... | collective-permute-start | bytes 196616 | tf_op jit(solution)/shard_map/ppermute | solution.py:18
  63.8 2.2 %collective-permute-start.18 = (bf16[2,2,64,128]{3,2,1,0:T(8,128)(2,1)S(1)}, bf16[2,2,64,128]{3,2,1,0:T(8,128)(2,1)S(1)}, u32[]{:S(2)}, u32[]{:S(2)}) collective-permute-start(bf16[2,2,64,128]{3,2,1,0:T(8,128)(2,1)S(1)} %get-tuple-element.55), channel_id=1, source_target_pairs={{8,16},{16,8},{9,17},{17,9},{10,18},{18,10},{11,19},{19,11},{12,20... | collective-permute-start | bytes 196616 | tf_op jit(solution)/shard_map/ppermute | solution.py:24
  66.0 3.4 %collective-permute-done.18.refs_1_.refs_2_ = bf16[2,2,64,128]{3,2,1,0:T(8,128)(2,1)S(1)} collective-permute-done((bf16[2,2,64,128]{3,2,1,0:T(8,128)(2,1)S(1)}, bf16[2,2,64,128]{3,2,1,0:T(8,128)(2,1)S(1)}, u32[]{:S(2)}, u32[]{:S(2)}) %collective-permute-start.18) | collective-permute-done | bytes 65568 | tf_op jit(solution)/shard_map/ppermute | solution.py:24
  70.3 3.5 %collective-permute-start.22 = (bf16[2,64,128]{2,1,0:T(8,128)(2,1)S(1)}, bf16[2,64,128]{2,1,0:T(8,128)(2,1)S(1)}, u32[]{:S(2)}, u32[]{:S(2)}) collective-permute-start(bf16[2,64,128]{2,1,0:T(8,128)(2,1)S(1)} %get-tuple-element.58), channel_id=1, source_target_pairs={{1,2},{3,4},{5,6},{2,1},{4,3},{6,5},{9,10},{11,12},{13,14},{10,9},... | collective-permute-start | bytes 98312 | tf_op jit(solution)/shard_map/ppermute | solution.py:24
  73.8 2.6 %collective-permute-done.22.refs_6_ = bf16[2,64,128]{2,1,0:T(8,128)(2,1)S(1)} collective-permute-done((bf16[2,64,128]{2,1,0:T(8,128)(2,1)S(1)}, bf16[2,64,128]{2,1,0:T(8,128)(2,1)S(1)}, u32[]{:S(2)}, u32[]{:S(2)}) %collective-permute-start.22) | collective-permute-done | bytes 32800 | tf_op jit(solution)/shard_map/ppermute | solution.py:24
  76.4 1.8 %shard_map.68 = f32[4,2,64,128]{3,2,1,0:T(8,128)} custom-call(f32[4,2,64,128]{3,2,1,0:T(8,128)S(1)} %get-tuple-element.53.refs_0_, bf16[2,2,64,128]{3,2,1,0:T(8,128)(2,1)S(1)} %collective-permute-done.17.refs_0_.refs_1_, bf16[2,2,64,128]{3,2,1,0:T(8,128)(2,1)S(1)} %collective-permute-done.18.refs_1_.refs_2_, ...), custom_call_target="tpu_custom_call" | custom-call | tf_op jit(solution)/shard_map/pallas_call | solution.py:48
  (43 shorter events, 15.5 us)
Async XLA Ops:
  1.1 5.4 %collective-permute-start.1 = (bf16[128,512]{1,0:T(8,128)(2,1)S(1)}, bf16[128,512]{1,0:T(8,128)(2,1)S(1)}, u32[]{:S(2)}, u32[]{:S(2)}) collective-permute-start(bf16[128,512]{1,0:T(8,128)(2,1)S(1)} %shard_map.55.refs_0_.refs_1_), channel_id=1, source_target_pairs={{0,16},{8,24},{16,0},{24,8},{1,17},{9,25},{17,1},{25,9},{2,18},{10... | collective-permute-start | bytes 393224 | tf_op jit(solution)/shard_map/ppermute | solution.py:18
  1.2 16.1 %collective-permute-start = (bf16[128,512]{1,0:T(8,128)(2,1)S(1)}, bf16[128,512]{1,0:T(8,128)(2,1)S(1)}, u32[]{:S(2)}, u32[]{:S(2)}) collective-permute-start(bf16[128,512]{1,0:T(8,128)(2,1)S(1)} %shard_map.55.refs_0_.refs_1_), channel_id=1, source_target_pairs={{0,8},{8,0},{16,24},{24,16},{1,9},{9,1},{17,25},{25,17},{2,10},{10... | collective-permute-start | bytes 393224 | tf_op jit(solution)/shard_map/ppermute | solution.py:18
  6.4 11.4 %collective-permute-start.2 = (bf16[128,512]{1,0:T(8,128)(2,1)S(1)}, bf16[128,512]{1,0:T(8,128)(2,1)S(1)}, u32[]{:S(2)}, u32[]{:S(2)}) collective-permute-start(bf16[128,512]{1,0:T(8,128)(2,1)S(1)} %collective-permute-done.1.refs_2_), channel_id=1, source_target_pairs={{0,8},{8,0},{16,24},{24,16},{1,9},{9,1},{17,25},{25,17},{2,10},{10... | collective-permute-start | bytes 393224 | tf_op jit(solution)/shard_map/ppermute | solution.py:18
  19.4 2.6 %collective-permute-start.3 = (bf16[4,5,128,128]{3,2,1,0:T(8,128)(2,1)S(1)}, bf16[4,5,128,128]{3,2,1,0:T(8,128)(2,1)S(1)}, u32[]{:S(2)}, u32[]{:S(2)}) collective-permute-start(bf16[4,5,128,128]{3,2,1,0:T(8,128)(2,1)S(1)} %get-tuple-element.39), channel_id=1, source_target_pairs={{0,1},{1,0},{2,3},{3,2},{4,5},{5,4},{6,7},{7,6},{8,9},{9,8},{10,11... | collective-permute-start | bytes 1966088 | tf_op jit(solution)/shard_map/ppermute | solution.py:18
  22.0 5.5 %collective-permute-start.4 = (bf16[5,128,128]{2,1,0:T(8,128)(2,1)S(1)}, bf16[5,128,128]{2,1,0:T(8,128)(2,1)S(1)}, u32[]{:S(2)}, u32[]{:S(2)}) collective-permute-start(bf16[5,128,128]{2,1,0:T(8,128)(2,1)S(1)} %get-tuple-element.42), channel_id=1, source_target_pairs={{0,2},{1,3},{2,0},{3,1},{4,6},{5,7},{6,4},{7,5},{8,10},{9,11},{10,... | collective-permute-start | bytes 491528 | tf_op jit(solution)/shard_map/ppermute | solution.py:18
  22.4 5.1 %collective-permute-start.5 = (bf16[5,128,128]{2,1,0:T(8,128)(2,1)S(1)}, bf16[5,128,128]{2,1,0:T(8,128)(2,1)S(1)}, u32[]{:S(2)}, u32[]{:S(2)}) collective-permute-start(bf16[5,128,128]{2,1,0:T(8,128)(2,1)S(1)} %get-tuple-element.43), channel_id=1, source_target_pairs={{0,4},{1,5},{2,6},{3,7},{4,0},{5,1},{6,2},{7,3},{8,12},{9,13},{10,... | collective-permute-start | bytes 491528 | tf_op jit(solution)/shard_map/ppermute | solution.py:18
  23.6 8.4 %collective-permute-start.6 = (bf16[5,128,128]{2,1,0:T(8,128)(2,1)S(1)}, bf16[5,128,128]{2,1,0:T(8,128)(2,1)S(1)}, u32[]{:S(2)}, u32[]{:S(2)}) collective-permute-start(bf16[5,128,128]{2,1,0:T(8,128)(2,1)S(1)} %get-tuple-element.44), channel_id=1, source_target_pairs={{0,6},{1,7},{2,4},{3,5},{4,2},{5,3},{6,0},{7,1},{8,14},{9,15},{10,... | collective-permute-start | bytes 491528 | tf_op jit(solution)/shard_map/ppermute | solution.py:18
  32.1 7.3 %collective-permute-start.10 = (bf16[5,128,128]{2,1,0:T(8,128)(2,1)S(1)}, bf16[5,128,128]{2,1,0:T(8,128)(2,1)S(1)}, u32[]{:S(2)}, u32[]{:S(2)}) collective-permute-start(bf16[5,128,128]{2,1,0:T(8,128)(2,1)S(1)} %shard_map.62.refs_1_), channel_id=1, source_target_pairs={{0,4},{1,5},{2,6},{3,7},{4,0},{5,1},{6,2},{7,3},{8,12},{9,13},{10,... | collective-permute-start | bytes 491528 | tf_op jit(solution)/shard_map/ppermute | solution.py:18
  32.4 9.9 %collective-permute-start.12 = (bf16[5,128,128]{2,1,0:T(8,128)(2,1)S(1)}, bf16[5,128,128]{2,1,0:T(8,128)(2,1)S(1)}, u32[]{:S(2)}, u32[]{:S(2)}) collective-permute-start(bf16[5,128,128]{2,1,0:T(8,128)(2,1)S(1)} %shard_map.62.refs_1_), channel_id=1, source_target_pairs={{0,6},{1,7},{2,4},{3,5},{4,2},{5,3},{6,0},{7,1},{8,14},{9,15},{10,... | collective-permute-start | bytes 491528 | tf_op jit(solution)/shard_map/ppermute | solution.py:18
  33.7 8.7 %collective-permute-start.8 = (bf16[5,128,128]{2,1,0:T(8,128)(2,1)S(1)}, bf16[5,128,128]{2,1,0:T(8,128)(2,1)S(1)}, u32[]{:S(2)}, u32[]{:S(2)}) collective-permute-start(bf16[5,128,128]{2,1,0:T(8,128)(2,1)S(1)} %shard_map.62.refs_1_), channel_id=1, source_target_pairs={{0,2},{1,3},{2,0},{3,1},{4,6},{5,7},{6,4},{7,5},{8,10},{9,11},{10,... | collective-permute-start | bytes 491528 | tf_op jit(solution)/shard_map/ppermute | solution.py:18
  34.8 8.7 %collective-permute-start.7 = (bf16[5,128,128]{2,1,0:T(8,128)(2,1)S(1)}, bf16[5,128,128]{2,1,0:T(8,128)(2,1)S(1)}, u32[]{:S(2)}, u32[]{:S(2)}) collective-permute-start(bf16[5,128,128]{2,1,0:T(8,128)(2,1)S(1)} %shard_map.62.refs_1_), channel_id=1, source_target_pairs={{0,1},{1,0},{2,3},{3,2},{4,5},{5,4},{6,7},{7,6},{8,9},{9,8},{10,11... | collective-permute-start | bytes 491528 | tf_op jit(solution)/shard_map/ppermute | solution.py:18
  39.5 4.1 %collective-permute-start.11 = (bf16[5,128,128]{2,1,0:T(8,128)(2,1)S(1)}, bf16[5,128,128]{2,1,0:T(8,128)(2,1)S(1)}, u32[]{:S(2)}, u32[]{:S(2)}) collective-permute-start(bf16[5,128,128]{2,1,0:T(8,128)(2,1)S(1)} %collective-permute-done.10.refs_5_), channel_id=1, source_target_pairs={{0,1},{1,0},{2,3},{3,2},{4,5},{5,4},{6,7},{7,6},{8,9},{9,8},{10,11... | collective-permute-start | bytes 491528 | tf_op jit(solution)/shard_map/ppermute | solution.py:18
  42.3 1.4 %collective-permute-start.13 = (bf16[5,128,128]{2,1,0:T(8,128)(2,1)S(1)}, bf16[5,128,128]{2,1,0:T(8,128)(2,1)S(1)}, u32[]{:S(2)}, u32[]{:S(2)}) collective-permute-start(bf16[5,128,128]{2,1,0:T(8,128)(2,1)S(1)} %collective-permute-done.12.refs_7_), channel_id=1, source_target_pairs={{0,1},{1,0},{2,3},{3,2},{4,5},{5,4},{6,7},{7,6},{8,9},{9,8},{10,11... | collective-permute-start | bytes 491528 | tf_op jit(solution)/shard_map/ppermute | solution.py:18
  42.3 2.2 %collective-permute-start.9 = (bf16[5,128,128]{2,1,0:T(8,128)(2,1)S(1)}, bf16[5,128,128]{2,1,0:T(8,128)(2,1)S(1)}, u32[]{:S(2)}, u32[]{:S(2)}) collective-permute-start(bf16[5,128,128]{2,1,0:T(8,128)(2,1)S(1)} %collective-permute-done.8.refs_3_), channel_id=1, source_target_pairs={{0,1},{1,0},{2,3},{3,2},{4,5},{5,4},{6,7},{7,6},{8,9},{9,8},{10,11... | collective-permute-start | bytes 491528 | tf_op jit(solution)/shard_map/ppermute | solution.py:18
  45.8 4.7 %collective-permute-start.15 = (bf16[512,128]{1,0:T(8,128)(2,1)S(1)}, bf16[512,128]{1,0:T(8,128)(2,1)S(1)}, u32[]{:S(2)}, u32[]{:S(2)}) collective-permute-start(bf16[512,128]{1,0:T(8,128)(2,1)S(1)} %get-tuple-element.52), channel_id=1, source_target_pairs={{0,8},{8,0},{16,24},{24,16},{1,9},{9,1},{17,25},{25,17},{2,10},{10... | collective-permute-start | bytes 393224 | tf_op jit(solution)/shard_map/ppermute | solution.py:18
  45.9 9.6 %copy-start.1 = (f32[4,2,64,128]{3,2,1,0:T(8,128)S(1)}, f32[4,2,64,128]{3,2,1,0:T(8,128)}, u32[]{:S(2)}) copy-start(f32[4,2,64,128]{3,2,1,0:T(8,128)} %refs_0_.3) | copy-start | bytes 786436
  47.2 6.2 %collective-permute-start.14 = (bf16[512,128]{1,0:T(8,128)(2,1)S(1)}, bf16[512,128]{1,0:T(8,128)(2,1)S(1)}, u32[]{:S(2)}, u32[]{:S(2)}) collective-permute-start(bf16[512,128]{1,0:T(8,128)(2,1)S(1)} %get-tuple-element.50), channel_id=1, source_target_pairs={{0,8},{8,0},{16,24},{24,16},{1,9},{9,1},{17,25},{25,17},{2,10},{10... | collective-permute-start | bytes 393224 | tf_op jit(solution)/shard_map/ppermute | solution.py:18
  50.6 4.9 %collective-permute-start.16 = (bf16[512,128]{1,0:T(8,128)(2,1)S(1)}, bf16[512,128]{1,0:T(8,128)(2,1)S(1)}, u32[]{:S(2)}, u32[]{:S(2)}) collective-permute-start(bf16[512,128]{1,0:T(8,128)(2,1)S(1)} %shard_map.65), channel_id=1, source_target_pairs={{0,16},{8,24},{16,0},{24,8},{1,17},{9,25},{17,1},{25,9},{2,18},{10... | collective-permute-start | bytes 393224 | tf_op jit(solution)/shard_map/ppermute | solution.py:18
  55.6 20.8 %collective-permute-start.19 = (bf16[4,2,64,128]{3,2,1,0:T(8,128)(2,1)S(1)}, bf16[4,2,64,128]{3,2,1,0:T(8,128)(2,1)S(1)}, u32[]{:S(2)}, u32[]{:S(2)}) collective-permute-start(bf16[4,2,64,128]{3,2,1,0:T(8,128)(2,1)S(1)} %get-tuple-element.56), channel_id=1, source_target_pairs={{0,1},{1,0},{2,3},{3,2},{4,5},{5,4},{6,7},{7,6},{8,9},{9,8},{10,11... | collective-permute-start | bytes 393224 | tf_op jit(solution)/shard_map/ppermute | solution.py:18
  58.9 17.6 %collective-permute-start.20 = (bf16[4,2,64,128]{3,2,1,0:T(8,128)(2,1)S(1)}, bf16[4,2,64,128]{3,2,1,0:T(8,128)(2,1)S(1)}, u32[]{:S(2)}, u32[]{:S(2)}) collective-permute-start(bf16[4,2,64,128]{3,2,1,0:T(8,128)(2,1)S(1)} %get-tuple-element.56), channel_id=1, source_target_pairs={{1,2},{3,4},{5,6},{2,1},{4,3},{6,5},{9,10},{11,12},{13,14},{10,9},... | collective-permute-start | bytes 393224 | tf_op jit(solution)/shard_map/ppermute | solution.py:24
  61.9 4.2 %collective-permute-start.17 = (bf16[2,2,64,128]{3,2,1,0:T(8,128)(2,1)S(1)}, bf16[2,2,64,128]{3,2,1,0:T(8,128)(2,1)S(1)}, u32[]{:S(2)}, u32[]{:S(2)}) collective-permute-start(bf16[2,2,64,128]{3,2,1,0:T(8,128)(2,1)S(1)} %get-tuple-element.54), channel_id=1, source_target_pairs={{0,8},{8,0},{16,24},{24,16},{1,9},{9,1},{17,25},{25,17},{2,10},{10... | collective-permute-start | bytes 196616 | tf_op jit(solution)/shard_map/ppermute | solution.py:18
  63.8 5.6 %collective-permute-start.18 = (bf16[2,2,64,128]{3,2,1,0:T(8,128)(2,1)S(1)}, bf16[2,2,64,128]{3,2,1,0:T(8,128)(2,1)S(1)}, u32[]{:S(2)}, u32[]{:S(2)}) collective-permute-start(bf16[2,2,64,128]{3,2,1,0:T(8,128)(2,1)S(1)} %get-tuple-element.55), channel_id=1, source_target_pairs={{8,16},{16,8},{9,17},{17,9},{10,18},{18,10},{11,19},{19,11},{12,20... | collective-permute-start | bytes 196616 | tf_op jit(solution)/shard_map/ppermute | solution.py:24
  69.5 4.3 %collective-permute-start.21 = (bf16[2,64,128]{2,1,0:T(8,128)(2,1)S(1)}, bf16[2,64,128]{2,1,0:T(8,128)(2,1)S(1)}, u32[]{:S(2)}, u32[]{:S(2)}) collective-permute-start(bf16[2,64,128]{2,1,0:T(8,128)(2,1)S(1)} %get-tuple-element.57), channel_id=1, source_target_pairs={{0,1},{1,0},{2,3},{3,2},{4,5},{5,4},{6,7},{7,6},{8,9},{9,8},{10,11... | collective-permute-start | bytes 98312 | tf_op jit(solution)/shard_map/ppermute | solution.py:18
  70.3 6.1 %collective-permute-start.22 = (bf16[2,64,128]{2,1,0:T(8,128)(2,1)S(1)}, bf16[2,64,128]{2,1,0:T(8,128)(2,1)S(1)}, u32[]{:S(2)}, u32[]{:S(2)}) collective-permute-start(bf16[2,64,128]{2,1,0:T(8,128)(2,1)S(1)} %get-tuple-element.58), channel_id=1, source_target_pairs={{1,2},{3,4},{5,6},{2,1},{4,3},{6,5},{9,10},{11,12},{13,14},{10,9},... | collective-permute-start | bytes 98312 | tf_op jit(solution)/shard_map/ppermute | solution.py:24
  (1 other events, 0.9 us)

commit v4 on v3

--- a/solution.py
+++ b/solution.py
@@ -19,9 +19,21 @@
 
 
 def swap_odd(value, axis):
-    count = lax.axis_size(axis)
-    pairs = [(i, i + 1) for i in range(1, count - 1, 2)]
-    return lax.ppermute(value, axis, pairs + [(b, a) for a, b in pairs])
+    rows, cols = lax.axis_size("row"), lax.axis_size("col")
+
+    def partner(row, col):
+        along, count = (row, rows) if axis == "row" else (col, cols)
+        if along in (0, count - 1):
+            return (row, col ^ 1) if axis == "row" else (row ^ 1, col)
+        move = 1 if along % 2 else -1
+        return (row + move, col) if axis == "row" else (row, col + move)
+
+    pairs = []
+    for row in range(rows):
+        for col in range(cols):
+            target = partner(row, col)
+            pairs.append((row * cols + col, target[0] * cols + target[1]))
+    return lax.ppermute(value, ("row", "col"), pairs)
 
 
 def bits_of(count):
@@ -238,18 +250,22 @@
     me_row, me_col = lax.axis_index("row"), lax.axis_index("col")
     r_odd, c_odd = me_row % 2, me_col % 2
     r_even, c_even = 1 - r_odd, 1 - c_odd
+    low_x, high_x = me_row > 0, me_row < rows - 1
+    low_y, high_y = me_col > 0, me_col < cols - 1
+    within = lambda ref, inside: jnp.where(inside, ref.astype(F32), 0.0)
     field[2 : 2 + nx, 2 : 2 + ny] = moved_ref[...]
     far_x, far_y = nx + 2, ny + 2
     field[pl.ds(r_even * far_x, 2), 2 : 2 + ny] = row_even[...].astype(F32)
-    field[pl.ds(r_odd * far_x, 2), 2 : 2 + ny] = row_odd[...].astype(F32)
+    field[pl.ds(r_odd * far_x, 2), 2 : 2 + ny] = within(row_odd[...], low_x & high_x)
     field[2 : 2 + nx, pl.ds(c_even * far_y, 2)] = col_even[...].astype(F32)
-    field[2 : 2 + nx, pl.ds(c_odd * far_y, 2)] = col_odd[...].astype(F32)
-    for y, ref in ((c_even * (ny + 1) + 1, corner_even), (c_odd * (ny + 1) + 1, corner_odd)):
-        field[1, y] = ref[0].astype(F32)
-        field[nx + 2, y] = ref[1].astype(F32)
+    field[2 : 2 + nx, pl.ds(c_odd * far_y, 2)] = within(col_odd[...], low_y & high_y)
+    for y, ref, inside in (
+        (c_even * (ny + 1) + 1, corner_even, True),
+        (c_odd * (ny + 1) + 1, corner_odd, low_y & high_y),
+    ):
+        field[1, y] = within(ref[0], low_x & inside)
+        field[nx + 2, y] = within(ref[1], high_x & inside)
     level = lax.broadcasted_iota(jnp.int32, (depth, frames), 0)
-    low_x, high_x = me_row > 0, me_row < rows - 1
-    low_y, high_y = me_col > 0, me_col < cols - 1
 
     def along_depth(u):
         below = jnp.where(level == 0, 0.0, pltpu.roll(u, 1, 0))

time: 78.6 us -> 74.1 us (0.943)
  the two profiles are of different devices: /device:TPU:19 before, /device:TPU:0 now
where the time goes in v4:
time: 74.1 us; the launch traced here: 73.9 us
  waiting for transfers between devices  36 us (49%)
  starting transfers between devices  22.4 us (30%)
  Pallas kernels  13.5 us (18%)
  local copies, waits for them, and re-layouts  1.8 us (2%)
    ppermute x20, waiting for transfers between devices, swap(): return lax.ppermute(value, axis, [(i, i ^ distance) for i in range(count)])  33.2 us
    ppermute x20, starting transfers between devices, swap(): return lax.ppermute(value, axis, [(i, i ^ distance) for i in range(count)])  21.8 us
    pallas_call x12, Pallas kernels, call(): pl.pallas_call(run, out_shape=[kept(shape, kind) for shape, kind in outs]...  7.76 us
    pallas_call x2, Pallas kernels, load(): pl.pallas_call(load_kernel, out_shape=[pltpu.VMEM(factors.shape, factors....  5.75 us
    ppermute x3, waiting for transfers between devices, swap_odd(): return lax.ppermute(value, ('row', 'col'), pairs)  2.79 us
    unnamed x5, local copies, waits for them, and re-layouts  1.72 us
  transfers between devices with their start and end apart: 23, of which 14 were waited for; matrix products, arithmetic and copies ran while one was open for 1% of the time, Pallas kernels for 11%

profile of v4, /device:TPU:0, one launch (start us, length us, event | category | flops | bytes accessed | tf_op | source)
XLA Modules:
  0.0 73.9 jit_solution(3607782159453259519)
XLA Ops:
  1.1 4.1 %collective-permute-start.1 = (bf16[128,512]{1,0:T(8,128)(2,1)S(1)}, bf16[128,512]{1,0:T(8,128)(2,1)S(1)}, u32[]{:S(2)}, u32[]{:S(2)}) collective-permute-start(bf16[128,512]{1,0:T(8,128)(2,1)S(1)} %shard_map.55.refs_0_.refs_1_), channel_id=1, source_target_pairs={{0,16},{8,24},{16,0},{24,8},{1,17},{9,25},{17,1},{25,9},{2,18},{10... | collective-permute-start | bytes 393224 | tf_op jit(solution)/shard_map/ppermute | solution.py:18
  5.2 1.6 %collective-permute-start = (bf16[128,512]{1,0:T(8,128)(2,1)S(1)}, bf16[128,512]{1,0:T(8,128)(2,1)S(1)}, u32[]{:S(2)}, u32[]{:S(2)}) collective-permute-start(bf16[128,512]{1,0:T(8,128)(2,1)S(1)} %shard_map.55.refs_0_.refs_1_), channel_id=1, source_target_pairs={{0,8},{8,0},{16,24},{24,16},{1,9},{9,1},{17,25},{25,17},{2,10},{10... | collective-permute-start | bytes 393224 | tf_op jit(solution)/shard_map/ppermute | solution.py:18
  7.6 4.0 %collective-permute-done.1.refs_2_ = bf16[128,512]{1,0:T(8,128)(2,1)S(1)} collective-permute-done((bf16[128,512]{1,0:T(8,128)(2,1)S(1)}, bf16[128,512]{1,0:T(8,128)(2,1)S(1)}, u32[]{:S(2)}, u32[]{:S(2)}) %collective-permute-start.1) | collective-permute-done | bytes 131104 | tf_op jit(solution)/shard_map/ppermute | solution.py:18
  12.3 2.5 %shard_map.56 = (bf16[5,2,1024,256]{3,2,1,0:T(8,128)(2,1)S(1)}, bf16[5,128,128]{2,1,0:T(8,128)(2,1)S(1)}) custom-call(bf16[5,2,1024,256]{3,2,1,0:T(8,128)(2,1)} %factor_ref.2, bf16[5,8,128,128]{3,2,1,0:T(8,128)(2,1)} %bitcast.5, bf16[128,512]{1,0:T(8,128)(2,1)S(1)} %shard_map.55.refs_0_.refs_1_, f32[10,256]{1,0:T(8,128)S(1)} %fusion.refs_1_.refs_0_), custom_call_target="tpu_custom_call" | custom-call | tf_op jit(solution)/shard_map/pallas_call | solution.py:85
  14.8 3.2 %shard_map.58 = (bf16[5,2,1024,256]{3,2,1,0:T(8,128)(2,1)S(1)}, bf16[5,128,128]{2,1,0:T(8,128)(2,1)}) custom-call(bf16[5,2,1024,256]{3,2,1,0:T(8,128)(2,1)} %factor_ref.3, bf16[5,8,128,128]{3,2,1,0:T(8,128)(2,1)} %bitcast.6, bf16[128,512]{1,0:T(8,128)(2,1)S(1)} %shard_map.55.refs_0_.refs_1_, f32[10,256]{1,0:T(8,128)S(1)} %fusion.refs_1_.refs_0_), custom_call_target="tpu_custom_call" | custom-call | tf_op jit(solution)/shard_map/pallas_call | solution.py:85
  18.6 1.5 %shard_map.59 = (bf16[4,5,128,128]{3,2,1,0:T(8,128)(2,1)S(1)}, bf16[5,2,128,256]{3,2,1,0:T(8,128)(2,1)S(1)}, bf16[5,2,4,2,128,256]{5,4,3,2,1,0:T(8,128)(2,1)S(1)}, bf16[5,2,1024,256]{3,2,1,0:T(8,128)(2,1)S(1)}) custom-call(f32[10,256]{1,0:T(8,128)S(1)} %fusion.refs_1_.refs_0_, ...), custom_call_target="tpu_custom_call", output_to_operand_aliasing={{2}: (4, {}), {3}: (5, {})} | custom-call | tf_op jit(solution)/shard_map/pallas_call | solution.py:60
  21.1 1.2 %collective-permute-done.3.refs_1_ = bf16[4,5,128,128]{3,2,1,0:T(8,128)(2,1)S(1)} collective-permute-done((bf16[4,5,128,128]{3,2,1,0:T(8,128)(2,1)S(1)}, bf16[4,5,128,128]{3,2,1,0:T(8,128)(2,1)S(1)}, u32[]{:S(2)}, u32[]{:S(2)}) %collective-permute-start.3) | collective-permute-done | bytes 655392 | tf_op jit(solution)/shard_map/ppermute | solution.py:18
  22.4 1.6 %collective-permute-start.4 = (bf16[5,128,128]{2,1,0:T(8,128)(2,1)S(1)}, bf16[5,128,128]{2,1,0:T(8,128)(2,1)S(1)}, u32[]{:S(2)}, u32[]{:S(2)}) collective-permute-start(bf16[5,128,128]{2,1,0:T(8,128)(2,1)S(1)} %get-tuple-element.42), channel_id=1, source_target_pairs={{0,2},{1,3},{2,0},{3,1},{4,6},{5,7},{6,4},{7,5},{8,10},{9,11},{10,... | collective-permute-start | bytes 491528 | tf_op jit(solution)/shard_map/ppermute | solution.py:18
  24.0 1.5 %collective-permute-start.5 = (bf16[5,128,128]{2,1,0:T(8,128)(2,1)S(1)}, bf16[5,128,128]{2,1,0:T(8,128)(2,1)S(1)}, u32[]{:S(2)}, u32[]{:S(2)}) collective-permute-start(bf16[5,128,128]{2,1,0:T(8,128)(2,1)S(1)} %get-tuple-element.43), channel_id=1, source_target_pairs={{0,4},{1,5},{2,6},{3,7},{4,0},{5,1},{6,2},{7,3},{8,12},{9,13},{10,... | collective-permute-start | bytes 491528 | tf_op jit(solution)/shard_map/ppermute | solution.py:18
  26.0 3.6 %collective-permute-done.4.refs_1_ = bf16[5,128,128]{2,1,0:T(8,128)(2,1)S(1)} collective-permute-done((bf16[5,128,128]{2,1,0:T(8,128)(2,1)S(1)}, bf16[5,128,128]{2,1,0:T(8,128)(2,1)S(1)}, u32[]{:S(2)}, u32[]{:S(2)}) %collective-permute-start.4) | collective-permute-done | bytes 163872 | tf_op jit(solution)/shard_map/ppermute | solution.py:18
  29.6 3.9 %collective-permute-done.5.refs_2_ = bf16[5,128,128]{2,1,0:T(8,128)(2,1)S(1)} collective-permute-done((bf16[5,128,128]{2,1,0:T(8,128)(2,1)S(1)}, bf16[5,128,128]{2,1,0:T(8,128)(2,1)S(1)}, u32[]{:S(2)}, u32[]{:S(2)}) %collective-permute-start.5) | collective-permute-done | bytes 163872 | tf_op jit(solution)/shard_map/ppermute | solution.py:18
  33.6 1.6 %collective-permute-start.10 = (bf16[5,128,128]{2,1,0:T(8,128)(2,1)S(1)}, bf16[5,128,128]{2,1,0:T(8,128)(2,1)S(1)}, u32[]{:S(2)}, u32[]{:S(2)}) collective-permute-start(bf16[5,128,128]{2,1,0:T(8,128)(2,1)S(1)} %shard_map.62.refs_1_), channel_id=1, source_target_pairs={{0,4},{1,5},{2,6},{3,7},{4,0},{5,1},{6,2},{7,3},{8,12},{9,13},{10,... | collective-permute-start | bytes 491528 | tf_op jit(solution)/shard_map/ppermute | solution.py:18
  35.2 1.2 %collective-permute-start.12 = (bf16[5,128,128]{2,1,0:T(8,128)(2,1)S(1)}, bf16[5,128,128]{2,1,0:T(8,128)(2,1)S(1)}, u32[]{:S(2)}, u32[]{:S(2)}) collective-permute-start(bf16[5,128,128]{2,1,0:T(8,128)(2,1)S(1)} %shard_map.62.refs_1_), channel_id=1, source_target_pairs={{0,6},{1,7},{2,4},{3,5},{4,2},{5,3},{6,0},{7,1},{8,14},{9,15},{10,... | collective-permute-start | bytes 491528 | tf_op jit(solution)/shard_map/ppermute | solution.py:18
  37.2 4.7 %collective-permute-done.10.refs_5_ = bf16[5,128,128]{2,1,0:T(8,128)(2,1)S(1)} collective-permute-done((bf16[5,128,128]{2,1,0:T(8,128)(2,1)S(1)}, bf16[5,128,128]{2,1,0:T(8,128)(2,1)S(1)}, u32[]{:S(2)}, u32[]{:S(2)}) %collective-permute-start.10) | collective-permute-done | bytes 163872 | tf_op jit(solution)/shard_map/ppermute | solution.py:18
  45.0 1.3 %shard_map.63 = (f32[512,128]{1,0:T(8,128)S(1)}, bf16[512,128]{1,0:T(8,128)(2,1)S(1)}, bf16[5,2,1024,256]{3,2,1,0:T(8,128)(2,1)S(1)}, bf16[5,2,1024,256]{3,2,1,0:T(8,128)(2,1)S(1)}) custom-call(f32[10,256]{1,0:T(8,128)S(1)} %fusion.refs_1_.refs_0_, bf16[5,128,128]{2,1,0:T(8,128)(2,1)S(1)} %shard_map.62.refs_1_, ...), custom_call_target="tpu_custom_call", output_to_operand_aliasing={{2}: (9, {}), {3}: (10, {})} | custom-call | tf_op jit(solution)/shard_map/pallas_call | solution.py:60
  46.3 1.5 %collective-permute-start.15 = (bf16[512,128]{1,0:T(8,128)(2,1)S(1)}, bf16[512,128]{1,0:T(8,128)(2,1)S(1)}, u32[]{:S(2)}, u32[]{:S(2)}) collective-permute-start(bf16[512,128]{1,0:T(8,128)(2,1)S(1)} %get-tuple-element.52), channel_id=1, source_target_pairs={{0,8},{8,0},{16,24},{24,16},{1,9},{9,1},{17,25},{25,17},{2,10},{10... | collective-permute-start | bytes 393224 | tf_op jit(solution)/shard_map/ppermute | solution.py:18
  47.8 1.3 %shard_map.64 = (f32[512,128]{1,0:T(8,128)S(1)}, bf16[512,128]{1,0:T(8,128)(2,1)S(1)}, bf16[5,2,1024,256]{3,2,1,0:T(8,128)(2,1)S(1)}, bf16[5,2,1024,256]{3,2,1,0:T(8,128)(2,1)S(1)}) custom-call(f32[10,256]{1,0:T(8,128)S(1)} %fusion.refs_1_.refs_0_, bf16[5,128,128]{2,1,0:T(8,128)(2,1)S(1)} %shard_map.62.refs_1_, ...), custom_call_target="tpu_custom_call", output_to_operand_aliasing={{2}: (9, {}), {3}: (10, {})} | custom-call | tf_op jit(solution)/shard_map/pallas_call | solution.py:60
  49.7 2.5 %collective-permute-done.15.refs_1_ = bf16[512,128]{1,0:T(8,128)(2,1)S(1)} collective-permute-done((bf16[512,128]{1,0:T(8,128)(2,1)S(1)}, bf16[512,128]{1,0:T(8,128)(2,1)S(1)}, u32[]{:S(2)}, u32[]{:S(2)}) %collective-permute-start.15) | collective-permute-done | bytes 131104 | tf_op jit(solution)/shard_map/ppermute | solution.py:18
  52.2 4.0 %collective-permute-start.16 = (bf16[512,128]{1,0:T(8,128)(2,1)S(1)}, bf16[512,128]{1,0:T(8,128)(2,1)S(1)}, u32[]{:S(2)}, u32[]{:S(2)}) collective-permute-start(bf16[512,128]{1,0:T(8,128)(2,1)S(1)} %shard_map.65), channel_id=1, source_target_pairs={{0,16},{8,24},{16,0},{24,8},{1,17},{9,25},{17,1},{25,9},{2,18},{10... | collective-permute-start | bytes 393224 | tf_op jit(solution)/shard_map/ppermute | solution.py:18
  56.2 5.2 %collective-permute-done.16.refs_3_ = bf16[512,128]{1,0:T(8,128)(2,1)S(1)} collective-permute-done((bf16[512,128]{1,0:T(8,128)(2,1)S(1)}, bf16[512,128]{1,0:T(8,128)(2,1)S(1)}, u32[]{:S(2)}, u32[]{:S(2)}) %collective-permute-start.16) | collective-permute-done | bytes 131104 | tf_op jit(solution)/shard_map/ppermute | solution.py:18
  61.7 2.0 %collective-permute-start.17 = (bf16[2,2,64,128]{3,2,1,0:T(8,128)(2,1)S(1)}, bf16[2,2,64,128]{3,2,1,0:T(8,128)(2,1)S(1)}, u32[]{:S(2)}, u32[]{:S(2)}) collective-permute-start(bf16[2,2,64,128]{3,2,1,0:T(8,128)(2,1)S(1)} %get-tuple-element.54), channel_id=1, source_target_pairs={{0,8},{8,0},{16,24},{24,16},{1,9},{9,1},{17,25},{25,17},{2,10},{10... | collective-permute-start | bytes 196616 | tf_op jit(solution)/shard_map/ppermute | solution.py:18
  63.7 4.3 %collective-permute-done.17.refs_0_.refs_1_ = bf16[2,2,64,128]{3,2,1,0:T(8,128)(2,1)S(1)} collective-permute-done((bf16[2,2,64,128]{3,2,1,0:T(8,128)(2,1)S(1)}, bf16[2,2,64,128]{3,2,1,0:T(8,128)(2,1)S(1)}, u32[]{:S(2)}, u32[]{:S(2)}) %collective-permute-start.17) | collective-permute-done | bytes 65568 | tf_op jit(solution)/shard_map/ppermute | solution.py:18
  69.3 2.8 %collective-permute-done.22.refs_6_ = bf16[2,64,128]{2,1,0:T(8,128)(2,1)S(1)} collective-permute-done((bf16[2,64,128]{2,1,0:T(8,128)(2,1)S(1)}, bf16[2,64,128]{2,1,0:T(8,128)(2,1)S(1)}, u32[]{:S(2)}, u32[]{:S(2)}) %collective-permute-start.22) | collective-permute-done | bytes 32800 | tf_op jit(solution)/shard_map/ppermute | solution.py:36
  72.1 1.8 %shard_map.68 = f32[4,2,64,128]{3,2,1,0:T(8,128)} custom-call(f32[4,2,64,128]{3,2,1,0:T(8,128)S(1)} %get-tuple-element.53.refs_0_, bf16[2,2,64,128]{3,2,1,0:T(8,128)(2,1)S(1)} %collective-permute-done.17.refs_0_.refs_1_, bf16[2,2,64,128]{3,2,1,0:T(8,128)(2,1)S(1)} %collective-permute-done.18.refs_1_.refs_2_, ...), custom_call_target="tpu_custom_call" | custom-call | tf_op jit(solution)/shard_map/pallas_call | solution.py:60
  (43 shorter events, 10.9 us)
Async XLA Ops:
  1.1 10.5 %collective-permute-start.1 = (bf16[128,512]{1,0:T(8,128)(2,1)S(1)}, bf16[128,512]{1,0:T(8,128)(2,1)S(1)}, u32[]{:S(2)}, u32[]{:S(2)}) collective-permute-start(bf16[128,512]{1,0:T(8,128)(2,1)S(1)} %shard_map.55.refs_0_.refs_1_), channel_id=1, source_target_pairs={{0,16},{8,24},{16,0},{24,8},{1,17},{9,25},{17,1},{25,9},{2,18},{10... | collective-permute-start | bytes 393224 | tf_op jit(solution)/shard_map/ppermute | solution.py:18
  5.2 12.9 %collective-permute-start = (bf16[128,512]{1,0:T(8,128)(2,1)S(1)}, bf16[128,512]{1,0:T(8,128)(2,1)S(1)}, u32[]{:S(2)}, u32[]{:S(2)}) collective-permute-start(bf16[128,512]{1,0:T(8,128)(2,1)S(1)} %shard_map.55.refs_0_.refs_1_), channel_id=1, source_target_pairs={{0,8},{8,0},{16,24},{24,16},{1,9},{9,1},{17,25},{25,17},{2,10},{10... | collective-permute-start | bytes 393224 | tf_op jit(solution)/shard_map/ppermute | solution.py:18
  11.6 7.0 %collective-permute-start.2 = (bf16[128,512]{1,0:T(8,128)(2,1)S(1)}, bf16[128,512]{1,0:T(8,128)(2,1)S(1)}, u32[]{:S(2)}, u32[]{:S(2)}) collective-permute-start(bf16[128,512]{1,0:T(8,128)(2,1)S(1)} %collective-permute-done.1.refs_2_), channel_id=1, source_target_pairs={{0,8},{8,0},{16,24},{24,16},{1,9},{9,1},{17,25},{25,17},{2,10},{10... | collective-permute-start | bytes 393224 | tf_op jit(solution)/shard_map/ppermute | solution.py:18
  20.1 2.2 %collective-permute-start.3 = (bf16[4,5,128,128]{3,2,1,0:T(8,128)(2,1)S(1)}, bf16[4,5,128,128]{3,2,1,0:T(8,128)(2,1)S(1)}, u32[]{:S(2)}, u32[]{:S(2)}) collective-permute-start(bf16[4,5,128,128]{3,2,1,0:T(8,128)(2,1)S(1)} %get-tuple-element.39), channel_id=1, source_target_pairs={{0,1},{1,0},{2,3},{3,2},{4,5},{5,4},{6,7},{7,6},{8,9},{9,8},{10,11... | collective-permute-start | bytes 1966088 | tf_op jit(solution)/shard_map/ppermute | solution.py:18
  22.4 7.1 %collective-permute-start.4 = (bf16[5,128,128]{2,1,0:T(8,128)(2,1)S(1)}, bf16[5,128,128]{2,1,0:T(8,128)(2,1)S(1)}, u32[]{:S(2)}, u32[]{:S(2)}) collective-permute-start(bf16[5,128,128]{2,1,0:T(8,128)(2,1)S(1)} %get-tuple-element.42), channel_id=1, source_target_pairs={{0,2},{1,3},{2,0},{3,1},{4,6},{5,7},{6,4},{7,5},{8,10},{9,11},{10,... | collective-permute-start | bytes 491528 | tf_op jit(solution)/shard_map/ppermute | solution.py:18
  24.0 9.5 %collective-permute-start.5 = (bf16[5,128,128]{2,1,0:T(8,128)(2,1)S(1)}, bf16[5,128,128]{2,1,0:T(8,128)(2,1)S(1)}, u32[]{:S(2)}, u32[]{:S(2)}) collective-permute-start(bf16[5,128,128]{2,1,0:T(8,128)(2,1)S(1)} %get-tuple-element.43), channel_id=1, source_target_pairs={{0,4},{1,5},{2,6},{3,7},{4,0},{5,1},{6,2},{7,3},{8,12},{9,13},{10,... | collective-permute-start | bytes 491528 | tf_op jit(solution)/shard_map/ppermute | solution.py:18
  25.5 8.0 %collective-permute-start.6 = (bf16[5,128,128]{2,1,0:T(8,128)(2,1)S(1)}, bf16[5,128,128]{2,1,0:T(8,128)(2,1)S(1)}, u32[]{:S(2)}, u32[]{:S(2)}) collective-permute-start(bf16[5,128,128]{2,1,0:T(8,128)(2,1)S(1)} %get-tuple-element.44), channel_id=1, source_target_pairs={{0,6},{1,7},{2,4},{3,5},{4,2},{5,3},{6,0},{7,1},{8,14},{9,15},{10,... | collective-permute-start | bytes 491528 | tf_op jit(solution)/shard_map/ppermute | solution.py:18
  33.6 8.2 %collective-permute-start.10 = (bf16[5,128,128]{2,1,0:T(8,128)(2,1)S(1)}, bf16[5,128,128]{2,1,0:T(8,128)(2,1)S(1)}, u32[]{:S(2)}, u32[]{:S(2)}) collective-permute-start(bf16[5,128,128]{2,1,0:T(8,128)(2,1)S(1)} %shard_map.62.refs_1_), channel_id=1, source_target_pairs={{0,4},{1,5},{2,6},{3,7},{4,0},{5,1},{6,2},{7,3},{8,12},{9,13},{10,... | collective-permute-start | bytes 491528 | tf_op jit(solution)/shard_map/ppermute | solution.py:18
  35.2 7.5 %collective-permute-start.12 = (bf16[5,128,128]{2,1,0:T(8,128)(2,1)S(1)}, bf16[5,128,128]{2,1,0:T(8,128)(2,1)S(1)}, u32[]{:S(2)}, u32[]{:S(2)}) collective-permute-start(bf16[5,128,128]{2,1,0:T(8,128)(2,1)S(1)} %shard_map.62.refs_1_), channel_id=1, source_target_pairs={{0,6},{1,7},{2,4},{3,5},{4,2},{5,3},{6,0},{7,1},{8,14},{9,15},{10,... | collective-permute-start | bytes 491528 | tf_op jit(solution)/shard_map/ppermute | solution.py:18
  36.4 7.2 %collective-permute-start.8 = (bf16[5,128,128]{2,1,0:T(8,128)(2,1)S(1)}, bf16[5,128,128]{2,1,0:T(8,128)(2,1)S(1)}, u32[]{:S(2)}, u32[]{:S(2)}) collective-permute-start(bf16[5,128,128]{2,1,0:T(8,128)(2,1)S(1)} %shard_map.62.refs_1_), channel_id=1, source_target_pairs={{0,2},{1,3},{2,0},{3,1},{4,6},{5,7},{6,4},{7,5},{8,10},{9,11},{10,... | collective-permute-start | bytes 491528 | tf_op jit(solution)/shard_map/ppermute | solution.py:18
  37.2 6.4 %collective-permute-start.7 = (bf16[5,128,128]{2,1,0:T(8,128)(2,1)S(1)}, bf16[5,128,128]{2,1,0:T(8,128)(2,1)S(1)}, u32[]{:S(2)}, u32[]{:S(2)}) collective-permute-start(bf16[5,128,128]{2,1,0:T(8,128)(2,1)S(1)} %shard_map.62.refs_1_), channel_id=1, source_target_pairs={{0,1},{1,0},{2,3},{3,2},{4,5},{5,4},{6,7},{7,6},{8,9},{9,8},{10,11... | collective-permute-start | bytes 491528 | tf_op jit(solution)/shard_map/ppermute | solution.py:18
  41.8 1.8 %collective-permute-start.11 = (bf16[5,128,128]{2,1,0:T(8,128)(2,1)S(1)}, bf16[5,128,128]{2,1,0:T(8,128)(2,1)S(1)}, u32[]{:S(2)}, u32[]{:S(2)}) collective-permute-start(bf16[5,128,128]{2,1,0:T(8,128)(2,1)S(1)} %collective-permute-done.10.refs_5_), channel_id=1, source_target_pairs={{0,1},{1,0},{2,3},{3,2},{4,5},{5,4},{6,7},{7,6},{8,9},{9,8},{10,11... | collective-permute-start | bytes 491528 | tf_op jit(solution)/shard_map/ppermute | solution.py:18
  42.7 1.4 %collective-permute-start.13 = (bf16[5,128,128]{2,1,0:T(8,128)(2,1)S(1)}, bf16[5,128,128]{2,1,0:T(8,128)(2,1)S(1)}, u32[]{:S(2)}, u32[]{:S(2)}) collective-permute-start(bf16[5,128,128]{2,1,0:T(8,128)(2,1)S(1)} %collective-permute-done.12.refs_7_), channel_id=1, source_target_pairs={{0,1},{1,0},{2,3},{3,2},{4,5},{5,4},{6,7},{7,6},{8,9},{9,8},{10,11... | collective-permute-start | bytes 491528 | tf_op jit(solution)/shard_map/ppermute | solution.py:18
  43.6 1.4 %collective-permute-start.9 = (bf16[5,128,128]{2,1,0:T(8,128)(2,1)S(1)}, bf16[5,128,128]{2,1,0:T(8,128)(2,1)S(1)}, u32[]{:S(2)}, u32[]{:S(2)}) collective-permute-start(bf16[5,128,128]{2,1,0:T(8,128)(2,1)S(1)} %collective-permute-done.8.refs_3_), channel_id=1, source_target_pairs={{0,1},{1,0},{2,3},{3,2},{4,5},{5,4},{6,7},{7,6},{8,9},{9,8},{10,11... | collective-permute-start | bytes 491528 | tf_op jit(solution)/shard_map/ppermute | solution.py:18
  46.3 5.9 %collective-permute-start.15 = (bf16[512,128]{1,0:T(8,128)(2,1)S(1)}, bf16[512,128]{1,0:T(8,128)(2,1)S(1)}, u32[]{:S(2)}, u32[]{:S(2)}) collective-permute-start(bf16[512,128]{1,0:T(8,128)(2,1)S(1)} %get-tuple-element.52), channel_id=1, source_target_pairs={{0,8},{8,0},{16,24},{24,16},{1,9},{9,1},{17,25},{25,17},{2,10},{10... | collective-permute-start | bytes 393224 | tf_op jit(solution)/shard_map/ppermute | solution.py:18
  47.8 13.6 %copy-start.1 = (f32[4,2,64,128]{3,2,1,0:T(8,128)S(1)}, f32[4,2,64,128]{3,2,1,0:T(8,128)}, u32[]{:S(2)}) copy-start(f32[4,2,64,128]{3,2,1,0:T(8,128)} %refs_0_.3) | copy-start | bytes 786436
  49.0 7.1 %collective-permute-start.14 = (bf16[512,128]{1,0:T(8,128)(2,1)S(1)}, bf16[512,128]{1,0:T(8,128)(2,1)S(1)}, u32[]{:S(2)}, u32[]{:S(2)}) collective-permute-start(bf16[512,128]{1,0:T(8,128)(2,1)S(1)} %get-tuple-element.50), channel_id=1, source_target_pairs={{0,8},{8,0},{16,24},{24,16},{1,9},{9,1},{17,25},{25,17},{2,10},{10... | collective-permute-start | bytes 393224 | tf_op jit(solution)/shard_map/ppermute | solution.py:18
  52.2 9.2 %collective-permute-start.16 = (bf16[512,128]{1,0:T(8,128)(2,1)S(1)}, bf16[512,128]{1,0:T(8,128)(2,1)S(1)}, u32[]{:S(2)}, u32[]{:S(2)}) collective-permute-start(bf16[512,128]{1,0:T(8,128)(2,1)S(1)} %shard_map.65), channel_id=1, source_target_pairs={{0,16},{8,24},{16,0},{24,8},{1,17},{9,25},{17,1},{25,9},{2,18},{10... | collective-permute-start | bytes 393224 | tf_op jit(solution)/shard_map/ppermute | solution.py:18
  61.5 10.6 %collective-permute-start.19 = (bf16[4,2,64,128]{3,2,1,0:T(8,128)(2,1)S(1)}, bf16[4,2,64,128]{3,2,1,0:T(8,128)(2,1)S(1)}, u32[]{:S(2)}, u32[]{:S(2)}) collective-permute-start(bf16[4,2,64,128]{3,2,1,0:T(8,128)(2,1)S(1)} %get-tuple-element.56), channel_id=1, source_target_pairs={{0,1},{1,0},{2,3},{3,2},{4,5},{5,4},{6,7},{7,6},{8,9},{9,8},{10,11... | collective-permute-start | bytes 393224 | tf_op jit(solution)/shard_map/ppermute | solution.py:18
  61.6 10.5 %collective-permute-start.20 = (bf16[4,2,64,128]{3,2,1,0:T(8,128)(2,1)S(1)}, bf16[4,2,64,128]{3,2,1,0:T(8,128)(2,1)S(1)}, u32[]{:S(2)}, u32[]{:S(2)}) collective-permute-start(bf16[4,2,64,128]{3,2,1,0:T(8,128)(2,1)S(1)} %get-tuple-element.56), channel_id=1, source_target_pairs={{0,8},{1,2},{2,1},{3,4},{4,3},{5,6},{6,5},{7,15},{8,0},{9,10},{10,... | collective-permute-start | bytes 393224 | tf_op jit(solution)/shard_map/ppermute | solution.py:36
  61.7 6.4 %collective-permute-start.17 = (bf16[2,2,64,128]{3,2,1,0:T(8,128)(2,1)S(1)}, bf16[2,2,64,128]{3,2,1,0:T(8,128)(2,1)S(1)}, u32[]{:S(2)}, u32[]{:S(2)}) collective-permute-start(bf16[2,2,64,128]{3,2,1,0:T(8,128)(2,1)S(1)} %get-tuple-element.54), channel_id=1, source_target_pairs={{0,8},{8,0},{16,24},{24,16},{1,9},{9,1},{17,25},{25,17},{2,10},{10... | collective-permute-start | bytes 196616 | tf_op jit(solution)/shard_map/ppermute | solution.py:18
  63.7 4.3 %collective-permute-start.18 = (bf16[2,2,64,128]{3,2,1,0:T(8,128)(2,1)S(1)}, bf16[2,2,64,128]{3,2,1,0:T(8,128)(2,1)S(1)}, u32[]{:S(2)}, u32[]{:S(2)}) collective-permute-start(bf16[2,2,64,128]{3,2,1,0:T(8,128)(2,1)S(1)} %get-tuple-element.55), channel_id=1, source_target_pairs={{0,1},{1,0},{2,3},{3,2},{4,5},{5,4},{6,7},{7,6},{8,16},{9,17},{10,... | collective-permute-start | bytes 196616 | tf_op jit(solution)/shard_map/ppermute | solution.py:36
  68.0 1.3 %collective-permute-start.21 = (bf16[2,64,128]{2,1,0:T(8,128)(2,1)S(1)}, bf16[2,64,128]{2,1,0:T(8,128)(2,1)S(1)}, u32[]{:S(2)}, u32[]{:S(2)}) collective-permute-start(bf16[2,64,128]{2,1,0:T(8,128)(2,1)S(1)} %get-tuple-element.57), channel_id=1, source_target_pairs={{0,1},{1,0},{2,3},{3,2},{4,5},{5,4},{6,7},{7,6},{8,9},{9,8},{10,11... | collective-permute-start | bytes 98312 | tf_op jit(solution)/shard_map/ppermute | solution.py:18
  68.1 4.0 %collective-permute-start.22 = (bf16[2,64,128]{2,1,0:T(8,128)(2,1)S(1)}, bf16[2,64,128]{2,1,0:T(8,128)(2,1)S(1)}, u32[]{:S(2)}, u32[]{:S(2)}) collective-permute-start(bf16[2,64,128]{2,1,0:T(8,128)(2,1)S(1)} %get-tuple-element.58), channel_id=1, source_target_pairs={{0,8},{1,2},{2,1},{3,4},{4,3},{5,6},{6,5},{7,15},{8,0},{9,10},{10,... | collective-permute-start | bytes 98312 | tf_op jit(solution)/shard_map/ppermute | solution.py:36
  (1 other events, 0.9 us)

commit v5 on v4

--- a/solution.py
+++ b/solution.py
@@ -113,51 +113,52 @@
         near_ref[i] = (value * mask_ref[pl.ds(i * col_tiles + tile, 1)]).astype(BF16)
 
 
-def half_rows(u_ref, coef_ref, i, core):
+def half_rows(u_ref, coef_ref, i, low, core):
     total = None
     for j in range(u_ref.shape[1]):
-        rows = u_ref[i, j, :, core]
+        rows = u_ref[low + i, j, :, core]
         rows = rows.reshape(rows.shape[0] * rows.shape[1], rows.shape[2])
         term = dot_nt(rows, coef_ref[i, j])
         total = term if total is None else total + term
     return total.reshape(u_ref.shape[2], u_ref.shape[4], total.shape[1])
 
 
-def forward_kernel(mask_ref, near_ref, *refs):
+def forward_kernel(low, mask_ref, near_ref, *refs):
     pieces, (u_ref, v_ref, cross_ref, coef_ref, held) = refs[:-5], refs[-5:]
-    row_tiles, col_tiles, chips = u_ref.shape[:3]
+    col_tiles, chips = u_ref.shape[1:3]
     per_tile = len(pieces) // (col_tiles - 1)
     me_row, me_col = lax.axis_index("row"), lax.axis_index("col")
     own_tile = me_row // per_tile
     for n, piece in enumerate(pieces, per_tile):
         held[me_row ^ n] = piece[...]
-    for i in range(row_tiles):
-        coef_ref[i, own_tile] = near_ref[i]
+    for i in range(coef_ref.shape[0]):
+        coef_ref[i, own_tile] = near_ref[low + i]
     for n in range(1, col_tiles):
         tile = own_tile ^ n
         lhs = jnp.concatenate([held[tile * per_tile + p] for p in range(per_tile)], axis=1)
-        for i in range(row_tiles):
-            value = jnp.dot(lhs, v_ref[i, tile], preferred_element_type=F32)
-            coef_ref[i, tile] = (value * mask_ref[pl.ds(i * col_tiles + tile, 1)]).astype(BF16)
+        for i in range(coef_ref.shape[0]):
+            value = jnp.dot(lhs, v_ref[low + i, tile], preferred_element_type=F32)
+            value = value * mask_ref[pl.ds((low + i) * col_tiles + tile, 1)]
+            coef_ref[i, tile] = value.astype(BF16)
     chip, core = me_col // 2, me_col % 2
-    for i in range(row_tiles):
-        value = half_rows(u_ref, coef_ref, i, 1 - core)
+    for i in range(coef_ref.shape[0]):
+        value = half_rows(u_ref, coef_ref, i, low, 1 - core)
         for q in range(chips):
             cross_ref[chip ^ q, i] = value[q].astype(cross_ref.dtype)
 
 
-def own_kernel(coef_ref, u_ref, mine_ref):
+def own_kernel(low, coef_ref, u_ref, mine_ref):
     me_col = lax.axis_index("col")
     chip, core = me_col // 2, me_col % 2
-    for i in range(u_ref.shape[0]):
-        value = half_rows(u_ref, coef_ref, i, core)
+    for i in range(coef_ref.shape[0]):
+        value = half_rows(u_ref, coef_ref, i, low, core)
         for q in range(u_ref.shape[2]):
             mine_ref[chip ^ q, i] = value[q]
 
 
-def sum_kernel(mine_ref, crossed_ref, wanted_ref, own_ref, *send_refs):
+def sum_kernel(low, mine_ref, crossed_ref, wanted_ref, own_ref, *send_refs):
     value = mine_ref[0] + crossed_ref[0].astype(F32)
-    own_ref[...] = value - wanted_ref[...].astype(F32)
+    own_ref[...] = value - wanted_ref[pl.ds(low, own_ref.shape[0])].astype(F32)
     for q, send_ref in enumerate(send_refs, 1):
         send_ref[...] = (mine_ref[q] + crossed_ref[q].astype(F32)).astype(BF16)
 
@@ -171,38 +172,48 @@
         out_ref[i] = value.T.astype(BF16)
 
 
-def back_tile(held, mask_ref, u_ref, tile, i):
+def hold(held, pieces):
+    me_col = lax.axis_index("col")
+    for distance, piece in enumerate(pieces):
+        held[me_col ^ distance] = piece[...]
+
+
+def back_tile(held, mask_ref, u_ref, tile, i, low):
     count, col_tiles = held.shape[0], u_ref.shape[1]
     lhs = jnp.concatenate([held[p, i] for p in range(count)], axis=1)
-    value = jnp.dot(lhs, u_ref[i, tile], preferred_element_type=F32)
-    return (value * mask_ref[pl.ds(i * col_tiles + tile, 1)]).astype(BF16)
-
-
-def gradient_piece(v_ref, back_ref, tile, inside, brick):
-    total = None
-    for i in range(v_ref.shape[0]):
-        term = dot_nt(v_ref[i, tile, pl.ds(inside, brick)], back_ref[i])
-        total = term if total is None else total + term
-    return total
-
-
-def adjoint_kernel(count, first, mask_ref, *refs):
+    value = jnp.dot(lhs, u_ref[low + i, tile], preferred_element_type=F32)
+    return (value * mask_ref[pl.ds((low + i) * col_tiles + tile, 1)]).astype(BF16)
+
+
+def back_kernel(mask_ref, *refs):
+    pieces, (u_ref, back_ref, held) = refs[:-3], refs[-3:]
+    hold(held, pieces)
+    for i in range(back_ref.shape[0]):
+        for tile in range(u_ref.shape[1]):
+            back_ref[i, tile] = back_tile(held, mask_ref, u_ref, tile, i, 0)
+
+
+def adjoint_kernel(count, first, mask_ref, early_ref, *refs):
     pieces, (u_ref, v_ref), rest = refs[:count], refs[count : count + 2], refs[count + 2 :]
     outs, (held, back_ref) = rest[:-2], rest[-2:]
     row_tiles, tile_len = u_ref.shape[0], u_ref.shape[2]
+    low = early_ref.shape[0]
     brick = outs[0].shape[0]
     per_tile = tile_len // brick
-    me_row, me_col = lax.axis_index("row"), lax.axis_index("col")
-    for distance in range(count):
-        held[me_col ^ distance] = pieces[distance][...]
+    me_row = lax.axis_index("row")
+    hold(held, pieces)
     for n in range(len(outs) // per_tile):
         tile = (me_row // per_tile) ^ (first + n)
-        for i in range(row_tiles):
-            back_ref[i] = back_tile(held, mask_ref, u_ref, tile, i)
+        for i in range(row_tiles - low):
+            back_ref[i] = back_tile(held, mask_ref, u_ref, tile, i, low)
         for p in reversed(range(per_tile)):
             inside = pl.multiple_of(((me_row % per_tile) ^ p) * brick, brick)
+            value = None
+            for i in range(row_tiles):
+                back = early_ref[i, tile] if i < low else back_ref[i - low]
+                term = dot_nt(v_ref[i, tile, pl.ds(inside, brick)], back)
+                value = term if value is None else value + term
             out_ref = outs[n * per_tile + p]
-            value = gradient_piece(v_ref, back_ref, tile, inside, brick)
             out_ref[...] = value.astype(out_ref.dtype)
 
 
@@ -326,8 +337,9 @@
     v_factors, wanted = load(v_factors, samples, (own_x, mask))
     u_factors, _ = load(u_factors, samples, (own_x, mask))
 
-    u_parts = u_factors.reshape(row_tiles, col_tiles, chips, 2, part_len, rank_max)
-    half = (chips, row_tiles, part_len, frames)
+    u_factors = u_factors.reshape(row_tiles, col_tiles, chips, 2, part_len, rank_max)
+    split = (row_tiles + 1) // 2
+    groups = [(0, split), (split, row_tiles - split)]
     near, v_factors = call(
         near_kernel,
         (mask, *pieces[:per_tile], v_factors),
@@ -335,35 +347,60 @@
         [pltpu.VMEM((per_tile, frames, brick), BF16)],
         through=1,
     )
-    cross, coef, u_parts, v_factors = call(
-        forward_kernel,
-        (mask, near, *pieces[per_tile:], u_parts, v_factors),
-        [(half, BF16), ((row_tiles, col_tiles, frames, rank_max), BF16)],
-        [pltpu.VMEM((rows, frames, brick), BF16)],
-        through=2,
-    )
-    crossed = swap(cross, "col", 1)
-    mine, u_parts = call(own_kernel, (coef, u_parts), [(half, F32)], through=1)
-    u_factors = u_parts.reshape(u_factors.shape)
-    part = (row_tiles, part_len, frames)
-    own, *sends = call(
-        sum_kernel, (mine, crossed, wanted), [(part, F32)] + [(part, BF16)] * (chips - 1)
-    )
-    received = [swap(value, "col", 2 * q) for q, value in enumerate(sends, 1)]
-    (resid,) = call(resid_kernel, (own, *received), [((row_tiles, frames, part_len), BF16)])
-    parts = {}
-    for q in range(chips):
-        parts[2 * q] = swap(resid, "col", 2 * q) if q else resid
-        parts[2 * q + 1] = swap(parts[2 * q], "col", 1)
+    crossed, mine = [], []
+    for low, size in groups:
+        half = (chips, size, part_len, frames)
+        cross, coef, u_factors, v_factors = call(
+            functools.partial(forward_kernel, low),
+            (mask, near, *pieces[per_tile:], u_factors, v_factors),
+            [(half, BF16), ((size, col_tiles, frames, rank_max), BF16)],
+            [pltpu.VMEM((rows, frames, brick), BF16)],
+            through=2,
+        )
+        crossed.append(swap(cross, "col", 1))
+        value, u_factors = call(
+            functools.partial(own_kernel, low), (coef, u_factors), [(half, F32)], through=1
+        )
+        mine.append(value)
+    u_factors = u_factors.reshape(row_tiles, col_tiles, tile_len, rank_max)
+    own, received = [], []
+    for n, (low, size) in enumerate(groups):
+        part = (size, part_len, frames)
+        value, *sends = call(
+            functools.partial(sum_kernel, low),
+            (mine[n], crossed[n], wanted),
+            [(part, F32)] + [(part, BF16)] * (chips - 1),
+        )
+        own.append(value)
+        received.append([])
+        for q, value in enumerate(sends, 1):
+            received[n].append(swap(value, "col", 2 * q))
+    parts = []
+    for n, (low, size) in enumerate(groups):
+        (resid,) = call(resid_kernel, (own[n], *received[n]), [((size, frames, part_len), BF16)])
+        pieces = {}
+        for q in range(chips):
+            pieces[2 * q] = swap(resid, "col", 2 * q) if q else resid
+            pieces[2 * q + 1] = swap(pieces[2 * q], "col", 1)
+        parts.append([pieces[d] for d in range(cols)])
+    size = groups[0][1]
+    early, u_factors = call(
+        back_kernel,
+        (mask, *parts[0], u_factors),
+        [((size, col_tiles, frames, rank_max), BF16)],
+        [pltpu.VMEM((cols, size, frames, part_len), BF16)],
+        through=1,
+    )
 
     def adjoint(distances, kinds, u_factors, v_factors):
+        size = groups[1][1]
         return call(
             functools.partial(adjoint_kernel, cols, distances[0] // per_tile),
-            (mask, *[parts[d] for d in range(cols)], u_factors, v_factors),
+            (mask, early, *parts[1], u_factors, v_factors),
             [((brick, frames), kind) for kind in kinds],
             [
-                pltpu.VMEM((cols, row_tiles, frames, part_len), BF16),
-                pltpu.VMEM((row_tiles, frames, rank_max), BF16),
+                pltpu.VMEM((cols, size, frames, part_len), BF16),
+                pltpu.VMEM((size, frames, rank_max), BF16),
             ],
             through=2,
         )

time: 74.1 us -> 76.6 us (1.034)
  the two profiles are of different devices: /device:TPU:0 before, /device:TPU:19 now
where the time goes in v5:
time: 76.6 us; the launch traced here: 75.2 us
  starting transfers between devices  37.2 us (49%)
  waiting for transfers between devices  21.7 us (28%)
  Pallas kernels  14.2 us (19%)
  local copies, waits for them, and re-layouts  1.8 us (2%)
    ppermute x31, starting transfers between devices, swap(): return lax.ppermute(value, axis, [(i, i ^ distance) for i in range(count)])  32.4 us
    ppermute x31, waiting for transfers between devices, swap(): return lax.ppermute(value, axis, [(i, i ^ distance) for i in range(count)])  17.2 us
    pallas_call x17, Pallas kernels, call(): pl.pallas_call(run, out_shape=[kept(shape, kind) for shape, kind in outs]...  8.46 us
    pallas_call x2, Pallas kernels, load(): pl.pallas_call(load_kernel, out_shape=[pltpu.VMEM(factors.shape, factors....  5.75 us
    ppermute x3, starting transfers between devices, swap_odd(): return lax.ppermute(value, ('row', 'col'), pairs)  4.76 us
    ppermute x3, waiting for transfers between devices, swap_odd(): return lax.ppermute(value, ('row', 'col'), pairs)  4.54 us
    unnamed x5, local copies, waits for them, and re-layouts  1.72 us
  transfers between devices with their start and end apart: 34, of which 14 were waited for; matrix products, arithmetic and copies ran while one was open for 1% of the time, Pallas kernels for 13%

profile of v5, /device:TPU:19, one launch (start us, length us, event | category | flops | bytes accessed | tf_op | source)
XLA Modules:
  0.0 75.2 jit_solution(16547000476175265802)
XLA Ops:
  1.2 1.3 %collective-permute-start = (bf16[128,512]{1,0:T(8,128)(2,1)S(1)}, bf16[128,512]{1,0:T(8,128)(2,1)S(1)}, u32[]{:S(2)}, u32[]{:S(2)}) collective-permute-start(bf16[128,512]{1,0:T(8,128)(2,1)S(1)} %shard_map.55.refs_0_.refs_1_), channel_id=1, source_target_pairs={{0,8},{8,0},{16,24},{24,16},{1,9},{9,1},{17,25},{25,17},{2,10},{10... | collective-permute-start | bytes 393224 | tf_op jit(solution)/shard_map/ppermute | solution.py:18
  3.3 3.1 %collective-permute-done.1.refs_2_ = bf16[128,512]{1,0:T(8,128)(2,1)S(1)} collective-permute-done((bf16[128,512]{1,0:T(8,128)(2,1)S(1)}, bf16[128,512]{1,0:T(8,128)(2,1)S(1)}, u32[]{:S(2)}, u32[]{:S(2)}) %collective-permute-start.1) | collective-permute-done | bytes 131104 | tf_op jit(solution)/shard_map/ppermute | solution.py:18
  6.4 5.0 %collective-permute-start.2 = (bf16[128,512]{1,0:T(8,128)(2,1)S(1)}, bf16[128,512]{1,0:T(8,128)(2,1)S(1)}, u32[]{:S(2)}, u32[]{:S(2)}) collective-permute-start(bf16[128,512]{1,0:T(8,128)(2,1)S(1)} %collective-permute-done.1.refs_2_), channel_id=1, source_target_pairs={{0,8},{8,0},{16,24},{24,16},{1,9},{9,1},{17,25},{25,17},{2,10},{10... | collective-permute-start | bytes 393224 | tf_op jit(solution)/shard_map/ppermute | solution.py:18
  11.5 2.5 %shard_map.56 = (bf16[5,2,1024,256]{3,2,1,0:T(8,128)(2,1)S(1)}, bf16[5,128,128]{2,1,0:T(8,128)(2,1)S(1)}) custom-call(bf16[5,2,1024,256]{3,2,1,0:T(8,128)(2,1)} %factor_ref.2, bf16[5,8,128,128]{3,2,1,0:T(8,128)(2,1)} %bitcast.5, bf16[128,512]{1,0:T(8,128)(2,1)S(1)} %shard_map.55.refs_0_.refs_1_, f32[10,256]{1,0:T(8,128)S(1)} %fusion.refs_1_.refs_0_), custom_call_target="tpu_custom_call" | custom-call | tf_op jit(solution)/shard_map/pallas_call | solution.py:85
  14.1 3.2 %shard_map.58 = (bf16[5,2,1024,256]{3,2,1,0:T(8,128)(2,1)S(1)}, bf16[5,128,128]{2,1,0:T(8,128)(2,1)}) custom-call(bf16[5,2,1024,256]{3,2,1,0:T(8,128)(2,1)} %factor_ref.3, bf16[5,8,128,128]{3,2,1,0:T(8,128)(2,1)} %bitcast.6, bf16[128,512]{1,0:T(8,128)(2,1)S(1)} %shard_map.55.refs_0_.refs_1_, f32[10,256]{1,0:T(8,128)S(1)} %fusion.refs_1_.refs_0_), custom_call_target="tpu_custom_call" | custom-call | tf_op jit(solution)/shard_map/pallas_call | solution.py:85
  21.7 1.2 %collective-permute-start.5 = (bf16[3,128,128]{2,1,0:T(8,128)(2,1)S(1)}, bf16[3,128,128]{2,1,0:T(8,128)(2,1)S(1)}, u32[]{:S(2)}, u32[]{:S(2)}) collective-permute-start(bf16[3,128,128]{2,1,0:T(8,128)(2,1)S(1)} %get-tuple-element.55), channel_id=1, source_target_pairs={{0,4},{1,5},{2,6},{3,7},{4,0},{5,1},{6,2},{7,3},{8,12},{9,13},{10,... | collective-permute-start | bytes 294920 | tf_op jit(solution)/shard_map/ppermute | solution.py:18
  24.9 1.2 %collective-permute-start.16 = (bf16[2,128,128]{2,1,0:T(8,128)(2,1)S(1)}, bf16[2,128,128]{2,1,0:T(8,128)(2,1)S(1)}, u32[]{:S(2)}, u32[]{:S(2)}) collective-permute-start(bf16[2,128,128]{2,1,0:T(8,128)(2,1)S(1)} %get-tuple-element.67), channel_id=1, source_target_pairs={{0,4},{1,5},{2,6},{3,7},{4,0},{5,1},{6,2},{7,3},{8,12},{9,13},{10,... | collective-permute-start | bytes 196616 | tf_op jit(solution)/shard_map/ppermute | solution.py:18
  28.7 1.2 %collective-permute-start.10 = (bf16[3,128,128]{2,1,0:T(8,128)(2,1)S(1)}, bf16[3,128,128]{2,1,0:T(8,128)(2,1)S(1)}, u32[]{:S(2)}, u32[]{:S(2)}) collective-permute-start(bf16[3,128,128]{2,1,0:T(8,128)(2,1)S(1)} %shard_map.62.refs_1_), channel_id=1, source_target_pairs={{0,4},{1,5},{2,6},{3,7},{4,0},{5,1},{6,2},{7,3},{8,12},{9,13},{10,... | collective-permute-start | bytes 294920 | tf_op jit(solution)/shard_map/ppermute | solution.py:18
  31.1 3.4 %collective-permute-start.23 = (bf16[2,128,128]{2,1,0:T(8,128)(2,1)S(1)}, bf16[2,128,128]{2,1,0:T(8,128)(2,1)S(1)}, u32[]{:S(2)}, u32[]{:S(2)}) collective-permute-start(bf16[2,128,128]{2,1,0:T(8,128)(2,1)S(1)} %shard_map.67.refs_2_), channel_id=1, source_target_pairs={{0,6},{1,7},{2,4},{3,5},{4,2},{5,3},{6,0},{7,1},{8,14},{9,15},{10,... | collective-permute-start | bytes 196616 | tf_op jit(solution)/shard_map/ppermute | solution.py:18
  34.9 1.5 %collective-permute-done.23.refs_8_ = bf16[2,128,128]{2,1,0:T(8,128)(2,1)S(1)} collective-permute-done((bf16[2,128,128]{2,1,0:T(8,128)(2,1)S(1)}, bf16[2,128,128]{2,1,0:T(8,128)(2,1)S(1)}, u32[]{:S(2)}, u32[]{:S(2)}) %collective-permute-start.23) | collective-permute-done | bytes 65568 | tf_op jit(solution)/shard_map/ppermute | solution.py:18
  36.3 3.0 %collective-permute-start.7 = (bf16[3,128,128]{2,1,0:T(8,128)(2,1)S(1)}, bf16[3,128,128]{2,1,0:T(8,128)(2,1)S(1)}, u32[]{:S(2)}, u32[]{:S(2)}) collective-permute-start(bf16[3,128,128]{2,1,0:T(8,128)(2,1)S(1)} %shard_map.62.refs_1_), channel_id=1, source_target_pairs={{0,1},{1,0},{2,3},{3,2},{4,5},{5,4},{6,7},{7,6},{8,9},{9,8},{10,11... | collective-permute-start | bytes 294920 | tf_op jit(solution)/shard_map/ppermute | solution.py:18
  40.5 1.7 %collective-permute-start.9 = (bf16[3,128,128]{2,1,0:T(8,128)(2,1)S(1)}, bf16[3,128,128]{2,1,0:T(8,128)(2,1)S(1)}, u32[]{:S(2)}, u32[]{:S(2)}) collective-permute-start(bf16[3,128,128]{2,1,0:T(8,128)(2,1)S(1)} %collective-permute-done.8.refs_3_), channel_id=1, source_target_pairs={{0,1},{1,0},{2,3},{3,2},{4,5},{5,4},{6,7},{7,6},{8,9},{9,8},{10,11... | collective-permute-start | bytes 294920 | tf_op jit(solution)/shard_map/ppermute | solution.py:18
  42.9 2.0 %collective-permute-start.18 = (bf16[2,128,128]{2,1,0:T(8,128)(2,1)S(1)}, bf16[2,128,128]{2,1,0:T(8,128)(2,1)S(1)}, u32[]{:S(2)}, u32[]{:S(2)}) collective-permute-start(bf16[2,128,128]{2,1,0:T(8,128)(2,1)S(1)} %shard_map.67.refs_2_), channel_id=1, source_target_pairs={{0,1},{1,0},{2,3},{3,2},{4,5},{5,4},{6,7},{7,6},{8,9},{9,8},{10,11... | collective-permute-start | bytes 196616 | tf_op jit(solution)/shard_map/ppermute | solution.py:18
  48.8 1.5 %collective-permute-start.25 = (bf16[512,128]{1,0:T(8,128)(2,1)S(1)}, bf16[512,128]{1,0:T(8,128)(2,1)S(1)}, u32[]{:S(2)}, u32[]{:S(2)}) collective-permute-start(bf16[512,128]{1,0:T(8,128)(2,1)S(1)} %get-tuple-element.74), channel_id=1, source_target_pairs={{0,8},{8,0},{16,24},{24,16},{1,9},{9,1},{17,25},{25,17},{2,10},{10... | collective-permute-start | bytes 393224 | tf_op jit(solution)/shard_map/ppermute | solution.py:18
  50.3 2.4 %collective-permute-done.26.refs_1_ = bf16[512,128]{1,0:T(8,128)(2,1)S(1)} collective-permute-done((bf16[512,128]{1,0:T(8,128)(2,1)S(1)}, bf16[512,128]{1,0:T(8,128)(2,1)S(1)}, u32[]{:S(2)}, u32[]{:S(2)}) %collective-permute-start.26) | collective-permute-done | bytes 131104 | tf_op jit(solution)/shard_map/ppermute | solution.py:18
  52.8 2.7 %collective-permute-done.25.refs_2_ = bf16[512,128]{1,0:T(8,128)(2,1)S(1)} collective-permute-done((bf16[512,128]{1,0:T(8,128)(2,1)S(1)}, bf16[512,128]{1,0:T(8,128)(2,1)S(1)}, u32[]{:S(2)}, u32[]{:S(2)}) %collective-permute-start.25) | collective-permute-done | bytes 131104 | tf_op jit(solution)/shard_map/ppermute | solution.py:18
  55.5 2.1 %collective-permute-done.27.refs_3_ = bf16[512,128]{1,0:T(8,128)(2,1)S(1)} collective-permute-done((bf16[512,128]{1,0:T(8,128)(2,1)S(1)}, bf16[512,128]{1,0:T(8,128)(2,1)S(1)}, u32[]{:S(2)}, u32[]{:S(2)}) %collective-permute-start.27) | collective-permute-done | bytes 131104 | tf_op jit(solution)/shard_map/ppermute | solution.py:18
  57.7 3.9 %collective-permute-start.31 = (bf16[4,2,64,128]{3,2,1,0:T(8,128)(2,1)S(1)}, bf16[4,2,64,128]{3,2,1,0:T(8,128)(2,1)S(1)}, u32[]{:S(2)}, u32[]{:S(2)}) collective-permute-start(bf16[4,2,64,128]{3,2,1,0:T(8,128)(2,1)S(1)} %get-tuple-element.80), channel_id=1, source_target_pairs={{0,8},{1,2},{2,1},{3,4},{4,3},{5,6},{6,5},{7,15},{8,0},{9,10},{10,... | collective-permute-start | bytes 393224 | tf_op jit(solution)/shard_map/ppermute | solution.py:36
  61.6 2.3 %collective-permute-start.28 = (bf16[2,2,64,128]{3,2,1,0:T(8,128)(2,1)S(1)}, bf16[2,2,64,128]{3,2,1,0:T(8,128)(2,1)S(1)}, u32[]{:S(2)}, u32[]{:S(2)}) collective-permute-start(bf16[2,2,64,128]{3,2,1,0:T(8,128)(2,1)S(1)} %get-tuple-element.78), channel_id=1, source_target_pairs={{0,8},{8,0},{16,24},{24,16},{1,9},{9,1},{17,25},{25,17},{2,10},{10... | collective-permute-start | bytes 196616 | tf_op jit(solution)/shard_map/ppermute | solution.py:18
  64.0 1.9 %collective-permute-done.28.refs_0_.refs_1_ = bf16[2,2,64,128]{3,2,1,0:T(8,128)(2,1)S(1)} collective-permute-done((bf16[2,2,64,128]{3,2,1,0:T(8,128)(2,1)S(1)}, bf16[2,2,64,128]{3,2,1,0:T(8,128)(2,1)S(1)}, u32[]{:S(2)}, u32[]{:S(2)}) %collective-permute-start.28) | collective-permute-done | bytes 65568 | tf_op jit(solution)/shard_map/ppermute | solution.py:18
  65.9 1.2 %collective-permute-done.29.refs_1_.refs_2_ = bf16[2,2,64,128]{3,2,1,0:T(8,128)(2,1)S(1)} collective-permute-done((bf16[2,2,64,128]{3,2,1,0:T(8,128)(2,1)S(1)}, bf16[2,2,64,128]{3,2,1,0:T(8,128)(2,1)S(1)}, u32[]{:S(2)}, u32[]{:S(2)}) %collective-permute-start.29) | collective-permute-done | bytes 65568 | tf_op jit(solution)/shard_map/ppermute | solution.py:36
  67.1 2.0 %collective-permute-start.32 = (bf16[2,64,128]{2,1,0:T(8,128)(2,1)S(1)}, bf16[2,64,128]{2,1,0:T(8,128)(2,1)S(1)}, u32[]{:S(2)}, u32[]{:S(2)}) collective-permute-start(bf16[2,64,128]{2,1,0:T(8,128)(2,1)S(1)} %get-tuple-element.81), channel_id=1, source_target_pairs={{0,1},{1,0},{2,3},{3,2},{4,5},{5,4},{6,7},{7,6},{8,9},{9,8},{10,11... | collective-permute-start | bytes 98312 | tf_op jit(solution)/shard_map/ppermute | solution.py:18
  70.0 3.4 %collective-permute-done.33.refs_6_ = bf16[2,64,128]{2,1,0:T(8,128)(2,1)S(1)} collective-permute-done((bf16[2,64,128]{2,1,0:T(8,128)(2,1)S(1)}, bf16[2,64,128]{2,1,0:T(8,128)(2,1)S(1)}, u32[]{:S(2)}, u32[]{:S(2)}) %collective-permute-start.33) | collective-permute-done | bytes 32800 | tf_op jit(solution)/shard_map/ppermute | solution.py:36
  73.3 1.8 %shard_map.73 = f32[4,2,64,128]{3,2,1,0:T(8,128)} custom-call(f32[4,2,64,128]{3,2,1,0:T(8,128)S(1)} %get-tuple-element.77.refs_0_, bf16[2,2,64,128]{3,2,1,0:T(8,128)(2,1)S(1)} %collective-permute-done.28.refs_0_.refs_1_, bf16[2,2,64,128]{3,2,1,0:T(8,128)(2,1)S(1)} %collective-permute-done.29.refs_1_.refs_2_, ...), custom_call_target="tpu_custom_call" | custom-call | tf_op jit(solution)/shard_map/pallas_call | solution.py:60
  (70 shorter events, 19.4 us)
Async XLA Ops:
  1.1 5.4 %collective-permute-start.1 = (bf16[128,512]{1,0:T(8,128)(2,1)S(1)}, bf16[128,512]{1,0:T(8,128)(2,1)S(1)}, u32[]{:S(2)}, u32[]{:S(2)}) collective-permute-start(bf16[128,512]{1,0:T(8,128)(2,1)S(1)} %shard_map.55.refs_0_.refs_1_), channel_id=1, source_target_pairs={{0,16},{8,24},{16,0},{24,8},{1,17},{9,25},{17,1},{25,9},{2,18},{10... | collective-permute-start | bytes 393224 | tf_op jit(solution)/shard_map/ppermute | solution.py:18
  1.2 16.1 %collective-permute-start = (bf16[128,512]{1,0:T(8,128)(2,1)S(1)}, bf16[128,512]{1,0:T(8,128)(2,1)S(1)}, u32[]{:S(2)}, u32[]{:S(2)}) collective-permute-start(bf16[128,512]{1,0:T(8,128)(2,1)S(1)} %shard_map.55.refs_0_.refs_1_), channel_id=1, source_target_pairs={{0,8},{8,0},{16,24},{24,16},{1,9},{9,1},{17,25},{25,17},{2,10},{10... | collective-permute-start | bytes 393224 | tf_op jit(solution)/shard_map/ppermute | solution.py:18
  6.4 11.4 %collective-permute-start.2 = (bf16[128,512]{1,0:T(8,128)(2,1)S(1)}, bf16[128,512]{1,0:T(8,128)(2,1)S(1)}, u32[]{:S(2)}, u32[]{:S(2)}) collective-permute-start(bf16[128,512]{1,0:T(8,128)(2,1)S(1)} %collective-permute-done.1.refs_2_), channel_id=1, source_target_pairs={{0,8},{8,0},{16,24},{24,16},{1,9},{9,1},{17,25},{25,17},{2,10},{10... | collective-permute-start | bytes 393224 | tf_op jit(solution)/shard_map/ppermute | solution.py:18
  21.3 4.8 %collective-permute-start.4 = (bf16[3,128,128]{2,1,0:T(8,128)(2,1)S(1)}, bf16[3,128,128]{2,1,0:T(8,128)(2,1)S(1)}, u32[]{:S(2)}, u32[]{:S(2)}) collective-permute-start(bf16[3,128,128]{2,1,0:T(8,128)(2,1)S(1)} %get-tuple-element.54), channel_id=1, source_target_pairs={{0,2},{1,3},{2,0},{3,1},{4,6},{5,7},{6,4},{7,5},{8,10},{9,11},{10,... | collective-permute-start | bytes 294920 | tf_op jit(solution)/shard_map/ppermute | solution.py:18
  21.7 5.6 %collective-permute-start.5 = (bf16[3,128,128]{2,1,0:T(8,128)(2,1)S(1)}, bf16[3,128,128]{2,1,0:T(8,128)(2,1)S(1)}, u32[]{:S(2)}, u32[]{:S(2)}) collective-permute-start(bf16[3,128,128]{2,1,0:T(8,128)(2,1)S(1)} %get-tuple-element.55), channel_id=1, source_target_pairs={{0,4},{1,5},{2,6},{3,7},{4,0},{5,1},{6,2},{7,3},{8,12},{9,13},{10,... | collective-permute-start | bytes 294920 | tf_op jit(solution)/shard_map/ppermute | solution.py:18
  22.9 5.5 %collective-permute-start.6 = (bf16[3,128,128]{2,1,0:T(8,128)(2,1)S(1)}, bf16[3,128,128]{2,1,0:T(8,128)(2,1)S(1)}, u32[]{:S(2)}, u32[]{:S(2)}) collective-permute-start(bf16[3,128,128]{2,1,0:T(8,128)(2,1)S(1)} %get-tuple-element.56), channel_id=1, source_target_pairs={{0,6},{1,7},{2,4},{3,5},{4,2},{5,3},{6,0},{7,1},{8,14},{9,15},{10,... | collective-permute-start | bytes 294920 | tf_op jit(solution)/shard_map/ppermute | solution.py:18
  24.6 5.4 %collective-permute-start.15 = (bf16[2,128,128]{2,1,0:T(8,128)(2,1)S(1)}, bf16[2,128,128]{2,1,0:T(8,128)(2,1)S(1)}, u32[]{:S(2)}, u32[]{:S(2)}) collective-permute-start(bf16[2,128,128]{2,1,0:T(8,128)(2,1)S(1)} %get-tuple-element.66), channel_id=1, source_target_pairs={{0,2},{1,3},{2,0},{3,1},{4,6},{5,7},{6,4},{7,5},{8,10},{9,11},{10,... | collective-permute-start | bytes 196616 | tf_op jit(solution)/shard_map/ppermute | solution.py:18
  24.9 5.1 %collective-permute-start.16 = (bf16[2,128,128]{2,1,0:T(8,128)(2,1)S(1)}, bf16[2,128,128]{2,1,0:T(8,128)(2,1)S(1)}, u32[]{:S(2)}, u32[]{:S(2)}) collective-permute-start(bf16[2,128,128]{2,1,0:T(8,128)(2,1)S(1)} %get-tuple-element.67), channel_id=1, source_target_pairs={{0,4},{1,5},{2,6},{3,7},{4,0},{5,1},{6,2},{7,3},{8,12},{9,13},{10,... | collective-permute-start | bytes 196616 | tf_op jit(solution)/shard_map/ppermute | solution.py:18
  26.1 4.8 %collective-permute-start.17 = (bf16[2,128,128]{2,1,0:T(8,128)(2,1)S(1)}, bf16[2,128,128]{2,1,0:T(8,128)(2,1)S(1)}, u32[]{:S(2)}, u32[]{:S(2)}) collective-permute-start(bf16[2,128,128]{2,1,0:T(8,128)(2,1)S(1)} %get-tuple-element.68), channel_id=1, source_target_pairs={{0,6},{1,7},{2,4},{3,5},{4,2},{5,3},{6,0},{7,1},{8,14},{9,15},{10,... | collective-permute-start | bytes 196616 | tf_op jit(solution)/shard_map/ppermute | solution.py:18
  28.6 10.7 %collective-permute-start.12 = (bf16[3,128,128]{2,1,0:T(8,128)(2,1)S(1)}, bf16[3,128,128]{2,1,0:T(8,128)(2,1)S(1)}, u32[]{:S(2)}, u32[]{:S(2)}) collective-permute-start(bf16[3,128,128]{2,1,0:T(8,128)(2,1)S(1)} %shard_map.62.refs_1_), channel_id=1, source_target_pairs={{0,6},{1,7},{2,4},{3,5},{4,2},{5,3},{6,0},{7,1},{8,14},{9,15},{10,... | collective-permute-start | bytes 294920 | tf_op jit(solution)/shard_map/ppermute | solution.py:18
  28.7 10.6 %collective-permute-start.10 = (bf16[3,128,128]{2,1,0:T(8,128)(2,1)S(1)}, bf16[3,128,128]{2,1,0:T(8,128)(2,1)S(1)}, u32[]{:S(2)}, u32[]{:S(2)}) collective-permute-start(bf16[3,128,128]{2,1,0:T(8,128)(2,1)S(1)} %shard_map.62.refs_1_), channel_id=1, source_target_pairs={{0,4},{1,5},{2,6},{3,7},{4,0},{5,1},{6,2},{7,3},{8,12},{9,13},{10,... | collective-permute-start | bytes 294920 | tf_op jit(solution)/shard_map/ppermute | solution.py:18
  31.1 5.3 %collective-permute-start.23 = (bf16[2,128,128]{2,1,0:T(8,128)(2,1)S(1)}, bf16[2,128,128]{2,1,0:T(8,128)(2,1)S(1)}, u32[]{:S(2)}, u32[]{:S(2)}) collective-permute-start(bf16[2,128,128]{2,1,0:T(8,128)(2,1)S(1)} %shard_map.67.refs_2_), channel_id=1, source_target_pairs={{0,6},{1,7},{2,4},{3,5},{4,2},{5,3},{6,0},{7,1},{8,14},{9,15},{10,... | collective-permute-start | bytes 196616 | tf_op jit(solution)/shard_map/ppermute | solution.py:18
  34.5 6.0 %collective-permute-start.8 = (bf16[3,128,128]{2,1,0:T(8,128)(2,1)S(1)}, bf16[3,128,128]{2,1,0:T(8,128)(2,1)S(1)}, u32[]{:S(2)}, u32[]{:S(2)}) collective-permute-start(bf16[3,128,128]{2,1,0:T(8,128)(2,1)S(1)} %shard_map.62.refs_1_), channel_id=1, source_target_pairs={{0,2},{1,3},{2,0},{3,1},{4,6},{5,7},{6,4},{7,5},{8,10},{9,11},{10,... | collective-permute-start | bytes 294920 | tf_op jit(solution)/shard_map/ppermute | solution.py:18
  34.5 5.3 %collective-permute-start.21 = (bf16[2,128,128]{2,1,0:T(8,128)(2,1)S(1)}, bf16[2,128,128]{2,1,0:T(8,128)(2,1)S(1)}, u32[]{:S(2)}, u32[]{:S(2)}) collective-permute-start(bf16[2,128,128]{2,1,0:T(8,128)(2,1)S(1)} %shard_map.67.refs_2_), channel_id=1, source_target_pairs={{0,4},{1,5},{2,6},{3,7},{4,0},{5,1},{6,2},{7,3},{8,12},{9,13},{10,... | collective-permute-start | bytes 196616 | tf_op jit(solution)/shard_map/ppermute | solution.py:18
  36.3 8.6 %collective-permute-start.7 = (bf16[3,128,128]{2,1,0:T(8,128)(2,1)S(1)}, bf16[3,128,128]{2,1,0:T(8,128)(2,1)S(1)}, u32[]{:S(2)}, u32[]{:S(2)}) collective-permute-start(bf16[3,128,128]{2,1,0:T(8,128)(2,1)S(1)} %shard_map.62.refs_1_), channel_id=1, source_target_pairs={{0,1},{1,0},{2,3},{3,2},{4,5},{5,4},{6,7},{7,6},{8,9},{9,8},{10,11... | collective-permute-start | bytes 294920 | tf_op jit(solution)/shard_map/ppermute | solution.py:18
  39.3 5.6 %collective-permute-start.13 = (bf16[3,128,128]{2,1,0:T(8,128)(2,1)S(1)}, bf16[3,128,128]{2,1,0:T(8,128)(2,1)S(1)}, u32[]{:S(2)}, u32[]{:S(2)}) collective-permute-start(bf16[3,128,128]{2,1,0:T(8,128)(2,1)S(1)} %collective-permute-done.12.refs_7_), channel_id=1, source_target_pairs={{0,1},{1,0},{2,3},{3,2},{4,5},{5,4},{6,7},{7,6},{8,9},{9,8},{10,11... | collective-permute-start | bytes 294920 | tf_op jit(solution)/shard_map/ppermute | solution.py:18
  39.3 6.2 %collective-permute-start.11 = (bf16[3,128,128]{2,1,0:T(8,128)(2,1)S(1)}, bf16[3,128,128]{2,1,0:T(8,128)(2,1)S(1)}, u32[]{:S(2)}, u32[]{:S(2)}) collective-permute-start(bf16[3,128,128]{2,1,0:T(8,128)(2,1)S(1)} %collective-permute-done.10.refs_5_), channel_id=1, source_target_pairs={{0,1},{1,0},{2,3},{3,2},{4,5},{5,4},{6,7},{7,6},{8,9},{9,8},{10,11... | collective-permute-start | bytes 294920 | tf_op jit(solution)/shard_map/ppermute | solution.py:18
  40.5 5.0 %collective-permute-start.9 = (bf16[3,128,128]{2,1,0:T(8,128)(2,1)S(1)}, bf16[3,128,128]{2,1,0:T(8,128)(2,1)S(1)}, u32[]{:S(2)}, u32[]{:S(2)}) collective-permute-start(bf16[3,128,128]{2,1,0:T(8,128)(2,1)S(1)} %collective-permute-done.8.refs_3_), channel_id=1, source_target_pairs={{0,1},{1,0},{2,3},{3,2},{4,5},{5,4},{6,7},{7,6},{8,9},{9,8},{10,11... | collective-permute-start | bytes 294920 | tf_op jit(solution)/shard_map/ppermute | solution.py:18
  47.7 5.0 %collective-permute-start.26 = (bf16[512,128]{1,0:T(8,128)(2,1)S(1)}, bf16[512,128]{1,0:T(8,128)(2,1)S(1)}, u32[]{:S(2)}, u32[]{:S(2)}) collective-permute-start(bf16[512,128]{1,0:T(8,128)(2,1)S(1)} %get-tuple-element.76), channel_id=1, source_target_pairs={{0,8},{8,0},{16,24},{24,16},{1,9},{9,1},{17,25},{25,17},{2,10},{10... | collective-permute-start | bytes 393224 | tf_op jit(solution)/shard_map/ppermute | solution.py:18
  48.8 6.7 %collective-permute-start.25 = (bf16[512,128]{1,0:T(8,128)(2,1)S(1)}, bf16[512,128]{1,0:T(8,128)(2,1)S(1)}, u32[]{:S(2)}, u32[]{:S(2)}) collective-permute-start(bf16[512,128]{1,0:T(8,128)(2,1)S(1)} %get-tuple-element.74), channel_id=1, source_target_pairs={{0,8},{8,0},{16,24},{24,16},{1,9},{9,1},{17,25},{25,17},{2,10},{10... | collective-permute-start | bytes 393224 | tf_op jit(solution)/shard_map/ppermute | solution.py:18
  52.7 4.9 %collective-permute-start.27 = (bf16[512,128]{1,0:T(8,128)(2,1)S(1)}, bf16[512,128]{1,0:T(8,128)(2,1)S(1)}, u32[]{:S(2)}, u32[]{:S(2)}) collective-permute-start(bf16[512,128]{1,0:T(8,128)(2,1)S(1)} %shard_map.70), channel_id=1, source_target_pairs={{0,16},{8,24},{16,0},{24,8},{1,17},{9,25},{17,1},{25,9},{2,18},{10... | collective-permute-start | bytes 393224 | tf_op jit(solution)/shard_map/ppermute | solution.py:18
  57.7 15.7 %collective-permute-start.31 = (bf16[4,2,64,128]{3,2,1,0:T(8,128)(2,1)S(1)}, bf16[4,2,64,128]{3,2,1,0:T(8,128)(2,1)S(1)}, u32[]{:S(2)}, u32[]{:S(2)}) collective-permute-start(bf16[4,2,64,128]{3,2,1,0:T(8,128)(2,1)S(1)} %get-tuple-element.80), channel_id=1, source_target_pairs={{0,8},{1,2},{2,1},{3,4},{4,3},{5,6},{6,5},{7,15},{8,0},{9,10},{10,... | collective-permute-start | bytes 393224 | tf_op jit(solution)/shard_map/ppermute | solution.py:36
  61.6 11.7 %collective-permute-start.30 = (bf16[4,2,64,128]{3,2,1,0:T(8,128)(2,1)S(1)}, bf16[4,2,64,128]{3,2,1,0:T(8,128)(2,1)S(1)}, u32[]{:S(2)}, u32[]{:S(2)}) collective-permute-start(bf16[4,2,64,128]{3,2,1,0:T(8,128)(2,1)S(1)} %get-tuple-element.80), channel_id=1, source_target_pairs={{0,1},{1,0},{2,3},{3,2},{4,5},{5,4},{6,7},{7,6},{8,9},{9,8},{10,11... | collective-permute-start | bytes 393224 | tf_op jit(solution)/shard_map/ppermute | solution.py:18
  61.6 4.3 %collective-permute-start.28 = (bf16[2,2,64,128]{3,2,1,0:T(8,128)(2,1)S(1)}, bf16[2,2,64,128]{3,2,1,0:T(8,128)(2,1)S(1)}, u32[]{:S(2)}, u32[]{:S(2)}) collective-permute-start(bf16[2,2,64,128]{3,2,1,0:T(8,128)(2,1)S(1)} %get-tuple-element.78), channel_id=1, source_target_pairs={{0,8},{8,0},{16,24},{24,16},{1,9},{9,1},{17,25},{25,17},{2,10},{10... | collective-permute-start | bytes 196616 | tf_op jit(solution)/shard_map/ppermute | solution.py:18
  (12 other events, 36.9 us)

commit v6 on v5

--- a/solution.py
+++ b/solution.py
@@ -193,27 +193,30 @@
             back_ref[i, tile] = back_tile(held, mask_ref, u_ref, tile, i, 0)
 
 
-def adjoint_kernel(count, first, mask_ref, early_ref, *refs):
+def adjoint_kernel(count, brick, distances, mask_ref, early_ref, *refs):
     pieces, (u_ref, v_ref), rest = refs[:count], refs[count : count + 2], refs[count + 2 :]
     outs, (held, back_ref) = rest[:-2], rest[-2:]
     row_tiles, tile_len = u_ref.shape[0], u_ref.shape[2]
-    low = early_ref.shape[0]
-    brick = outs[0].shape[0]
-    per_tile = tile_len // brick
+    low, size = early_ref.shape[0], outs[0].shape[0]
+    per_tile, cuts = tile_len // brick, brick // size
     me_row = lax.axis_index("row")
     hold(held, pieces)
-    for n in range(len(outs) // per_tile):
-        tile = (me_row // per_tile) ^ (first + n)
-        for i in range(row_tiles - low):
-            back_ref[i] = back_tile(held, mask_ref, u_ref, tile, i, low)
-        for p in reversed(range(per_tile)):
-            inside = pl.multiple_of(((me_row % per_tile) ^ p) * brick, brick)
+    ready = None
+    for n, distance in enumerate(distances):
+        tile = (me_row // per_tile) ^ (distance // per_tile)
+        if ready != distance // per_tile:
+            ready = distance // per_tile
+            for i in range(row_tiles - low):
+                back_ref[i] = back_tile(held, mask_ref, u_ref, tile, i, low)
+        for cut in range(cuts):
+            inside = ((me_row % per_tile) ^ (distance % per_tile)) * brick + cut * size
+            inside = pl.multiple_of(inside, size)
             value = None
             for i in range(row_tiles):
                 back = early_ref[i, tile] if i < low else back_ref[i - low]
-                term = dot_nt(v_ref[i, tile, pl.ds(inside, brick)], back)
+                term = dot_nt(v_ref[i, tile, pl.ds(inside, size)], back)
                 value = term if value is None else value + term
-            out_ref = outs[n * per_tile + p]
+            out_ref = outs[n * cuts + cut]
             out_ref[...] = value.astype(out_ref.dtype)
 
 
@@ -224,11 +227,15 @@
     refs[-1][...] = value.astype(BF16)
 
 
-def move_kernel(image_ref, part_ref, *refs):
-    received, (moved_ref, even_ref, odd_ref, side_ref) = refs[:-4], refs[-4:]
-    gradient = part_ref[...]
-    for ref in received:
-        gradient = gradient + ref[...].astype(F32)
+def move_kernel(cuts, image_ref, *refs):
+    parts, (moved_ref, even_ref, odd_ref, side_ref) = refs[:-4], refs[-4:]
+    terms = []
+    for cut in range(cuts):
+        value = parts[cut][...]
+        for ref in parts[cuts + cut :: cuts]:
+            value = value + ref[...].astype(F32)
+        terms.append(value)
+    gradient = jnp.concatenate(terms, axis=0)
     moved = image_ref[...] - gradient.reshape(image_ref.shape)
     moved_ref[...] = moved
     side_ref[...] = moved.astype(BF16)
@@ -255,66 +262,114 @@
     return delta / (1.0 + scaled * scaled)
 
 
-def diffuse_kernel(moved_ref, row_even, row_odd, col_even, col_odd, corner_even, corner_odd, out_ref, field):
-    nx, ny, depth, frames = moved_ref.shape
+def grid_position():
     rows, cols = lax.axis_size("row"), lax.axis_size("col")
     me_row, me_col = lax.axis_index("row"), lax.axis_index("col")
-    r_odd, c_odd = me_row % 2, me_col % 2
-    r_even, c_even = 1 - r_odd, 1 - c_odd
-    low_x, high_x = me_row > 0, me_row < rows - 1
-    low_y, high_y = me_col > 0, me_col < cols - 1
-    within = lambda ref, inside: jnp.where(inside, ref.astype(F32), 0.0)
-    field[2 : 2 + nx, 2 : 2 + ny] = moved_ref[...]
-    far_x, far_y = nx + 2, ny + 2
-    field[pl.ds(r_even * far_x, 2), 2 : 2 + ny] = row_even[...].astype(F32)
-    field[pl.ds(r_odd * far_x, 2), 2 : 2 + ny] = within(row_odd[...], low_x & high_x)
-    field[2 : 2 + nx, pl.ds(c_even * far_y, 2)] = col_even[...].astype(F32)
-    field[2 : 2 + nx, pl.ds(c_odd * far_y, 2)] = within(col_odd[...], low_y & high_y)
-    for y, ref, inside in (
-        (c_even * (ny + 1) + 1, corner_even, True),
-        (c_odd * (ny + 1) + 1, corner_odd, low_y & high_y),
-    ):
-        field[1, y] = within(ref[0], low_x & inside)
-        field[nx + 2, y] = within(ref[1], high_x & inside)
-    level = lax.broadcasted_iota(jnp.int32, (depth, frames), 0)
-
-    def along_depth(u):
+    return me_row, me_col, (me_row > 0, me_row < rows - 1), (me_col > 0, me_col < cols - 1)
+
+
+def within(value, inside):
+    return jnp.where(inside, value.astype(F32), 0.0)
+
+
+def diffuse(cells, get):
+    faces = {}
+
+    def face(kind, x, y):
+        key = (kind, x, y)
+        if key not in faces:
+            x2, y2 = (x + 1, y) if kind == 0 else (x, y + 1)
+            faces[key] = flux(get(x2, y2) - get(x, y))
+        return faces[key]
+
+    new = {}
+    for x, y in cells:
+        u = get(x, y)
+        depth = u.shape[0]
+        level = lax.broadcasted_iota(jnp.int32, u.shape, 0)
         below = jnp.where(level == 0, 0.0, pltpu.roll(u, 1, 0))
         down = flux(u - below)
         up = jnp.where(level == depth - 1, flux(-u), pltpu.roll(down, depth - 1, 0))
-        return up - down
-
-    def diffuse(cells, get):
-        faces = {}
-
-        def face(kind, x, y):
-            key = (kind, x, y)
-            if key not in faces:
-                x2, y2 = (x + 1, y) if kind == 0 else (x, y + 1)
-                faces[key] = flux(get(x2, y2) - get(x, y))
-            return faces[key]
-
-        new = {}
-        for x, y in cells:
-            u = get(x, y)
-            total = face(0, x, y) - face(0, x - 1, y)
-            total = total + (face(1, x, y) - face(1, x, y - 1))
-            new[x, y] = u + diff_rate * (total + along_depth(u))
-        return new
-
-    inner = [(x, y) for x in range(2, 2 + nx) for y in range(2, 2 + ny)]
-    ring = [(x, y) for x in (1, nx + 2) for y in range(2, 2 + ny)]
-    ring += [(x, y) for x in range(2, 2 + nx) for y in (1, ny + 2)]
-    first = diffuse(sorted(inner + ring), lambda x, y: field[x, y])
-    for x, y in first:
-        value = first[x, y]
-        for at, end, open_end in ((x, 1, low_x), (x, nx + 2, high_x), (y, 1, low_y), (y, ny + 2, high_y)):
-            if at == end:
-                value = jnp.where(open_end, value, 0.0)
-        field[x, y] = value
-    second = diffuse(inner, lambda x, y: field[x, y])
-    for x, y in inner:
-        out_ref[x - 2, y - 2] = second[x, y]
+        total = face(0, x, y) - face(0, x - 1, y)
+        total = total + (face(1, x, y) - face(1, x, y - 1))
+        new[x, y] = u + diff_rate * (total + (up - down))
+    return new
+
+
+def inner_kernel(moved_ref, row_even, row_odd, col_even, col_odd, field, fresh_ref):
+    nx, ny = moved_ref.shape[:2]
+    me_row, me_col, (low_x, high_x), (low_y, high_y) = grid_position()
+    r_odd, c_odd = me_row % 2, me_col % 2
+    field[2 : 2 + nx, 2 : 2 + ny] = moved_ref[...]
+    far_x, far_y = nx + 2, ny + 2
+    field[pl.ds((1 - r_odd) * far_x, 2), 2 : 2 + ny] = row_even[...].astype(F32)
+    field[pl.ds(r_odd * far_x, 2), 2 : 2 + ny] = within(row_odd[...], low_x & high_x)
+    field[2 : 2 + nx, pl.ds((1 - c_odd) * far_y, 2)] = col_even[...].astype(F32)
+    field[2 : 2 + nx, pl.ds(c_odd * far_y, 2)] = within(col_odd[...], low_y & high_y)
+    cells = [(x, y) for x in range(2, 2 + nx) for y in range(2, 2 + ny)]
+    for (x, y), value in diffuse(cells, lambda x, y: field[x, y]).items():
+        fresh_ref[x - 2, y - 2] = value
+
+
+def outer_kernel(field, fresh_ref, corner_even, corner_odd, out_ref, corners, middle, ready, sems):
+    nx, ny = fresh_ref.shape[:2]
+    me_row, me_col, (low_x, high_x), (low_y, high_y) = grid_position()
+    c_odd = me_col % 2
+    for side, ref, inside in (
+        (1 - c_odd, corner_even, True),
+        (c_odd, corner_odd, low_y & high_y),
+    ):
+        corners[0, side] = within(ref[0], low_x & inside)
+        corners[1, side] = within(ref[1], high_x & inside)
+    ends_x, ends_y = (1, nx + 2), (1, ny + 2)
+
+    def get(x, y):
+        if x in ends_x and y in ends_y:
+            return corners[ends_x.index(x), ends_y.index(y)]
+        return field[x, y]
+
+    ring = [(x, y) for x in ends_x for y in range(2, 2 + ny)]
+    ring += [(x, y) for x in range(2, 2 + nx) for y in ends_y]
+    opens = {**dict(zip([("x", x) for x in ends_x], (low_x, high_x)))}
+    opens.update(dict(zip([("y", y) for y in ends_y], (low_y, high_y))))
+    for (x, y), value in diffuse(ring, get).items():
+        inside = opens["x", x] if x in ends_x else opens["y", y]
+        middle[x, y] = jnp.where(inside, value, 0.0)
+
+    def later(x, y):
+        if 2 <= x < 2 + nx and 2 <= y < 2 + ny:
+            return fresh_ref[x - 2, y - 2]
+        return middle[x, y]
+
+    cells = [(x, y) for x in range(2, 2 + nx) for y in range(2, 2 + ny)]
+    copies = []
+    for (x, y), value in diffuse(cells, later).items():
+        ready[x - 2, y - 2] = value
+        if y == ny + 1:
+            copies.append(pltpu.make_async_copy(ready.at[x - 2], out_ref.at[x - 2], sems.at[x - 2]))
+            copies[-1].start()
+    for copy in copies:
+        copy.wait()
+
+
+def finish(field, fresh, corner_even, corner_odd):
+    nx, ny, depth, frames = fresh.shape
+    vmem = pl.BlockSpec(memory_space=pltpu.VMEM)
+    arrays = (field, fresh, corner_even, corner_odd)
+    return pl.pallas_call(
+        outer_kernel,
+        name="outer",
+        out_shape=jax.ShapeDtypeStruct(fresh.shape, F32),
+        in_specs=[vmem] * 4,
+        out_specs=pl.BlockSpec(memory_space=pltpu.HBM),
+        scratch_shapes=[
+            pltpu.VMEM((2, 2, depth, frames), F32),
+            pltpu.VMEM((nx + 4, ny + 4, depth, frames), F32),
+            pltpu.VMEM(fresh.shape, F32),
+            pltpu.SemaphoreType.DMA((nx,)),
+        ],
+        compiler_params=pltpu.CompilerParams(vmem_limit_bytes=2**23),
+    )(*[pltpu.with_memory_space_constraint(value, pltpu.VMEM) for value in arrays])
 
 
 def step(image, u_factors, v_factors, ranks, measured):
@@ -392,39 +447,48 @@
         through=1,
     )
 
-    def adjoint(distances, kinds, u_factors, v_factors):
+    cuts = 1
+
+    def adjoint(distances, u_factors, v_factors):
         size = groups[1][1]
-        return call(
-            functools.partial(adjoint_kernel, cols, distances[0] // per_tile),
+        kinds = [BF16 if d % 2 else F32 for d in distances for _ in range(cuts)]
+        *terms, u_factors, v_factors = call(
+            functools.partial(adjoint_kernel, cols, brick, distances),
             (mask, early, *parts[1], u_factors, v_factors),
-            [((brick, frames), kind) for kind in kinds],
+            [((brick // cuts, frames), kind) for kind in kinds],
             [
                 pltpu.VMEM((cols, size, frames, part_len), BF16),
                 pltpu.VMEM((size, frames, rank_max), BF16),
             ],
             through=2,
         )
-
-    kinds = [BF16 if d % 2 else F32 for d in range(rows)]
-    *far, u_factors, v_factors = adjoint(
-        range(per_tile, rows), kinds[per_tile:], u_factors, v_factors
-    )
-    *close, u_factors, v_factors = adjoint(range(per_tile), kinds[:per_tile], u_factors, v_factors)
-    terms = close + far
-    sums = {}
-    for d in range(0, rows, 2):
-        sums[d] = (terms[d], [swap(terms[d + 1], "row", 1)])
+        for n, d in enumerate(distances):
+            pieces[d] = terms[n * cuts : (n + 1) * cuts]
+        return u_factors, v_factors
+
+    pieces, sums = {}, {}
+    u_factors, v_factors = adjoint(list(range(3, rows, 2)), u_factors, v_factors)
+    for d in range(3, rows, 2):
+        for cut in range(cuts):
+            sums[d - 1, cut] = [swap(pieces[d][cut], "row", 1)]
+    rest = [*range(2, rows, 2), 1, 0]
+    u_factors, v_factors = adjoint(rest, u_factors, v_factors)
+    for cut in range(cuts):
+        sums[0, cut] = [swap(pieces[1][cut], "row", 1)]
     for bit in bits_of(rows)[1:]:
-        for d in [d for d in sums if d & bit]:
-            base, extra = sums.pop(d)
-            (base,) = call(add_kernel, (base, *extra), [(base.shape, BF16)])
-            sums[d ^ bit][1].append(swap(base, "row", bit))
-    base, extra = sums[0]
+        for d in range(bit, rows, 2 * bit):
+            for cut in range(cuts):
+                (value,) = call(
+                    add_kernel, (pieces[d][cut], *sums[d, cut]), [(pieces[d][cut].shape, BF16)]
+                )
+                sums[d ^ bit, cut].append(swap(value, "row", bit))
+    terms = [*zip(*[sums[0, cut] for cut in range(cuts)])]
+    terms = [*pieces[0], *[value for pair in terms for value in pair]]
 
     edge = (2, ny, depth, frames)
     moved, to_even, to_odd, side = call(
-        move_kernel,
-        (image, base, *extra),
+        functools.partial(move_kernel, cuts),
+        (image, *terms),
         [(image.shape, F32), (edge, BF16), (edge, BF16), (image.shape, BF16)],
     )
     row_even = swap(to_even, "row", 1)
@@ -435,13 +499,12 @@
     to_even, to_odd = call(corner_kernel, (row_even, row_odd), [(corner, BF16)] * 2)
     corner_odd = swap_odd(to_odd, "col")
     corner_even = swap(to_even, "col", 1)
-    return call(
-        diffuse_kernel,
-        (moved, row_even, row_odd, col_even, col_odd, corner_even, corner_odd),
-        [(image.shape, F32)],
-        [pltpu.VMEM((nx + 4, ny + 4, depth, frames), F32)],
-        jax.ShapeDtypeStruct,
-    )[0]
+    field, fresh = call(
+        inner_kernel,
+        (moved, row_even, row_odd, col_even, col_odd),
+        [((nx + 4, ny + 4, depth, frames), F32), (image.shape, F32)],
+    )
+    return finish(field, fresh, corner_even, corner_odd)
 
 
 def solution(mesh):

time: 76.6 us -> 76 us (level)
  waiting for transfers between devices: 21.7 us -> 20.8 us
    pallas_call x0 -> x1, Pallas kernels: none -> 1.5 us  [finish(): pl.pallas_call(outer_kernel, name='outer', out_shape=jax.ShapeDtypeStruct...]
    pallas_call x17, Pallas kernels: 8.46 us -> 7.24 us  [call(): pl.pallas_call(run, out_shape=[kept(shape, kind) for shape, kind in outs]...]
  transfers between devices with their start and end apart: 34 -> 34, of which waited for: 14 -> 13; matrix products, arithmetic and copies ran while one was open for 1% -> 1% of each run, Pallas kernels for 13% -> 15%
where the time goes in v6:
time: 76 us; the launch traced here: 74.5 us
  starting transfers between devices  37.2 us (49%)
  waiting for transfers between devices  20.8 us (27%)
  Pallas kernels  14.5 us (19%)
  local copies, waits for them, and re-layouts  1.8 us (2%)
    ppermute x31, starting transfers between devices, swap(): return lax.ppermute(value, axis, [(i, i ^ distance) for i in range(count)])  32.4 us
    ppermute x31, waiting for transfers between devices, swap(): return lax.ppermute(value, axis, [(i, i ^ distance) for i in range(count)])  16.5 us
    pallas_call x17, Pallas kernels, call(): pl.pallas_call(run, out_shape=[kept(shape, kind) for shape, kind in outs]...  7.24 us
    pallas_call x2, Pallas kernels, load(): pl.pallas_call(load_kernel, out_shape=[pltpu.VMEM(factors.shape, factors....  5.75 us
    ppermute x3, starting transfers between devices, swap_odd(): return lax.ppermute(value, ('row', 'col'), pairs)  4.81 us
    ppermute x3, waiting for transfers between devices, swap_odd(): return lax.ppermute(value, ('row', 'col'), pairs)  4.22 us
    unnamed x5, local copies, waits for them, and re-layouts  1.72 us
  transfers between devices with their start and end apart: 34, of which 13 were waited for; matrix products, arithmetic and copies ran while one was open for 1% of the time, Pallas kernels for 15%

profile of v6, /device:TPU:19, one launch (start us, length us, event | category | flops | bytes accessed | tf_op | source)
XLA Modules:
  0.0 74.5 jit_solution(9252097326210816891)
XLA Ops:
  1.2 1.3 %collective-permute-start = (bf16[128,512]{1,0:T(8,128)(2,1)S(1)}, bf16[128,512]{1,0:T(8,128)(2,1)S(1)}, u32[]{:S(2)}, u32[]{:S(2)}) collective-permute-start(bf16[128,512]{1,0:T(8,128)(2,1)S(1)} %shard_map.55.refs_0_.refs_1_), channel_id=1, source_target_pairs={{0,8},{8,0},{16,24},{24,16},{1,9},{9,1},{17,25},{25,17},{2,10},{10... | collective-permute-start | bytes 393224 | tf_op jit(solution)/shard_map/ppermute | solution.py:18
  3.3 3.1 %collective-permute-done.1.refs_2_ = bf16[128,512]{1,0:T(8,128)(2,1)S(1)} collective-permute-done((bf16[128,512]{1,0:T(8,128)(2,1)S(1)}, bf16[128,512]{1,0:T(8,128)(2,1)S(1)}, u32[]{:S(2)}, u32[]{:S(2)}) %collective-permute-start.1) | collective-permute-done | bytes 131104 | tf_op jit(solution)/shard_map/ppermute | solution.py:18
  6.4 5.0 %collective-permute-start.2 = (bf16[128,512]{1,0:T(8,128)(2,1)S(1)}, bf16[128,512]{1,0:T(8,128)(2,1)S(1)}, u32[]{:S(2)}, u32[]{:S(2)}) collective-permute-start(bf16[128,512]{1,0:T(8,128)(2,1)S(1)} %collective-permute-done.1.refs_2_), channel_id=1, source_target_pairs={{0,8},{8,0},{16,24},{24,16},{1,9},{9,1},{17,25},{25,17},{2,10},{10... | collective-permute-start | bytes 393224 | tf_op jit(solution)/shard_map/ppermute | solution.py:18
  11.5 2.5 %shard_map.56 = (bf16[5,2,1024,256]{3,2,1,0:T(8,128)(2,1)S(1)}, bf16[5,128,128]{2,1,0:T(8,128)(2,1)S(1)}) custom-call(bf16[5,2,1024,256]{3,2,1,0:T(8,128)(2,1)} %factor_ref.2, bf16[5,8,128,128]{3,2,1,0:T(8,128)(2,1)} %bitcast.5, bf16[128,512]{1,0:T(8,128)(2,1)S(1)} %shard_map.55.refs_0_.refs_1_, f32[10,256]{1,0:T(8,128)S(1)} %fusion.refs_1_.refs_0_), custom_call_target="tpu_custom_call" | custom-call | tf_op jit(solution)/shard_map/pallas_call | solution.py:85
  14.1 3.2 %shard_map.58 = (bf16[5,2,1024,256]{3,2,1,0:T(8,128)(2,1)S(1)}, bf16[5,128,128]{2,1,0:T(8,128)(2,1)}) custom-call(bf16[5,2,1024,256]{3,2,1,0:T(8,128)(2,1)} %factor_ref.3, bf16[5,8,128,128]{3,2,1,0:T(8,128)(2,1)} %bitcast.6, bf16[128,512]{1,0:T(8,128)(2,1)S(1)} %shard_map.55.refs_0_.refs_1_, f32[10,256]{1,0:T(8,128)S(1)} %fusion.refs_1_.refs_0_), custom_call_target="tpu_custom_call" | custom-call | tf_op jit(solution)/shard_map/pallas_call | solution.py:85
  21.7 1.2 %collective-permute-start.5 = (bf16[3,128,128]{2,1,0:T(8,128)(2,1)S(1)}, bf16[3,128,128]{2,1,0:T(8,128)(2,1)S(1)}, u32[]{:S(2)}, u32[]{:S(2)}) collective-permute-start(bf16[3,128,128]{2,1,0:T(8,128)(2,1)S(1)} %get-tuple-element.57), channel_id=1, source_target_pairs={{0,4},{1,5},{2,6},{3,7},{4,0},{5,1},{6,2},{7,3},{8,12},{9,13},{10,... | collective-permute-start | bytes 294920 | tf_op jit(solution)/shard_map/ppermute | solution.py:18
  24.9 1.2 %collective-permute-start.16 = (bf16[2,128,128]{2,1,0:T(8,128)(2,1)S(1)}, bf16[2,128,128]{2,1,0:T(8,128)(2,1)S(1)}, u32[]{:S(2)}, u32[]{:S(2)}) collective-permute-start(bf16[2,128,128]{2,1,0:T(8,128)(2,1)S(1)} %get-tuple-element.69), channel_id=1, source_target_pairs={{0,4},{1,5},{2,6},{3,7},{4,0},{5,1},{6,2},{7,3},{8,12},{9,13},{10,... | collective-permute-start | bytes 196616 | tf_op jit(solution)/shard_map/ppermute | solution.py:18
  28.7 1.2 %collective-permute-start.10 = (bf16[3,128,128]{2,1,0:T(8,128)(2,1)S(1)}, bf16[3,128,128]{2,1,0:T(8,128)(2,1)S(1)}, u32[]{:S(2)}, u32[]{:S(2)}) collective-permute-start(bf16[3,128,128]{2,1,0:T(8,128)(2,1)S(1)} %shard_map.62.refs_1_), channel_id=1, source_target_pairs={{0,4},{1,5},{2,6},{3,7},{4,0},{5,1},{6,2},{7,3},{8,12},{9,13},{10,... | collective-permute-start | bytes 294920 | tf_op jit(solution)/shard_map/ppermute | solution.py:18
  31.1 3.4 %collective-permute-start.23 = (bf16[2,128,128]{2,1,0:T(8,128)(2,1)S(1)}, bf16[2,128,128]{2,1,0:T(8,128)(2,1)S(1)}, u32[]{:S(2)}, u32[]{:S(2)}) collective-permute-start(bf16[2,128,128]{2,1,0:T(8,128)(2,1)S(1)} %shard_map.67.refs_2_), channel_id=1, source_target_pairs={{0,6},{1,7},{2,4},{3,5},{4,2},{5,3},{6,0},{7,1},{8,14},{9,15},{10,... | collective-permute-start | bytes 196616 | tf_op jit(solution)/shard_map/ppermute | solution.py:18
  34.9 1.5 %collective-permute-done.23.refs_8_ = bf16[2,128,128]{2,1,0:T(8,128)(2,1)S(1)} collective-permute-done((bf16[2,128,128]{2,1,0:T(8,128)(2,1)S(1)}, bf16[2,128,128]{2,1,0:T(8,128)(2,1)S(1)}, u32[]{:S(2)}, u32[]{:S(2)}) %collective-permute-start.23) | collective-permute-done | bytes 65568 | tf_op jit(solution)/shard_map/ppermute | solution.py:18
  36.3 3.0 %collective-permute-start.7 = (bf16[3,128,128]{2,1,0:T(8,128)(2,1)S(1)}, bf16[3,128,128]{2,1,0:T(8,128)(2,1)S(1)}, u32[]{:S(2)}, u32[]{:S(2)}) collective-permute-start(bf16[3,128,128]{2,1,0:T(8,128)(2,1)S(1)} %shard_map.62.refs_1_), channel_id=1, source_target_pairs={{0,1},{1,0},{2,3},{3,2},{4,5},{5,4},{6,7},{7,6},{8,9},{9,8},{10,11... | collective-permute-start | bytes 294920 | tf_op jit(solution)/shard_map/ppermute | solution.py:18
  40.5 1.7 %collective-permute-start.9 = (bf16[3,128,128]{2,1,0:T(8,128)(2,1)S(1)}, bf16[3,128,128]{2,1,0:T(8,128)(2,1)S(1)}, u32[]{:S(2)}, u32[]{:S(2)}) collective-permute-start(bf16[3,128,128]{2,1,0:T(8,128)(2,1)S(1)} %collective-permute-done.8.refs_3_), channel_id=1, source_target_pairs={{0,1},{1,0},{2,3},{3,2},{4,5},{5,4},{6,7},{7,6},{8,9},{9,8},{10,11... | collective-permute-start | bytes 294920 | tf_op jit(solution)/shard_map/ppermute | solution.py:18
  42.9 2.0 %collective-permute-start.18 = (bf16[2,128,128]{2,1,0:T(8,128)(2,1)S(1)}, bf16[2,128,128]{2,1,0:T(8,128)(2,1)S(1)}, u32[]{:S(2)}, u32[]{:S(2)}) collective-permute-start(bf16[2,128,128]{2,1,0:T(8,128)(2,1)S(1)} %shard_map.67.refs_2_), channel_id=1, source_target_pairs={{0,1},{1,0},{2,3},{3,2},{4,5},{5,4},{6,7},{7,6},{8,9},{9,8},{10,11... | collective-permute-start | bytes 196616 | tf_op jit(solution)/shard_map/ppermute | solution.py:18
  47.5 1.5 %shard_map.69 = (f32[512,128]{1,0:T(8,128)S(1)}, bf16[512,128]{1,0:T(8,128)(2,1)S(1)}, f32[512,128]{1,0:T(8,128)S(1)}, bf16[5,2,1024,256]{3,2,1,0:T(8,128)(2,1)S(1)}, bf16[5,2,1024,256]{3,2,1,0:T(8,128)(2,1)S(1)}) custom-call(f32[10,256]{1,0:T(8,128)S(1)} %fusion.refs_1_.refs_0_, ...), custom_call_target="tpu_custom_call", output_to_operand_aliasing={{3}: (10, {}), {4}: (11, {})} | custom-call | tf_op jit(solution)/shard_map/pallas_call | solution.py:60
  49.0 1.5 %collective-permute-start.25 = (bf16[512,128]{1,0:T(8,128)(2,1)S(1)}, bf16[512,128]{1,0:T(8,128)(2,1)S(1)}, u32[]{:S(2)}, u32[]{:S(2)}) collective-permute-start(bf16[512,128]{1,0:T(8,128)(2,1)S(1)} %get-tuple-element.76), channel_id=1, source_target_pairs={{0,8},{8,0},{16,24},{24,16},{1,9},{9,1},{17,25},{25,17},{2,10},{10... | collective-permute-start | bytes 393224 | tf_op jit(solution)/shard_map/ppermute | solution.py:18
  50.5 1.9 %collective-permute-done.26.refs_1_ = bf16[512,128]{1,0:T(8,128)(2,1)S(1)} collective-permute-done((bf16[512,128]{1,0:T(8,128)(2,1)S(1)}, bf16[512,128]{1,0:T(8,128)(2,1)S(1)}, u32[]{:S(2)}, u32[]{:S(2)}) %collective-permute-start.26) | collective-permute-done | bytes 131104 | tf_op jit(solution)/shard_map/ppermute | solution.py:18
  52.5 2.7 %collective-permute-done.25.refs_2_ = bf16[512,128]{1,0:T(8,128)(2,1)S(1)} collective-permute-done((bf16[512,128]{1,0:T(8,128)(2,1)S(1)}, bf16[512,128]{1,0:T(8,128)(2,1)S(1)}, u32[]{:S(2)}, u32[]{:S(2)}) %collective-permute-start.25) | collective-permute-done | bytes 131104 | tf_op jit(solution)/shard_map/ppermute | solution.py:18
  55.2 2.1 %collective-permute-done.27.refs_3_ = bf16[512,128]{1,0:T(8,128)(2,1)S(1)} collective-permute-done((bf16[512,128]{1,0:T(8,128)(2,1)S(1)}, bf16[512,128]{1,0:T(8,128)(2,1)S(1)}, u32[]{:S(2)}, u32[]{:S(2)}) %collective-permute-start.27) | collective-permute-done | bytes 131104 | tf_op jit(solution)/shard_map/ppermute | solution.py:18
  57.4 4.0 %collective-permute-start.31 = (bf16[4,2,64,128]{3,2,1,0:T(8,128)(2,1)S(1)}, bf16[4,2,64,128]{3,2,1,0:T(8,128)(2,1)S(1)}, u32[]{:S(2)}, u32[]{:S(2)}) collective-permute-start(bf16[4,2,64,128]{3,2,1,0:T(8,128)(2,1)S(1)} %get-tuple-element.82), channel_id=1, source_target_pairs={{0,8},{1,2},{2,1},{3,4},{4,3},{5,6},{6,5},{7,15},{8,0},{9,10},{10,... | collective-permute-start | bytes 393224 | tf_op jit(solution)/shard_map/ppermute | solution.py:36
  61.3 2.3 %collective-permute-start.28 = (bf16[2,2,64,128]{3,2,1,0:T(8,128)(2,1)S(1)}, bf16[2,2,64,128]{3,2,1,0:T(8,128)(2,1)S(1)}, u32[]{:S(2)}, u32[]{:S(2)}) collective-permute-start(bf16[2,2,64,128]{3,2,1,0:T(8,128)(2,1)S(1)} %get-tuple-element.80), channel_id=1, source_target_pairs={{0,8},{8,0},{16,24},{24,16},{1,9},{9,1},{17,25},{25,17},{2,10},{10... | collective-permute-start | bytes 196616 | tf_op jit(solution)/shard_map/ppermute | solution.py:18
  63.8 1.9 %collective-permute-done.28.refs_1_.refs_0_ = bf16[2,2,64,128]{3,2,1,0:T(8,128)(2,1)S(1)} collective-permute-done((bf16[2,2,64,128]{3,2,1,0:T(8,128)(2,1)S(1)}, bf16[2,2,64,128]{3,2,1,0:T(8,128)(2,1)S(1)}, u32[]{:S(2)}, u32[]{:S(2)}) %collective-permute-start.28) | collective-permute-done | bytes 65568 | tf_op jit(solution)/shard_map/ppermute | solution.py:18
  66.8 2.0 %collective-permute-start.32 = (bf16[2,64,128]{2,1,0:T(8,128)(2,1)S(1)}, bf16[2,64,128]{2,1,0:T(8,128)(2,1)S(1)}, u32[]{:S(2)}, u32[]{:S(2)}) collective-permute-start(bf16[2,64,128]{2,1,0:T(8,128)(2,1)S(1)} %get-tuple-element.85), channel_id=1, source_target_pairs={{0,1},{1,0},{2,3},{3,2},{4,5},{5,4},{6,7},{7,6},{8,9},{9,8},{10,11... | collective-permute-start | bytes 98312 | tf_op jit(solution)/shard_map/ppermute | solution.py:18
  70.0 3.1 %collective-permute-done.33.corner_odd = bf16[2,64,128]{2,1,0:T(8,128)(2,1)S(1)} collective-permute-done((bf16[2,64,128]{2,1,0:T(8,128)(2,1)S(1)}, bf16[2,64,128]{2,1,0:T(8,128)(2,1)S(1)}, u32[]{:S(2)}, u32[]{:S(2)}) %collective-permute-start.33) | collective-permute-done | bytes 32800 | tf_op jit(solution)/shard_map/ppermute | solution.py:36
  73.0 1.5 %outer.1 = f32[4,2,64,128]{3,2,1,0:T(8,128)} custom-call(f32[8,6,64,128]{3,2,1,0:T(8,128)S(1)} %get-tuple-element.83.field, f32[4,2,64,128]{3,2,1,0:T(8,128)S(1)} %get-tuple-element.84.fresh_ref, bf16[2,64,128]{2,1,0:T(8,128)(2,1)S(1)} %collective-permute-done.32.corner_even, bf16[2,64,128]{2,1,0:T(8,128)(2,1)S(1)} %collective-permute-done.33.corner_odd), custom_call_target="tpu_custom_call" | custom-call | tf_op jit(solution)/shard_map/outer/pallas_call | solution.py:359
  (71 shorter events, 19.5 us)
Async XLA Ops:
  1.1 5.4 %collective-permute-start.1 = (bf16[128,512]{1,0:T(8,128)(2,1)S(1)}, bf16[128,512]{1,0:T(8,128)(2,1)S(1)}, u32[]{:S(2)}, u32[]{:S(2)}) collective-permute-start(bf16[128,512]{1,0:T(8,128)(2,1)S(1)} %shard_map.55.refs_0_.refs_1_), channel_id=1, source_target_pairs={{0,16},{8,24},{16,0},{24,8},{1,17},{9,25},{17,1},{25,9},{2,18},{10... | collective-permute-start | bytes 393224 | tf_op jit(solution)/shard_map/ppermute | solution.py:18
  1.2 16.1 %collective-permute-start = (bf16[128,512]{1,0:T(8,128)(2,1)S(1)}, bf16[128,512]{1,0:T(8,128)(2,1)S(1)}, u32[]{:S(2)}, u32[]{:S(2)}) collective-permute-start(bf16[128,512]{1,0:T(8,128)(2,1)S(1)} %shard_map.55.refs_0_.refs_1_), channel_id=1, source_target_pairs={{0,8},{8,0},{16,24},{24,16},{1,9},{9,1},{17,25},{25,17},{2,10},{10... | collective-permute-start | bytes 393224 | tf_op jit(solution)/shard_map/ppermute | solution.py:18
  6.4 11.4 %collective-permute-start.2 = (bf16[128,512]{1,0:T(8,128)(2,1)S(1)}, bf16[128,512]{1,0:T(8,128)(2,1)S(1)}, u32[]{:S(2)}, u32[]{:S(2)}) collective-permute-start(bf16[128,512]{1,0:T(8,128)(2,1)S(1)} %collective-permute-done.1.refs_2_), channel_id=1, source_target_pairs={{0,8},{8,0},{16,24},{24,16},{1,9},{9,1},{17,25},{25,17},{2,10},{10... | collective-permute-start | bytes 393224 | tf_op jit(solution)/shard_map/ppermute | solution.py:18
  21.3 4.8 %collective-permute-start.4 = (bf16[3,128,128]{2,1,0:T(8,128)(2,1)S(1)}, bf16[3,128,128]{2,1,0:T(8,128)(2,1)S(1)}, u32[]{:S(2)}, u32[]{:S(2)}) collective-permute-start(bf16[3,128,128]{2,1,0:T(8,128)(2,1)S(1)} %get-tuple-element.56), channel_id=1, source_target_pairs={{0,2},{1,3},{2,0},{3,1},{4,6},{5,7},{6,4},{7,5},{8,10},{9,11},{10,... | collective-permute-start | bytes 294920 | tf_op jit(solution)/shard_map/ppermute | solution.py:18
  21.7 5.6 %collective-permute-start.5 = (bf16[3,128,128]{2,1,0:T(8,128)(2,1)S(1)}, bf16[3,128,128]{2,1,0:T(8,128)(2,1)S(1)}, u32[]{:S(2)}, u32[]{:S(2)}) collective-permute-start(bf16[3,128,128]{2,1,0:T(8,128)(2,1)S(1)} %get-tuple-element.57), channel_id=1, source_target_pairs={{0,4},{1,5},{2,6},{3,7},{4,0},{5,1},{6,2},{7,3},{8,12},{9,13},{10,... | collective-permute-start | bytes 294920 | tf_op jit(solution)/shard_map/ppermute | solution.py:18
  22.9 5.5 %collective-permute-start.6 = (bf16[3,128,128]{2,1,0:T(8,128)(2,1)S(1)}, bf16[3,128,128]{2,1,0:T(8,128)(2,1)S(1)}, u32[]{:S(2)}, u32[]{:S(2)}) collective-permute-start(bf16[3,128,128]{2,1,0:T(8,128)(2,1)S(1)} %get-tuple-element.58), channel_id=1, source_target_pairs={{0,6},{1,7},{2,4},{3,5},{4,2},{5,3},{6,0},{7,1},{8,14},{9,15},{10,... | collective-permute-start | bytes 294920 | tf_op jit(solution)/shard_map/ppermute | solution.py:18
  24.6 5.4 %collective-permute-start.15 = (bf16[2,128,128]{2,1,0:T(8,128)(2,1)S(1)}, bf16[2,128,128]{2,1,0:T(8,128)(2,1)S(1)}, u32[]{:S(2)}, u32[]{:S(2)}) collective-permute-start(bf16[2,128,128]{2,1,0:T(8,128)(2,1)S(1)} %get-tuple-element.68), channel_id=1, source_target_pairs={{0,2},{1,3},{2,0},{3,1},{4,6},{5,7},{6,4},{7,5},{8,10},{9,11},{10,... | collective-permute-start | bytes 196616 | tf_op jit(solution)/shard_map/ppermute | solution.py:18
  24.9 5.0 %collective-permute-start.16 = (bf16[2,128,128]{2,1,0:T(8,128)(2,1)S(1)}, bf16[2,128,128]{2,1,0:T(8,128)(2,1)S(1)}, u32[]{:S(2)}, u32[]{:S(2)}) collective-permute-start(bf16[2,128,128]{2,1,0:T(8,128)(2,1)S(1)} %get-tuple-element.69), channel_id=1, source_target_pairs={{0,4},{1,5},{2,6},{3,7},{4,0},{5,1},{6,2},{7,3},{8,12},{9,13},{10,... | collective-permute-start | bytes 196616 | tf_op jit(solution)/shard_map/ppermute | solution.py:18
  26.1 4.8 %collective-permute-start.17 = (bf16[2,128,128]{2,1,0:T(8,128)(2,1)S(1)}, bf16[2,128,128]{2,1,0:T(8,128)(2,1)S(1)}, u32[]{:S(2)}, u32[]{:S(2)}) collective-permute-start(bf16[2,128,128]{2,1,0:T(8,128)(2,1)S(1)} %get-tuple-element.70), channel_id=1, source_target_pairs={{0,6},{1,7},{2,4},{3,5},{4,2},{5,3},{6,0},{7,1},{8,14},{9,15},{10,... | collective-permute-start | bytes 196616 | tf_op jit(solution)/shard_map/ppermute | solution.py:18
  28.5 10.7 %collective-permute-start.12 = (bf16[3,128,128]{2,1,0:T(8,128)(2,1)S(1)}, bf16[3,128,128]{2,1,0:T(8,128)(2,1)S(1)}, u32[]{:S(2)}, u32[]{:S(2)}) collective-permute-start(bf16[3,128,128]{2,1,0:T(8,128)(2,1)S(1)} %shard_map.62.refs_1_), channel_id=1, source_target_pairs={{0,6},{1,7},{2,4},{3,5},{4,2},{5,3},{6,0},{7,1},{8,14},{9,15},{10,... | collective-permute-start | bytes 294920 | tf_op jit(solution)/shard_map/ppermute | solution.py:18
  28.7 10.6 %collective-permute-start.10 = (bf16[3,128,128]{2,1,0:T(8,128)(2,1)S(1)}, bf16[3,128,128]{2,1,0:T(8,128)(2,1)S(1)}, u32[]{:S(2)}, u32[]{:S(2)}) collective-permute-start(bf16[3,128,128]{2,1,0:T(8,128)(2,1)S(1)} %shard_map.62.refs_1_), channel_id=1, source_target_pairs={{0,4},{1,5},{2,6},{3,7},{4,0},{5,1},{6,2},{7,3},{8,12},{9,13},{10,... | collective-permute-start | bytes 294920 | tf_op jit(solution)/shard_map/ppermute | solution.py:18
  31.1 5.3 %collective-permute-start.23 = (bf16[2,128,128]{2,1,0:T(8,128)(2,1)S(1)}, bf16[2,128,128]{2,1,0:T(8,128)(2,1)S(1)}, u32[]{:S(2)}, u32[]{:S(2)}) collective-permute-start(bf16[2,128,128]{2,1,0:T(8,128)(2,1)S(1)} %shard_map.67.refs_2_), channel_id=1, source_target_pairs={{0,6},{1,7},{2,4},{3,5},{4,2},{5,3},{6,0},{7,1},{8,14},{9,15},{10,... | collective-permute-start | bytes 196616 | tf_op jit(solution)/shard_map/ppermute | solution.py:18
  34.5 6.0 %collective-permute-start.8 = (bf16[3,128,128]{2,1,0:T(8,128)(2,1)S(1)}, bf16[3,128,128]{2,1,0:T(8,128)(2,1)S(1)}, u32[]{:S(2)}, u32[]{:S(2)}) collective-permute-start(bf16[3,128,128]{2,1,0:T(8,128)(2,1)S(1)} %shard_map.62.refs_1_), channel_id=1, source_target_pairs={{0,2},{1,3},{2,0},{3,1},{4,6},{5,7},{6,4},{7,5},{8,10},{9,11},{10,... | collective-permute-start | bytes 294920 | tf_op jit(solution)/shard_map/ppermute | solution.py:18
  34.5 5.3 %collective-permute-start.21 = (bf16[2,128,128]{2,1,0:T(8,128)(2,1)S(1)}, bf16[2,128,128]{2,1,0:T(8,128)(2,1)S(1)}, u32[]{:S(2)}, u32[]{:S(2)}) collective-permute-start(bf16[2,128,128]{2,1,0:T(8,128)(2,1)S(1)} %shard_map.67.refs_2_), channel_id=1, source_target_pairs={{0,4},{1,5},{2,6},{3,7},{4,0},{5,1},{6,2},{7,3},{8,12},{9,13},{10,... | collective-permute-start | bytes 196616 | tf_op jit(solution)/shard_map/ppermute | solution.py:18
  36.3 8.6 %collective-permute-start.7 = (bf16[3,128,128]{2,1,0:T(8,128)(2,1)S(1)}, bf16[3,128,128]{2,1,0:T(8,128)(2,1)S(1)}, u32[]{:S(2)}, u32[]{:S(2)}) collective-permute-start(bf16[3,128,128]{2,1,0:T(8,128)(2,1)S(1)} %shard_map.62.refs_1_), channel_id=1, source_target_pairs={{0,1},{1,0},{2,3},{3,2},{4,5},{5,4},{6,7},{7,6},{8,9},{9,8},{10,11... | collective-permute-start | bytes 294920 | tf_op jit(solution)/shard_map/ppermute | solution.py:18
  39.3 5.6 %collective-permute-start.13 = (bf16[3,128,128]{2,1,0:T(8,128)(2,1)S(1)}, bf16[3,128,128]{2,1,0:T(8,128)(2,1)S(1)}, u32[]{:S(2)}, u32[]{:S(2)}) collective-permute-start(bf16[3,128,128]{2,1,0:T(8,128)(2,1)S(1)} %collective-permute-done.12.refs_7_), channel_id=1, source_target_pairs={{0,1},{1,0},{2,3},{3,2},{4,5},{5,4},{6,7},{7,6},{8,9},{9,8},{10,11... | collective-permute-start | bytes 294920 | tf_op jit(solution)/shard_map/ppermute | solution.py:18
  39.3 6.1 %collective-permute-start.11 = (bf16[3,128,128]{2,1,0:T(8,128)(2,1)S(1)}, bf16[3,128,128]{2,1,0:T(8,128)(2,1)S(1)}, u32[]{:S(2)}, u32[]{:S(2)}) collective-permute-start(bf16[3,128,128]{2,1,0:T(8,128)(2,1)S(1)} %collective-permute-done.10.refs_5_), channel_id=1, source_target_pairs={{0,1},{1,0},{2,3},{3,2},{4,5},{5,4},{6,7},{7,6},{8,9},{9,8},{10,11... | collective-permute-start | bytes 294920 | tf_op jit(solution)/shard_map/ppermute | solution.py:18
  40.5 5.0 %collective-permute-start.9 = (bf16[3,128,128]{2,1,0:T(8,128)(2,1)S(1)}, bf16[3,128,128]{2,1,0:T(8,128)(2,1)S(1)}, u32[]{:S(2)}, u32[]{:S(2)}) collective-permute-start(bf16[3,128,128]{2,1,0:T(8,128)(2,1)S(1)} %collective-permute-done.8.refs_3_), channel_id=1, source_target_pairs={{0,1},{1,0},{2,3},{3,2},{4,5},{5,4},{6,7},{7,6},{8,9},{9,8},{10,11... | collective-permute-start | bytes 294920 | tf_op jit(solution)/shard_map/ppermute | solution.py:18
  47.4 5.0 %collective-permute-start.26 = (bf16[512,128]{1,0:T(8,128)(2,1)S(1)}, bf16[512,128]{1,0:T(8,128)(2,1)S(1)}, u32[]{:S(2)}, u32[]{:S(2)}) collective-permute-start(bf16[512,128]{1,0:T(8,128)(2,1)S(1)} %get-tuple-element.78), channel_id=1, source_target_pairs={{0,8},{8,0},{16,24},{24,16},{1,9},{9,1},{17,25},{25,17},{2,10},{10... | collective-permute-start | bytes 393224 | tf_op jit(solution)/shard_map/ppermute | solution.py:18
  49.0 6.2 %collective-permute-start.25 = (bf16[512,128]{1,0:T(8,128)(2,1)S(1)}, bf16[512,128]{1,0:T(8,128)(2,1)S(1)}, u32[]{:S(2)}, u32[]{:S(2)}) collective-permute-start(bf16[512,128]{1,0:T(8,128)(2,1)S(1)} %get-tuple-element.76), channel_id=1, source_target_pairs={{0,8},{8,0},{16,24},{24,16},{1,9},{9,1},{17,25},{25,17},{2,10},{10... | collective-permute-start | bytes 393224 | tf_op jit(solution)/shard_map/ppermute | solution.py:18
  52.4 4.9 %collective-permute-start.27 = (bf16[512,128]{1,0:T(8,128)(2,1)S(1)}, bf16[512,128]{1,0:T(8,128)(2,1)S(1)}, u32[]{:S(2)}, u32[]{:S(2)}) collective-permute-start(bf16[512,128]{1,0:T(8,128)(2,1)S(1)} %shard_map.70), channel_id=1, source_target_pairs={{0,16},{8,24},{16,0},{24,8},{1,17},{9,25},{17,1},{25,9},{2,18},{10... | collective-permute-start | bytes 393224 | tf_op jit(solution)/shard_map/ppermute | solution.py:18
  57.4 12.2 %collective-permute-start.31 = (bf16[4,2,64,128]{3,2,1,0:T(8,128)(2,1)S(1)}, bf16[4,2,64,128]{3,2,1,0:T(8,128)(2,1)S(1)}, u32[]{:S(2)}, u32[]{:S(2)}) collective-permute-start(bf16[4,2,64,128]{3,2,1,0:T(8,128)(2,1)S(1)} %get-tuple-element.82), channel_id=1, source_target_pairs={{0,8},{1,2},{2,1},{3,4},{4,3},{5,6},{6,5},{7,15},{8,0},{9,10},{10,... | collective-permute-start | bytes 393224 | tf_op jit(solution)/shard_map/ppermute | solution.py:36
  61.3 8.2 %collective-permute-start.30 = (bf16[4,2,64,128]{3,2,1,0:T(8,128)(2,1)S(1)}, bf16[4,2,64,128]{3,2,1,0:T(8,128)(2,1)S(1)}, u32[]{:S(2)}, u32[]{:S(2)}) collective-permute-start(bf16[4,2,64,128]{3,2,1,0:T(8,128)(2,1)S(1)} %get-tuple-element.82), channel_id=1, source_target_pairs={{0,1},{1,0},{2,3},{3,2},{4,5},{5,4},{6,7},{7,6},{8,9},{9,8},{10,11... | collective-permute-start | bytes 393224 | tf_op jit(solution)/shard_map/ppermute | solution.py:18
  61.3 4.3 %collective-permute-start.28 = (bf16[2,2,64,128]{3,2,1,0:T(8,128)(2,1)S(1)}, bf16[2,2,64,128]{3,2,1,0:T(8,128)(2,1)S(1)}, u32[]{:S(2)}, u32[]{:S(2)}) collective-permute-start(bf16[2,2,64,128]{3,2,1,0:T(8,128)(2,1)S(1)} %get-tuple-element.80), channel_id=1, source_target_pairs={{0,8},{8,0},{16,24},{24,16},{1,9},{9,1},{17,25},{25,17},{2,10},{10... | collective-permute-start | bytes 196616 | tf_op jit(solution)/shard_map/ppermute | solution.py:18
  (12 other events, 37.2 us)
